TPU v7x, 128 devices: a whole 4x4x4 slice. The times are simulated.
128 devices in a mesh: box: 8 (over y, core), samp: 16 (over x, z).
Axes of the slice: x: 4, y: 4, z: 4, core: 2. Of those that a mesh axis runs over, the one named last changes fastest.
Arguments:
- children: bfloat16 [2048, 2, 64, 128], P('box', None, 'samp'), may hold values from -6 to 6
- interp_theta: bfloat16 [64, 128], replicated, may hold values from -0.75 to 0.75
- interp_phi: bfloat16 [128, 256], replicated, may hold values from -0.5 to 0.5
- translator: bfloat16 [316, 2, 128, 256], P(None, None, 'samp'), may hold values from -0.1796875 to 0.1796875
- send_index: int32 [8, 8, 16], P('box'), may hold values from 0 to 31, as said below
- list_slots: int32 [256, 64], P('box'), may hold values from 0 to 127, as said below
- list_kinds: int32 [256, 64], P('box'), may hold values from 0 to 315
Outputs:
- parent_pattern: bfloat16 [256, 2, 128, 256], P('box', None, 'samp')
- local_field: float32 [256, 2, 128, 256], P('box', None, 'samp')
Inputs may be any that keep to these rules, and one draw needn't show every extreme that they name: The 16 entries of send_index[s, d] are distinct, and 31 is among them. `list_slots`: each sender sends a receiver a number of live slots between 4 and 16, the first ones; codes name only live slots, senders are spread over all devices of box, and some receiver has a sender with all 16 slots live.
All inputs are finite; a program needn't handle non-finite values.
Results may differ from a plain program's by a relative error of at most 0.0049.
Values may be sent and summed in bfloat16 or wider, within the bound.
No kernel may reach another device: no remote copies, remote signals or barrier semaphores. Data moves between devices by JAX's collectives and lax.ppermute only.
A program may use at most 192 MiB of HBM per device.

v0:
```python
import math

import jax
import jax.numpy as jnp
from jax import lax
from jax.sharding import PartitionSpec as P

KAPPA_H = 12.0


def octant_phase(polar_rows, polar_total, azimuth_total):
    polar = (polar_rows.astype(jnp.float32) + 0.5) * (math.pi / polar_total)
    azimuth = jnp.arange(azimuth_total, dtype=jnp.int32).astype(jnp.float32) * (
        2.0 * math.pi / azimuth_total
    )
    octant = jnp.arange(8, dtype=jnp.int32)
    sign_x = ((octant & 1) * 2 - 1).astype(jnp.float32)[:, None, None]
    sign_y = ((octant >> 1 & 1) * 2 - 1).astype(jnp.float32)[:, None, None]
    sign_z = ((octant >> 2 & 1) * 2 - 1).astype(jnp.float32)[:, None, None]
    along_x = jnp.sin(polar)[:, None] * jnp.cos(azimuth)[None, :]
    along_y = jnp.sin(polar)[:, None] * jnp.sin(azimuth)[None, :]
    along_z = jnp.cos(polar)[:, None] + jnp.zeros((1, azimuth_total), jnp.float32)
    phase_angle = KAPPA_H * (sign_x * along_x + sign_y * along_y + sign_z * along_z)
    return (jnp.cos(phase_angle), jnp.sin(phase_angle))


def aggregate(group, theta_cols, interp_phi, polar_rows, polar_total):
    theta_int = jnp.einsum(
        "nocta,tu->nocua", group, theta_cols, preferred_element_type=jnp.float32
    ).astype(jnp.bfloat16)
    raised = jnp.einsum(
        "nocua,ag->nocug", theta_int, interp_phi, preferred_element_type=jnp.float32
    )
    cosine, sine_part = octant_phase(polar_rows, polar_total, interp_phi.shape[1])
    real_part = raised[:, :, 0]
    imag_part = raised[:, :, 1]
    rotated_real = jnp.sum(cosine * real_part - sine_part * imag_part, axis=1)
    rotated_imag = jnp.sum(sine_part * real_part + cosine * imag_part, axis=1)
    return jnp.stack([rotated_real, rotated_imag], axis=1).astype(jnp.bfloat16)


def local(children, interp_theta, interp_phi, translator, send_index, list_slots, list_kinds):
    samp_count = lax.axis_size("samp")
    samp_position = lax.axis_index("samp")
    polar_total = interp_theta.shape[1]
    child_boxes = children.shape[0]
    gathered = lax.all_gather(children, "samp", axis=2, tiled=True)
    row_count = polar_total // samp_count
    first_row = samp_position * row_count
    theta_cols = lax.dynamic_slice_in_dim(interp_theta, first_row, row_count, 1)
    polar_rows = first_row + jnp.arange(row_count, dtype=jnp.int32)
    grouped = gathered.reshape(child_boxes // 8, 8, 2, gathered.shape[2], gathered.shape[3])
    parents = aggregate(grouped, theta_cols, interp_phi, polar_rows, polar_total)
    parent_boxes = parents.shape[0]
    slot_count = send_index.shape[2]
    outgoing = parents[send_index[0].reshape(-1)]
    outgoing = outgoing.reshape(
        send_index.shape[1], slot_count, 2, parents.shape[2], parents.shape[3]
    )
    received = lax.all_to_all(outgoing, "box", split_axis=0, concat_axis=0, tiled=True)
    source_pool = received.reshape(-1, 2, parents.shape[2], parents.shape[3])
    field_real = jnp.zeros((parent_boxes, parents.shape[2], parents.shape[3]), jnp.float32)
    field_imag = jnp.zeros((parent_boxes, parents.shape[2], parents.shape[3]), jnp.float32)
    for offset in range(0, list_slots.shape[1], 16):
        picked = list_slots[:, offset : offset + 16]
        picked_kinds = list_kinds[:, offset : offset + 16]
        sources = source_pool[picked].astype(jnp.float32)
        factors = translator[picked_kinds].astype(jnp.float32)
        field_real = field_real + jnp.sum(
            factors[:, :, 0] * sources[:, :, 0] - factors[:, :, 1] * sources[:, :, 1], axis=1
        )
        field_imag = field_imag + jnp.sum(
            factors[:, :, 0] * sources[:, :, 1] + factors[:, :, 1] * sources[:, :, 0], axis=1
        )
    local_field = jnp.stack([field_real, field_imag], axis=1)
    return (parents, local_field)


def solution(mesh):
    return jax.shard_map(
        local,
        mesh=mesh,
        in_specs=(
            P("box", None, "samp", None),
            P(),
            P(),
            P(None, None, "samp", None),
            P("box", None, None),
            P("box", None),
            P("box", None),
        ),
        out_specs=(P("box", None, "samp", None), P("box", None, "samp", None)),
        check_vma=False,
    )
```

profile of v0, /device:TPU:1, one launch (start us, length us, event | category | flops | bytes accessed | tf_op | source)
XLA Modules:
  0.0 198.4 jit_solution(10882163428178676322)
XLA Ops:
  7.2 2.1 %copy.12 = bf16[256,2,4,128]{3,0,1,2:T(8,128)(2,1)} copy(bf16[256,2,4,128]{3,2,1,0:T(4,128)(2,1)} %param.7) | data formatting | bytes 1048576 | tf_op args[0]
  9.3 0.8 reshape_squeeze.3
  10.1 0.9 compare_select_fusion.4
  11.0 0.1 reshape.263
  11.1 0.9 compare_select_fusion.5
  12.1 0.1 reshape.255
  12.1 0.1 reshape.247
  12.2 0.1 reshape.231
  12.3 3.4 %gather_fusion.3 = bf16[512,2,8,256]{3,2,1,0:T(8,128)(2,1)} fusion(bf16[316,2,8,256]{3,2,1,0:T(8,128)(2,1)S(1)} %copy-done, s32[1024]{0:T(1024)S(1)} %pad_clamp_fusion.5), kind=kCustom, calls=%fused_computation.3 | custom fusion | bytes 8390656 | tf_op jit(solution)/shard_map/gather | solution.py:68
  15.8 3.5 %gather_fusion = bf16[512,2,8,256]{3,2,1,0:T(8,128)(2,1)} fusion(bf16[316,2,8,256]{3,2,1,0:T(8,128)(2,1)S(1)} %copy-done, s32[1024]{0:T(1024)S(1)} %pad_clamp_fusion.8), kind=kCustom, calls=%fused_computation | custom fusion | bytes 8390656 | tf_op jit(solution)/shard_map/gather | solution.py:68
  19.2 0.1 reshape.279
  19.3 0.1 reshape.271
  19.4 3.5 %gather_fusion.5 = bf16[512,2,8,256]{3,2,1,0:T(8,128)(2,1)} fusion(bf16[316,2,8,256]{3,2,1,0:T(8,128)(2,1)S(1)} %copy-done, s32[1024]{0:T(1024)S(1)} %pad_clamp_fusion.3), kind=kCustom, calls=%fused_computation.5 | custom fusion | bytes 8390656 | tf_op jit(solution)/shard_map/gather | solution.py:68
  22.9 0.1 reshape.295
  22.9 0.1 reshape.287
  23.0 3.6 %gather_fusion.7 = bf16[512,2,8,256]{3,2,1,0:T(8,128)(2,1)} fusion(bf16[316,2,8,256]{3,2,1,0:T(8,128)(2,1)S(1)} %copy-done, s32[1024]{0:T(1024)S(1)} %pad_clamp_fusion.1), kind=kCustom, calls=%fused_computation.7 | custom fusion | bytes 8390656 | tf_op jit(solution)/shard_map/gather | solution.py:68
  26.8 0.1 broadcast_multiply_fusion.1
  26.9 0.3 fusion.4
  27.2 6.7 %bitcast_convert_fusion.5 = f32[32,16,2,8,256]{4,3,2,1,0:T(8,128)} fusion(bf16[512,2,8,256]{3,2,1,0:T(8,128)(2,1)} %gather_fusion.3), kind=kLoop, calls=%fused_computation.72 | loop fusion | flops 2097152 | bytes 12582912 | tf_op jit(solution)/shard_map/convert_element_type | solution.py:68
  33.9 4.4 %bitcast_convert_fusion.7 = f32[32,16,2,8,256]{4,3,2,1,0:T(8,128)} fusion(bf16[512,2,8,256]{3,2,1,0:T(8,128)(2,1)S(1)} %copy-done.3), kind=kLoop, calls=%fused_computation.74 | loop fusion | flops 2097152 | bytes 12582912 | tf_op jit(solution)/shard_map/convert_element_type | solution.py:68
  38.3 46.4 %all-gather.2.cloned.1.call-done = bf16[256,2,64,128]{3,0,1,2:T(8,128)(2,1)} async-done(((bf16[256,2,4,128]{3,0,1,2:T(8,128)(2,1)}), bf16[256,2,64,128]{3,0,1,2:T(8,128)(2,1)}) %all-gather.2.cloned.1.call-update) | async-done | bytes 8388624 | tf_op jit(solution)/shard_map/all_gather | solution.py:47
  84.8 12.0 %copy.13 = bf16[256,2,64,128]{3,2,1,0:T(8,128)(2,1)} copy(bf16[256,2,64,128]{3,0,1,2:T(8,128)(2,1)} %all-gather.2.cloned.1.call-done) | data formatting | bytes 16777216 | tf_op jit(solution)/shard_map/all_gather | solution.py:47
  96.8 7.2 %fusion.1 = f32[32,8,2,8,256]{4,3,2,1,0:T(8,128)} fusion(bf16[32,8,2,64,128]{4,3,2,1,0:T(8,128)(2,1)} %bitcast.82, bf16[128,256]{1,0:T(8,128)(2,1)S(1)} %copy-done.5, bf16[64,128]{1,0:T(8,128)(2,1)S(1)} %copy-done.6, s32[]{:T(128)S(6)} %select_n.37), kind=kOutput, calls=%fused_computation.23 | convolution fusion | flops 336068608 | bytes 12664836 | tf_op jit(solution)/shard_map/nocua,ag->nocug/dot_general | solution.py:31
  104.0 2.9 %subtract_reduce_fusion.4 = (bf16[32,8,256]{2,1,0:T(8,128)(2,1)S(1)}, bf16[32,8,256]{2,1,0:T(8,128)(2,1)S(1)}) fusion(f32[32,8,2,8,256]{4,3,2,1,0:T(8,128)} %fusion.1, f32[8,8,256]{2,1,0:T(8,128)S(1)} %get-tuple-element.13, f32[8,8,256]{2,1,0:T(8,128)S(1)} %get-tuple-element.12), kind=kLoop, calls=%fused_computation.20 | loop fusion | flops 4063232 | bytes 4587520 | tf_op jit(solution)/shard_map/reduce_sum | solution.py:37
  107.0 1.6 gather_fusion.1
  108.6 5.1 %all-to-all-start = ((bf16[8,16,2,8,256]{4,3,2,1,0:T(8,128)(2,1)}), bf16[8,16,2,8,256]{4,3,2,1,0:T(8,128)(2,1)S(1)}, u32[]{:S(2)}, u32[]{:S(2)}) async-start(bf16[8,16,2,8,256]{4,3,2,1,0:T(8,128)(2,1)} %bitcast.12), calls=%async_computation | async-start | bytes 2097152 | tf_op jit(solution)/shard_map/all_to_all | solution.py:60
  113.7 6.7 %bitcast_convert_fusion.3 = f32[32,16,2,8,256]{4,3,2,1,0:T(8,128)} fusion(bf16[512,2,8,256]{3,2,1,0:T(8,128)(2,1)} %gather_fusion.5), kind=kLoop, calls=%fused_computation.70 | loop fusion | flops 2097152 | bytes 12582912 | tf_op jit(solution)/shard_map/convert_element_type | solution.py:68
  120.4 4.4 %bitcast_convert_fusion.1 = f32[32,16,2,8,256]{4,3,2,1,0:T(8,128)} fusion(bf16[512,2,8,256]{3,2,1,0:T(8,128)(2,1)S(1)} %copy-done.2), kind=kLoop, calls=%fused_computation.68 | loop fusion | flops 2097152 | bytes 12582912 | tf_op jit(solution)/shard_map/convert_element_type | solution.py:68
  124.8 3.9 %all-to-all-done = bf16[8,16,2,8,256]{4,3,2,1,0:T(8,128)(2,1)S(1)} async-done(((bf16[8,16,2,8,256]{4,3,2,1,0:T(8,128)(2,1)}), bf16[8,16,2,8,256]{4,3,2,1,0:T(8,128)(2,1)S(1)}, u32[]{:S(2)}, u32[]{:S(2)}) %all-to-all-start) | async-done | bytes 1048608 | tf_op jit(solution)/shard_map/all_to_all | solution.py:60
  128.7 3.4 %gather_fusion.4 = bf16[512,2,8,256]{3,2,1,0:T(8,128)(2,1)} fusion(bf16[128,2,8,256]{3,2,1,0:T(8,128)(2,1)S(1)} %bitcast.70, s32[1024]{0:T(1024)S(1)} %pad_clamp_fusion.4), kind=kCustom, calls=%fused_computation.4 | custom fusion | bytes 8390656 | tf_op jit(solution)/shard_map/gather | solution.py:67
  132.1 6.5 %bitcast_convert_fusion.4 = f32[32,16,2,8,256]{4,3,2,1,0:T(8,128)} fusion(bf16[512,2,8,256]{3,2,1,0:T(8,128)(2,1)} %gather_fusion.4), kind=kLoop, calls=%fused_computation.71 | loop fusion | flops 2097152 | bytes 12582912 | tf_op jit(solution)/shard_map/convert_element_type | solution.py:67
  138.7 3.6 %gather_fusion.2 = bf16[512,2,8,256]{3,2,1,0:T(8,128)(2,1)} fusion(bf16[128,2,8,256]{3,2,1,0:T(8,128)(2,1)S(1)} %bitcast.71, s32[1024]{0:T(1024)S(1)} %pad_clamp_fusion.6), kind=kCustom, calls=%fused_computation.2 | custom fusion | bytes 8390656 | tf_op jit(solution)/shard_map/gather | solution.py:67
  142.2 6.6 %bitcast_convert_fusion.6 = f32[32,16,2,8,256]{4,3,2,1,0:T(8,128)} fusion(bf16[512,2,8,256]{3,2,1,0:T(8,128)(2,1)} %gather_fusion.2), kind=kLoop, calls=%fused_computation.73 | loop fusion | flops 2097152 | bytes 12582912 | tf_op jit(solution)/shard_map/convert_element_type | solution.py:67
  148.8 3.4 %gather_fusion.6 = bf16[512,2,8,256]{3,2,1,0:T(8,128)(2,1)} fusion(bf16[128,2,8,256]{3,2,1,0:T(8,128)(2,1)S(1)} %bitcast.72, s32[1024]{0:T(1024)S(1)} %pad_clamp_fusion.2), kind=kCustom, calls=%fused_computation.6 | custom fusion | bytes 8390656 | tf_op jit(solution)/shard_map/gather | solution.py:67
  152.2 6.5 %bitcast_convert_fusion.2 = f32[32,16,2,8,256]{4,3,2,1,0:T(8,128)} fusion(bf16[512,2,8,256]{3,2,1,0:T(8,128)(2,1)} %gather_fusion.6), kind=kLoop, calls=%fused_computation.69 | loop fusion | flops 2097152 | bytes 12582912 | tf_op jit(solution)/shard_map/convert_element_type | solution.py:67
  158.8 3.5 %gather_fusion.8 = bf16[512,2,8,256]{3,2,1,0:T(8,128)(2,1)} fusion(bf16[128,2,8,256]{3,2,1,0:T(8,128)(2,1)S(1)} %bitcast.73, s32[1024]{0:T(1024)S(1)} %pad_clamp_fusion), kind=kCustom, calls=%fused_computation.8 | custom fusion | bytes 8390656 | tf_op jit(solution)/shard_map/gather | solution.py:67
  162.3 6.7 %bitcast_convert_fusion = f32[32,16,2,8,256]{4,3,2,1,0:T(8,128)} fusion(bf16[512,2,8,256]{3,2,1,0:T(8,128)(2,1)} %gather_fusion.8), kind=kLoop, calls=%fused_computation.67 | loop fusion | flops 2097152 | bytes 12582912 | tf_op jit(solution)/shard_map/convert_element_type | solution.py:67
  169.0 6.9 %subtract_reduce_fusion.2 = (f32[32,8,256]{2,1,0:T(8,128)S(1)}, f32[32,8,256]{2,1,0:T(8,128)S(1)}) fusion(f32[32,16,2,8,256]{4,3,2,1,0:T(8,128)} %bitcast_convert_fusion.4, f32[32,16,2,8,256]{4,3,2,1,0:T(8,128)} %bitcast_convert_fusion.5), kind=kLoop, calls=%fused_computation.15 | loop fusion | flops 8257536 | bytes 17301504 | tf_op jit(solution)/shard_map/reduce_sum | solution.py:69
  175.9 0.1 slice-done.1
  176.0 5.3 %subtract_reduce_fusion.3 = (f32[32,8,256]{2,1,0:T(8,128)S(1)}, f32[32,8,256]{2,1,0:T(8,128)S(1)}) fusion(f32[32,16,2,8,256]{4,3,2,1,0:T(8,128)} %bitcast_convert_fusion.6, f32[32,16,2,8,256]{4,3,2,1,0:T(8,128)S(1)} %bitcast.75), kind=kLoop, calls=%fused_computation.16 | loop fusion | flops 8257536 | bytes 17301504 | tf_op jit(solution)/shard_map/reduce_sum | solution.py:69
  181.3 1.0 slice-done.5
  182.4 1.2 slice-done.7
  183.6 2.2 %subtract_reduce_fusion.1 = (f32[32,8,256]{2,1,0:T(8,128)S(1)}, f32[32,8,256]{2,1,0:T(8,128)S(1)}) fusion(f32[32,16,2,8,256]{4,3,2,1,0:T(8,128)S(1)} %bitcast.81, f32[32,16,2,8,256]{4,3,2,1,0:T(8,128)S(1)} %bitcast.79), kind=kLoop, calls=%fused_computation.14 | loop fusion | flops 8257536 | bytes 17301504 | tf_op jit(solution)/shard_map/reduce_sum | solution.py:69
  185.8 0.2 slice-done.3
  186.0 4.6 %subtract_reduce_fusion = (f32[32,8,256]{2,1,0:T(8,128)S(1)}, f32[32,8,256]{2,1,0:T(8,128)S(1)}) fusion(f32[32,16,2,8,256]{4,3,2,1,0:T(8,128)} %bitcast_convert_fusion, f32[32,16,2,8,256]{4,3,2,1,0:T(8,128)S(1)} %bitcast.77), kind=kLoop, calls=%fused_computation.13 | loop fusion | flops 8257536 | bytes 17301504 | tf_op jit(solution)/shard_map/reduce_sum | solution.py:69
  190.6 0.1 add_bitcast_fusion.1
  190.7 0.1 add_bitcast_fusion
  190.7 0.8 pad_maximum_fusion
  (47 shorter events, 0.3 us)
Async XLA Ops:
  7.2 5.1 %copy-start = (bf16[316,2,8,256]{3,2,1,0:T(8,128)(2,1)S(1)}, bf16[316,2,8,256]{3,2,1,0:T(8,128)(2,1)}, u32[]{:S(2)}) copy-start(bf16[316,2,8,256]{3,2,1,0:T(8,128)(2,1)} %param.10) | copy-start | bytes 7766020
  7.2 77.6 %all-gather.2.cloned.1.call-start = ((), (), s32[]{:S(2)}) async-start(), calls=%async_computation.1 | async-start | bytes 8912896 | tf_op jit(solution)/shard_map/all_gather | solution.py:47
  27.2 6.7 %copy-start.3 = (bf16[512,2,8,256]{3,2,1,0:T(8,128)(2,1)S(1)}, bf16[512,2,8,256]{3,2,1,0:T(8,128)(2,1)}, u32[]{:S(2)}) copy-start(bf16[512,2,8,256]{3,2,1,0:T(8,128)(2,1)} %gather_fusion) | copy-start | bytes 12582916
  38.3 58.4 %copy-start.5 = (bf16[128,256]{1,0:T(8,128)(2,1)S(1)}, bf16[128,256]{1,0:T(8,128)(2,1)}, u32[]{:S(2)}) copy-start(bf16[128,256]{1,0:T(8,128)(2,1)} %param.9) | copy-start | bytes 196612
  38.3 58.4 %copy-start.6 = (bf16[64,128]{1,0:T(8,128)(2,1)S(1)}, bf16[64,128]{1,0:T(8,128)(2,1)}, u32[]{:S(2)}) copy-start(bf16[64,128]{1,0:T(8,128)(2,1)} %param.8) | copy-start | bytes 49156
  107.0 13.5 %copy-start.4 = (bf16[32,2,8,256]{3,2,1,0:T(8,128)(2,1)}, bf16[32,2,8,256]{3,2,1,0:T(8,128)(2,1)S(1)}, u32[]{:S(2)}) copy-start(bf16[32,2,8,256]{3,2,1,0:T(8,128)(2,1)S(1)} %pad_maximum_fusion.1) | copy-start | bytes 786436
  108.6 20.1 %all-to-all-start = ((bf16[8,16,2,8,256]{4,3,2,1,0:T(8,128)(2,1)}), bf16[8,16,2,8,256]{4,3,2,1,0:T(8,128)(2,1)S(1)}, u32[]{:S(2)}, u32[]{:S(2)}) async-start(bf16[8,16,2,8,256]{4,3,2,1,0:T(8,128)(2,1)} %bitcast.12), calls=%async_computation | async-start | bytes 2097152 | tf_op jit(solution)/shard_map/all_to_all | solution.py:60
  113.7 6.7 %copy-start.2 = (bf16[512,2,8,256]{3,2,1,0:T(8,128)(2,1)S(1)}, bf16[512,2,8,256]{3,2,1,0:T(8,128)(2,1)}, u32[]{:S(2)}) copy-start(bf16[512,2,8,256]{3,2,1,0:T(8,128)(2,1)} %gather_fusion.7) | copy-start | bytes 12582916
  162.3 13.6 %slice-start = ((s8[8388608]{0:T(1024)(128)(4,1)}), s8[4194304]{0:T(1024)(128)(4,1)S(1)}, s32[]{:S(2)}) async-start(s8[8388608]{0:T(1024)(128)(4,1)} %bitcast.74), calls=%async_computation.2 | async-start | bytes 8388608
  169.0 7.0 %slice-start.1 = ((s8[8388608]{0:T(1024)(128)(4,1)}), s8[4194304]{0:T(1024)(128)(4,1)S(1)}, s32[]{:S(2)}) async-start(s8[8388608]{0:T(1024)(128)(4,1)} %bitcast.74), calls=%async_computation.3 | async-start | bytes 8388608
  169.0 12.3 %slice-start.4 = ((s8[8388608]{0:T(1024)(128)(4,1)}), s8[4194304]{0:T(1024)(128)(4,1)S(1)}, s32[]{:S(2)}) async-start(s8[8388608]{0:T(1024)(128)(4,1)} %bitcast.78), calls=%async_computation.6 | async-start | bytes 8388608
  169.0 12.3 %slice-start.6 = ((s8[8388608]{0:T(1024)(128)(4,1)}), s8[4194304]{0:T(1024)(128)(4,1)S(1)}, s32[]{:S(2)}) async-start(s8[8388608]{0:T(1024)(128)(4,1)} %bitcast.80), calls=%async_computation.8 | async-start | bytes 8388608
  176.0 6.3 %slice-start.5 = ((s8[8388608]{0:T(1024)(128)(4,1)}), s8[4194304]{0:T(1024)(128)(4,1)S(1)}, s32[]{:S(2)}) async-start(s8[8388608]{0:T(1024)(128)(4,1)} %bitcast.78), calls=%async_computation.7 | async-start | bytes 8388608
  176.0 7.5 %slice-start.7 = ((s8[8388608]{0:T(1024)(128)(4,1)}), s8[4194304]{0:T(1024)(128)(4,1)S(1)}, s32[]{:S(2)}) async-start(s8[8388608]{0:T(1024)(128)(4,1)} %bitcast.80), calls=%async_computation.9 | async-start | bytes 8388608
  176.0 9.8 %slice-start.2 = ((s8[8388608]{0:T(1024)(128)(4,1)}), s8[4194304]{0:T(1024)(128)(4,1)S(1)}, s32[]{:S(2)}) async-start(s8[8388608]{0:T(1024)(128)(4,1)} %bitcast.76), calls=%async_computation.4 | async-start | bytes 8388608
  183.5 2.4 %slice-start.3 = ((s8[8388608]{0:T(1024)(128)(4,1)}), s8[4194304]{0:T(1024)(128)(4,1)S(1)}, s32[]{:S(2)}) async-start(s8[8388608]{0:T(1024)(128)(4,1)} %bitcast.76), calls=%async_computation.5 | async-start | bytes 8388608
  186.0 5.6 %copy-start.1 = (bf16[316,2,8,256]{3,2,1,0:T(8,128)(2,1)S(1)}, bf16[316,2,8,256]{3,2,1,0:T(8,128)(2,1)}, u32[]{:S(2)}) copy-start(bf16[316,2,8,256]{3,2,1,0:T(8,128)(2,1)} %param.10) | copy-start | bytes 7766020
Sparse Core Ops, SparseCore 0:
  10.7 74.0 all-gather.1
where the time goes:
time: 199 us; the launch traced here: 198 us
  other arithmetic  73.9 us (37%)
  waiting for transfers between devices  50.3 us (25%)
  local copies, waits for them, and re-layouts  47.5 us (24%)
  between operations  14.3 us (7%)
  matrix products  7.23 us (4%)
  starting transfers between devices  5.16 us (3%)
    all_gather x1, waiting for transfers between devices, local(): gathered = lax.all_gather(children, 'samp', axis=2, tiled=True)  46.4 us
    convert_element_type x4, other arithmetic, local(): sources = source_pool[picked].astype(jnp.float32)  26.3 us
    convert_element_type x4, other arithmetic, local(): factors = translator[picked_kinds].astype(jnp.float32)  22.2 us
    reduce_sum x4, other arithmetic, local(): jnp.sum(factors[:, :, 0] * sources[:, :, 0] - factors[:, :, 1] * sources[...  19 us
    gather x4, local copies, waits for them, and re-layouts, local(): factors = translator[picked_kinds].astype(jnp.float32)  14 us
    gather x4, local copies, waits for them, and re-layouts, local(): sources = source_pool[picked].astype(jnp.float32)  13.9 us
    all_gather x1, local copies, waits for them, and re-layouts, local(): gathered = lax.all_gather(children, 'samp', axis=2, tiled=True)  12 us
    dot_general x1, matrix products, aggregate(): jnp.einsum('nocua,ag->nocug', theta_int, interp_phi, preferred_element_ty...  7.23 us
  transfers between devices with their start and end apart: 2, of which 2 were waited for; matrix products, arithmetic and copies ran while one was open for 20% of the time, Pallas kernels for 0%

commit v1 on v0

v1 whole, which is shorter than its diff:
```python
import math

import jax
import jax.numpy as jnp
from jax import lax
from jax.experimental import pallas as pl
from jax.experimental.pallas import tpu as pltpu
from jax.sharding import PartitionSpec as P

KAPPA_H = 12.0


def phase_tables(polar_total, azimuth_total):
    polar = (jnp.arange(polar_total, dtype=jnp.int32).astype(jnp.float32) + 0.5) * (
        math.pi / polar_total
    )
    azimuth = jnp.arange(azimuth_total, dtype=jnp.int32).astype(jnp.float32) * (
        2.0 * math.pi / azimuth_total
    )
    octant = jnp.arange(4, dtype=jnp.int32)
    sign_x = ((octant & 1) * 2 - 1).astype(jnp.float32)[:, None, None]
    sign_y = ((octant >> 1 & 1) * 2 - 1).astype(jnp.float32)[:, None, None]
    along_x = jnp.sin(polar)[:, None] * jnp.cos(azimuth)[None, :]
    along_y = jnp.sin(polar)[:, None] * jnp.sin(azimuth)[None, :]
    along_z = jnp.cos(polar)[:, None] + jnp.zeros((1, azimuth_total), jnp.float32)
    phase = KAPPA_H * (sign_x * along_x + sign_y * along_y - along_z)
    return jnp.cos(phase), jnp.sin(phase)


def aggregate_kernel(x_ref, theta_ref, phi_ref, cos_ref, sin_ref, out_ref, mid_ref, raised_ref):
    theta = theta_ref[...]
    phi = phi_ref[...]
    polar_total = theta.shape[0]
    slabs, parents = out_ref.shape[0], out_ref.shape[1]
    for p in range(parents):
        for o in range(8):
            for r in range(2):
                x = x_ref[:, p * 8 + o, r].reshape(theta.shape[1], phi.shape[0])
                mid = jnp.dot(theta, x, preferred_element_type=jnp.float32)
                k = o * 2 + r
                mid_ref[k * polar_total : (k + 1) * polar_total, :] = mid.astype(jnp.bfloat16)
        raised_ref[...] = jnp.dot(mid_ref[...], phi, preferred_element_type=jnp.float32).reshape(
            raised_ref.shape
        )

        def slab(s, carry):
            rows = pl.ds(pl.multiple_of(s * 8, 8), 8)
            real = imag = None
            for o in range(4):
                c = cos_ref[o, rows, :]
                d = sin_ref[o, rows, :]
                ar, ai = raised_ref[2 * o, rows, :], raised_ref[2 * o + 1, rows, :]
                br, bi = raised_ref[14 - 2 * o, rows, :], raised_ref[15 - 2 * o, rows, :]
                tr = c * (ar + br) - d * (ai - bi)
                ti = d * (ar - br) + c * (ai + bi)
                real = tr if real is None else real + tr
                imag = ti if imag is None else imag + ti
            for r, v in ((0, real), (1, imag)):
                both = jnp.concatenate([v[:, :128], v[:, 128:]], axis=0)
                out_ref[s, p, r] = both.astype(jnp.bfloat16)
            return carry

        lax.fori_loop(0, slabs, slab, 0)


def translate_kernel(slots_ref, kinds_ref, pool_ref, trans_ref, out_ref):
    boxes, entries = out_ref.shape[0], slots_ref.shape[1]

    def box(b, carry):
        def quad(q, acc):
            real, imag = acc
            fr = fi = None
            for j in range(4):
                code = slots_ref[b, q * 4 + j]
                kind = kinds_ref[b, q * 4 + j]
                sr, si = pool_ref[code, 0], pool_ref[code, 1]
                tr, ti = trans_ref[kind, 0], trans_ref[kind, 1]
                er = tr * sr - ti * si
                ei = tr * si + ti * sr
                if j % 2 == 0:
                    fr, fi = er, ei
                else:
                    real = real + (fr + er).astype(jnp.float32)
                    imag = imag + (fi + ei).astype(jnp.float32)
            return real, imag

        zero = jnp.zeros((16, 128), jnp.float32)
        real, imag = lax.fori_loop(0, entries // 4, quad, (zero, zero), unroll=4)
        for r, v in ((0, real), (1, imag)):
            out_ref[b, r, :, 0:128] = v[0:8]
            out_ref[b, r, :, 128:256] = v[8:16]
        return carry

    lax.fori_loop(0, boxes, box, 0)


VMEM = pl.BlockSpec(memory_space=pltpu.VMEM)
SMEM = pl.BlockSpec(memory_space=pltpu.SMEM)


def local(children, interp_theta, interp_phi, translator, send_index, list_slots, list_kinds):
    samp_count = lax.axis_size("samp")
    polar_total = interp_theta.shape[1]
    azimuth_total = interp_phi.shape[1]
    child_boxes, _, rows, child_azimuth = children.shape
    own_children = child_boxes // samp_count
    own_parents = own_children // 8
    parent_boxes = child_boxes // 8
    out_rows = polar_total // samp_count

    x = children.reshape(samp_count, own_children, 2, rows, child_azimuth)
    x = lax.all_to_all(x, "samp", split_axis=0, concat_axis=0, tiled=True)
    cosine, sine = phase_tables(polar_total, azimuth_total)
    mine = pl.pallas_call(
        aggregate_kernel,
        out_shape=jax.ShapeDtypeStruct(
            (samp_count, own_parents, 2, 2 * out_rows, azimuth_total // 2), jnp.bfloat16
        ),
        in_specs=[VMEM] * 5,
        out_specs=VMEM,
        scratch_shapes=[
            pltpu.VMEM((16 * polar_total, child_azimuth), jnp.bfloat16),
            pltpu.VMEM((16, polar_total, azimuth_total), jnp.float32),
        ],
        compiler_params=pltpu.CompilerParams(vmem_limit_bytes=16 << 20),
        name="aggregate",
    )(x, interp_theta.T, interp_phi, cosine, sine)
    mine = lax.all_to_all(mine, "samp", split_axis=0, concat_axis=0, tiled=True)
    mine = mine.reshape(parent_boxes, 2, 2 * out_rows, azimuth_total // 2)
    parents = (
        mine.reshape(parent_boxes, 2, 2, out_rows, azimuth_total // 2)
        .transpose(0, 1, 3, 2, 4)
        .reshape(parent_boxes, 2, out_rows, azimuth_total)
    )

    outgoing = mine[send_index[0].reshape(-1)]
    outgoing = outgoing.reshape(send_index.shape[1], send_index.shape[2], *mine.shape[1:])
    received = lax.all_to_all(outgoing, "box", split_axis=0, concat_axis=0, tiled=True)
    pool = received.reshape(-1, *mine.shape[1:])
    trans = (
        translator.reshape(-1, 2, out_rows, 2, azimuth_total // 2)
        .transpose(0, 1, 3, 2, 4)
        .reshape(-1, 2, 2 * out_rows, azimuth_total // 2)
    )
    field = pl.pallas_call(
        translate_kernel,
        out_shape=jax.ShapeDtypeStruct((parent_boxes, 2, out_rows, azimuth_total), jnp.float32),
        in_specs=[SMEM, SMEM, VMEM, VMEM],
        out_specs=VMEM,
        compiler_params=pltpu.CompilerParams(vmem_limit_bytes=16 << 20),
        name="translate",
    )(list_slots, list_kinds, pool, trans)
    return parents, field


def solution(mesh):
    return jax.shard_map(
        local,
        mesh=mesh,
        in_specs=(
            P("box", None, "samp", None),
            P(),
            P(),
            P(None, None, "samp", None),
            P("box", None, None),
            P("box", None),
            P("box", None),
        ),
        out_specs=(P("box", None, "samp", None), P("box", None, "samp", None)),
        check_vma=False,
    )
```

time: 199 us -> 70.7 us (0.36)
  other arithmetic: 73.9 us -> 2.2 us
  local copies, waits for them, and re-layouts: 47.5 us -> 5.7 us
  waiting for transfers between devices: 50.3 us -> 28.8 us
  starting transfers between devices: 5.16 us -> 19.9 us
  between operations: 14.3 us -> 0.7 us
  Pallas kernels: 0 us -> 12.9 us
  matrix products: 7.23 us -> 0 us
    convert_element_type x10 -> x1, other arithmetic: 48.6 us -> 0.01 us  [phase_tables(): sign_y = ((octant >> 1 & 1) * 2 - 1).astype(jnp.float32)[:, None, None]]
    all_gather x1 -> x0, waiting for transfers between devices: 46.4 us -> none  [local(): gathered = lax.all_gather(children, 'samp', axis=2, tiled=True)]
    gather x9 -> x1, local copies, waits for them, and re-layouts: 29.5 us -> 1.66 us  [local(): outgoing = mine[send_index[0].reshape(-1)]]
    reduce_sum x5 -> x0, other arithmetic: 21.9 us -> none  [the longest x4 19 us: local(): jnp.sum(factors[:, :, 0] * sources[:, :, 0] - factors[:, :, 1] * sources[...]
    all_to_all x0 -> x2, waiting for transfers between devices: none -> 13.9 us  [the longest x1 7.3 us: local(): mine = lax.all_to_all(mine, 'samp', split_axis=0, concat_axis=0, tiled=True)]
    pallas_call x0 -> x2, Pallas kernels: none -> 12.9 us  [the longest x1 9.81 us: local(): pl.pallas_call(translate_kernel, out_shape=jax.ShapeDtypeStruct((parent_b...]
    all_to_all x0 -> x2, starting transfers between devices: none -> 12.2 us  [the longest x1 8.56 us: local(): x = lax.all_to_all(x, 'samp', split_axis=0, concat_axis=0, tiled=True)]
    all_gather x1 -> x0, local copies, waits for them, and re-layouts: 12 us -> none  [local(): gathered = lax.all_gather(children, 'samp', axis=2, tiled=True)]
  transfers between devices with their start and end apart: 2 -> 3, of which waited for: 2 -> 3; matrix products, arithmetic and copies ran while one was open for 20% -> 5% of each run, Pallas kernels for 0% -> 0%
where the time goes in v1:
time: 70.7 us; the launch traced here: 70.2 us
  waiting for transfers between devices  28.8 us (41%)
  starting transfers between devices  19.9 us (28%)
  Pallas kernels  12.9 us (18%)
  local copies, waits for them, and re-layouts  5.7 us (8%)
  other arithmetic  2.2 us (3%)
    all_to_all x1, waiting for transfers between devices, local(): lax.all_to_all(outgoing, 'box', split_axis=0, concat_axis=0, tiled=True)  15 us
    pallas_call x1, Pallas kernels, local(): pl.pallas_call(translate_kernel, out_shape=jax.ShapeDtypeStruct((parent_b...  9.81 us
    all_to_all x1, starting transfers between devices, local(): x = lax.all_to_all(x, 'samp', split_axis=0, concat_axis=0, tiled=True)  8.56 us
    all_to_all x1, starting transfers between devices, local(): lax.all_to_all(outgoing, 'box', split_axis=0, concat_axis=0, tiled=True)  7.65 us
    all_to_all x1, waiting for transfers between devices, local(): mine = lax.all_to_all(mine, 'samp', split_axis=0, concat_axis=0, tiled=True)  7.3 us
    all_to_all x1, waiting for transfers between devices, local(): x = lax.all_to_all(x, 'samp', split_axis=0, concat_axis=0, tiled=True)  6.56 us
    all_to_all x1, starting transfers between devices, local(): mine = lax.all_to_all(mine, 'samp', split_axis=0, concat_axis=0, tiled=True)  3.66 us
    unnamed x10, local copies, waits for them, and re-layouts  3.27 us
  transfers between devices with their start and end apart: 3, of which 3 were waited for; matrix products, arithmetic and copies ran while one was open for 5% of the time, Pallas kernels for 0%

profile of v1, /device:TPU:1, one launch (start us, length us, event | category | flops | bytes accessed | tf_op | source)
XLA Modules:
  0.0 70.2 jit_solution(5738551183253199854)
XLA Ops:
  0.6 0.0 copy-start.1
  0.6 8.6 %all-to-all-start = ((bf16[16,16,2,4,128]{4,3,2,1,0:T(4,128)(2,1)}), bf16[16,16,2,4,128]{4,3,2,1,0:T(4,128)(2,1)S(1)}, u32[]{:S(2)}, u32[]{:S(2)}) async-start(bf16[16,16,2,4,128]{4,3,2,1,0:T(4,128)(2,1)} %bitcast.22), calls=%async_computation | async-start | bytes 1048576 | tf_op jit(solution)/shard_map/all_to_all | solution.py:112
  9.4 0.8 %reshape_squeeze.3 = s32[128,1]{0,1:T(1,128)S(1)} reshape(s32[1,8,16]{2,1,0:T(8,128)} %param.11) | data formatting | bytes 1024 | tf_op jit(solution)/shard_map/reshape;squeeze | solution.py:136
  10.1 0.8 %copy.9 = bf16[64,128]{0,1:T(8,128)(2,1)S(1)} copy(bf16[64,128]{1,0:T(8,128)(2,1)} %param.8) | data formatting | bytes 32768 | tf_op args[1]
  11.0 0.1 broadcast_multiply_fusion.1
  11.1 2.0 %fusion = (f32[4,128,256]{2,1,0:T(8,128)S(1)}, f32[4,128,256]{2,1,0:T(8,128)S(1)}) fusion(f32[128]{0:T(128)S(1)} %fusion.5, f32[128,256]{1,0:T(8,128)S(1)} %get-tuple-element.5, f32[4]{0:T(128)S(1)} %get-tuple-element.8, f32[128,256]{1,0:T(8,128)S(1)} %get-tuple-element.4, f32[4]{0:T(128)S(1)} %get-tuple-element.9), kind=kLoop, calls=%fused_computation.2 | loop fusion | flops 655360 | bytes 1311264 | tf_op jit(solution)/shard_map/sin | solution.py:27
  13.0 6.6 %all-to-all-done.x_ref = bf16[16,16,2,4,128]{4,3,2,1,0:T(4,128)(2,1)S(1)} async-done(((bf16[16,16,2,4,128]{4,3,2,1,0:T(4,128)(2,1)}), bf16[16,16,2,4,128]{4,3,2,1,0:T(4,128)(2,1)S(1)}, u32[]{:S(2)}, u32[]{:S(2)}) %all-to-all-start) | async-done | bytes 524320 | tf_op jit(solution)/shard_map/all_to_all | solution.py:112
  19.6 0.0 copy-done.1
  19.6 3.1 %aggregate.1 = bf16[16,2,2,16,128]{4,3,2,1,0:T(8,128)(2,1)} custom-call(bf16[16,16,2,4,128]{4,3,2,1,0:T(4,128)(2,1)S(1)} %all-to-all-done.x_ref, bf16[128,64]{1,0:T(8,128)(2,1)S(1)} %bitcast.19, bf16[128,256]{1,0:T(8,128)(2,1)S(1)} %copy-done.1, f32[4,128,256]{2,1,0:T(8,128)S(1)} %get-tuple-element.3.cos_ref, f32[4,128,256]{2,1,0:T(8,128)S(1)} %get-tuple-element.2.sin_ref), custom_call_target="tpu_custom_call" | custom-call | tf_op jit(solution)/shard_map/aggregate/pallas_call | solution.py:114
  22.6 0.0 copy-start.2
  22.6 0.0 copy-start.3
  22.6 3.7 %all-to-all-start.1 = ((bf16[16,2,2,16,128]{4,3,2,1,0:T(8,128)(2,1)}), bf16[16,2,2,16,128]{4,3,2,1,0:T(8,128)(2,1)S(1)}, u32[]{:S(2)}, u32[]{:S(2)}) async-start(bf16[16,2,2,16,128]{4,3,2,1,0:T(8,128)(2,1)} %aggregate.1), calls=%async_computation.1 | async-start | bytes 524288 | tf_op jit(solution)/shard_map/all_to_all | solution.py:128
  26.3 7.3 %all-to-all-done.1 = bf16[16,2,2,16,128]{4,3,2,1,0:T(8,128)(2,1)S(1)} async-done(((bf16[16,2,2,16,128]{4,3,2,1,0:T(8,128)(2,1)}), bf16[16,2,2,16,128]{4,3,2,1,0:T(8,128)(2,1)S(1)}, u32[]{:S(2)}, u32[]{:S(2)}) %all-to-all-start.1) | async-done | bytes 262176 | tf_op jit(solution)/shard_map/all_to_all | solution.py:128
  33.6 1.7 %gather_fusion = bf16[128,2,16,128]{3,2,1,0:T(8,128)(2,1)} fusion(bf16[32,2,16,128]{3,2,1,0:T(8,128)(2,1)S(1)} %bitcast.20, s32[1024]{0:T(1024)S(1)} %pad_clamp_fusion), kind=kCustom, calls=%fused_computation | custom fusion | bytes 2097664 | tf_op jit(solution)/shard_map/gather | solution.py:136
  35.3 7.7 %all-to-all-start.2 = ((bf16[8,16,2,16,128]{4,3,2,1,0:T(8,128)(2,1)}), bf16[8,16,2,16,128]{4,3,2,1,0:T(8,128)(2,1)S(1)}, u32[]{:S(2)}, u32[]{:S(2)}) async-start(bf16[8,16,2,16,128]{4,3,2,1,0:T(8,128)(2,1)} %bitcast.7), calls=%async_computation.2 | async-start | bytes 2097152 | tf_op jit(solution)/shard_map/all_to_all | solution.py:138
  43.0 15.0 %all-to-all-done.2 = bf16[8,16,2,16,128]{4,3,2,1,0:T(8,128)(2,1)S(1)} async-done(((bf16[8,16,2,16,128]{4,3,2,1,0:T(8,128)(2,1)}), bf16[8,16,2,16,128]{4,3,2,1,0:T(8,128)(2,1)S(1)}, u32[]{:S(2)}, u32[]{:S(2)}) %all-to-all-start.2) | async-done | bytes 1048608 | tf_op jit(solution)/shard_map/all_to_all | solution.py:138
  57.9 0.0 copy-done.2
  57.9 0.0 copy-done.3
  57.9 0.0 copy-start
  57.9 1.7 %copy-done = bf16[316,2,8,256]{3,2,1,0:T(8,128)(2,1)S(1)} copy-done((bf16[316,2,8,256]{3,2,1,0:T(8,128)(2,1)S(1)}, bf16[316,2,8,256]{3,2,1,0:T(8,128)(2,1)}, u32[]{:S(2)}) %copy-start) | copy-done | bytes 2588696
  59.7 9.8 %translate.1 = f32[32,2,8,256]{3,2,1,0:T(8,128)} custom-call(s32[32,64]{1,0:T(8,128)S(1)} %copy-done.2, s32[32,64]{1,0:T(8,128)S(1)} %copy-done.3, bf16[128,2,16,128]{3,2,1,0:T(8,128)(2,1)S(1)} %bitcast.17, bf16[316,2,16,128]{3,2,1,0:T(8,128)(2,1)S(1)} %bitcast.18), custom_call_target="tpu_custom_call" | custom-call | tf_op jit(solution)/shard_map/translate/pallas_call | solution.py:145
  69.5 0.7 %copy.11 = bf16[32,2,8,256]{3,2,1,0:T(8,128)(2,1)} copy(bf16[32,2,8,256]{3,2,1,0:T(8,128)(2,1)S(1)} %bitcast.21) | data formatting | bytes 524288
  (6 shorter events, 0.1 us)
Async XLA Ops:
  0.6 18.9 %copy-start.1 = (bf16[128,256]{1,0:T(8,128)(2,1)S(1)}, bf16[128,256]{1,0:T(8,128)(2,1)}, u32[]{:S(2)}) copy-start(bf16[128,256]{1,0:T(8,128)(2,1)} %phi_ref.1) | copy-start | bytes 196612
  0.6 18.9 %all-to-all-start = ((bf16[16,16,2,4,128]{4,3,2,1,0:T(4,128)(2,1)}), bf16[16,16,2,4,128]{4,3,2,1,0:T(4,128)(2,1)S(1)}, u32[]{:S(2)}, u32[]{:S(2)}) async-start(bf16[16,16,2,4,128]{4,3,2,1,0:T(4,128)(2,1)} %bitcast.22), calls=%async_computation | async-start | bytes 1048576 | tf_op jit(solution)/shard_map/all_to_all | solution.py:112
  22.6 35.3 %copy-start.2 = (s32[32,64]{1,0:T(8,128)S(1)}, s32[32,64]{1,0:T(8,128)}, u32[]{:S(2)}) copy-start(s32[32,64]{1,0:T(8,128)} %slots_ref.1) | copy-start | bytes 24580
  22.6 35.3 %copy-start.3 = (s32[32,64]{1,0:T(8,128)S(1)}, s32[32,64]{1,0:T(8,128)}, u32[]{:S(2)}) copy-start(s32[32,64]{1,0:T(8,128)} %kinds_ref.1) | copy-start | bytes 24580
  22.6 11.0 %all-to-all-start.1 = ((bf16[16,2,2,16,128]{4,3,2,1,0:T(8,128)(2,1)}), bf16[16,2,2,16,128]{4,3,2,1,0:T(8,128)(2,1)S(1)}, u32[]{:S(2)}, u32[]{:S(2)}) async-start(bf16[16,2,2,16,128]{4,3,2,1,0:T(8,128)(2,1)} %aggregate.1), calls=%async_computation.1 | async-start | bytes 524288 | tf_op jit(solution)/shard_map/all_to_all | solution.py:128
  35.3 22.6 %all-to-all-start.2 = ((bf16[8,16,2,16,128]{4,3,2,1,0:T(8,128)(2,1)}), bf16[8,16,2,16,128]{4,3,2,1,0:T(8,128)(2,1)S(1)}, u32[]{:S(2)}, u32[]{:S(2)}) async-start(bf16[8,16,2,16,128]{4,3,2,1,0:T(8,128)(2,1)} %bitcast.7), calls=%async_computation.2 | async-start | bytes 2097152 | tf_op jit(solution)/shard_map/all_to_all | solution.py:138
  57.9 1.7 %copy-start = (bf16[316,2,8,256]{3,2,1,0:T(8,128)(2,1)S(1)}, bf16[316,2,8,256]{3,2,1,0:T(8,128)(2,1)}, u32[]{:S(2)}) copy-start(bf16[316,2,8,256]{3,2,1,0:T(8,128)(2,1)} %param.10) | copy-start | bytes 7766020

commit v2 on v1

v2 whole, which is shorter than its diff:
```python
import functools
import math

import jax
import jax.numpy as jnp
from jax import lax
from jax.experimental import pallas as pl
from jax.experimental.pallas import tpu as pltpu
from jax.sharding import Mesh, PartitionSpec as P

KAPPA_H = 12.0
SAMP = ("x", "z")
BOX = ("y", "c")
STEP = 4
WIDTH = 128
POOL_BLOCKS = (2, 4, 2)
VMEM = pl.BlockSpec(memory_space=pltpu.VMEM)
SMEM = pl.BlockSpec(memory_space=pltpu.SMEM)


def phase_tables(polar_total, azimuth_total):
    polar = (jnp.arange(polar_total, dtype=jnp.int32).astype(jnp.float32) + 0.5) * (
        math.pi / polar_total
    )
    azimuth = jnp.arange(azimuth_total, dtype=jnp.int32).astype(jnp.float32) * (
        2.0 * math.pi / azimuth_total
    )
    octant = jnp.arange(4, dtype=jnp.int32)
    sign_x = ((octant & 1) * 2 - 1).astype(jnp.float32)[:, None, None]
    sign_y = ((octant >> 1 & 1) * 2 - 1).astype(jnp.float32)[:, None, None]
    along_x = jnp.sin(polar)[:, None] * jnp.cos(azimuth)[None, :]
    along_y = jnp.sin(polar)[:, None] * jnp.sin(azimuth)[None, :]
    along_z = jnp.cos(polar)[:, None] + jnp.zeros((1, azimuth_total), jnp.float32)
    phase = KAPPA_H * (sign_x * along_x + sign_y * along_y - along_z)
    return jnp.cos(phase), jnp.sin(phase)


def aggregate_kernel(x_ref, theta_ref, phi_ref, cos_ref, sin_ref, out_ref, mid_ref, raised_ref):
    theta = theta_ref[...]
    phi = phi_ref[...]
    polar_total = theta.shape[0]
    for p in range(out_ref.shape[1]):
        for o in range(8):
            for r in range(2):
                x = x_ref[:, p * 8 + o, r].reshape(theta.shape[1], phi.shape[0])
                mid = jnp.dot(theta, x, preferred_element_type=jnp.float32)
                k = o * 2 + r
                mid_ref[k * polar_total : (k + 1) * polar_total, :] = mid.astype(jnp.bfloat16)
        raised_ref[...] = jnp.dot(mid_ref[...], phi, preferred_element_type=jnp.float32).reshape(
            raised_ref.shape
        )

        def slab(s, carry):
            rows = pl.ds(pl.multiple_of(s * 8, 8), 8)
            real = imag = None
            for o in range(4):
                c = cos_ref[o, rows, :]
                d = sin_ref[o, rows, :]
                ar, ai = raised_ref[2 * o, rows, :], raised_ref[2 * o + 1, rows, :]
                br, bi = raised_ref[14 - 2 * o, rows, :], raised_ref[15 - 2 * o, rows, :]
                tr = c * (ar + br) - d * (ai - bi)
                ti = d * (ar - br) + c * (ai + bi)
                real = tr if real is None else real + tr
                imag = ti if imag is None else imag + ti
            out_ref[s, p, 0] = real.astype(jnp.bfloat16)
            out_ref[s, p, 1] = imag.astype(jnp.bfloat16)
            return carry

        lax.fori_loop(0, out_ref.shape[0], slab, 0)


def widen_kernel(x_ref, out_ref, buffer, sems):
    parts = sems.shape[0]
    size = x_ref.shape[0] // parts

    def copy(i):
        at = pl.ds(i * size, size)
        return pltpu.make_async_copy(x_ref.at[at], buffer.at[at], sems.at[i])

    for i in range(parts):
        copy(i).start()
    for i in range(parts):
        copy(i).wait()

        def widen(k, carry):
            out_ref[k] = buffer[k].astype(jnp.float32)
            return carry

        lax.fori_loop(i * size, (i + 1) * size, widen, 0)


def translate_kernel(k, at_ref, kind_ref, bound_ref, trans_ref, *refs):
    first = k == 0
    if first:
        *blocks, out_ref, parents_ref, pool_ref, sem = refs
        copy = pltpu.make_async_copy(blocks[0], parents_ref, sem)
        copy.start()
    else:
        sum_ref, *blocks, out_ref, pool_ref = refs
    start = 0
    for block in blocks:

        def widen(i, carry, block=block, start=start):
            pool_ref[start + i] = block[i].astype(jnp.float32)
            return carry

        lax.fori_loop(0, block.shape[0], widen, 0, unroll=4)
        start += block.shape[0]
    pool_ref[start] = jnp.zeros(pool_ref.shape[1:], jnp.float32)

    def box(b, carry):
        def group(g, acc):
            real, imag = acc
            for j in range(STEP):
                at, kind = at_ref[g * STEP + j], kind_ref[g * STEP + j]
                sr, si = pool_ref[at, 0], pool_ref[at, 1]
                tr, ti = trans_ref[kind, 0], trans_ref[kind, 1]
                real = real + (tr * sr - ti * si)
                imag = imag + (tr * si + ti * sr)
            return real, imag

        if first:
            zero = jnp.zeros(out_ref.shape[2:], jnp.float32)
            acc = (zero, zero)
        else:
            acc = (sum_ref[b, 0], sum_ref[b, 1])
        real, imag = lax.fori_loop(bound_ref[b, 2 * k], bound_ref[b, 2 * k + 1], group, acc)
        out_ref[b, 0] = real
        out_ref[b, 1] = imag
        return carry

    lax.fori_loop(0, out_ref.shape[0], box, 0)
    if first:
        copy.wait()


def shift(x, axis, step):
    size = lax.axis_size(axis)
    return lax.ppermute(x, axis, [(i, (i + step) % size) for i in range(size)])


def plan_kernel(place_ref, own_ref, after_ref, far_ref, before_ref, slots_ref, kinds_ref, *outs):
    at_ref, kind_ref, bound_ref = outs
    y, c = place_ref[0], place_ref[1]
    cores, receivers, cap = own_ref.shape
    local_boxes = slots_ref.shape[0]
    me = y * cores + c
    slots = slots_ref[...]
    sender = lax.shift_right_logical(slots, 4)
    dy = (lax.shift_right_logical(sender, 1) - y) & 3
    dc = (sender & 1) ^ c
    code = (dy * cores + dc) * cap + (slots & (cap - 1))
    row = jnp.zeros_like(slots)
    tables = (own_ref, after_ref, far_ref, before_ref)
    for k, table in enumerate(tables):
        side = cores if k == 3 else 0
        for core in range(cores):
            for u in range(cap):
                value = table[core, me, u] + (side + core) * local_boxes
                row = jnp.where(code == (k * cores + core) * cap + u, value, row)
    entries = slots.shape[1]
    klass = jnp.where(dy == 0, 0, jnp.where(dy == 2, 2, 1))
    first = lax.broadcasted_iota(jnp.int32, (entries, entries), 0)
    second = lax.broadcasted_iota(jnp.int32, (entries, entries), 1)
    ahead = (first < second).astype(jnp.float32)
    lane = lax.broadcasted_iota(jnp.int32, (local_boxes, WIDTH), 1)
    begin = jnp.zeros((local_boxes, 1), jnp.int32)
    spot = jnp.zeros_like(slots)
    fill = jnp.zeros((local_boxes, WIDTH), jnp.int32)
    line = lax.broadcasted_iota(jnp.int32, (local_boxes, WIDTH), 0) * (WIDTH // STEP)
    bound = line
    for k, rows in enumerate(POOL_BLOCKS):
        mine = klass == k
        ones = mine.astype(jnp.float32)
        inside = jnp.dot(ones, ahead, preferred_element_type=jnp.float32).astype(jnp.int32)
        count = jnp.sum(mine.astype(jnp.int32), axis=1, keepdims=True)
        spot = jnp.where(mine, begin + inside, spot)
        end = begin + ((count + STEP - 1) & -STEP)
        fill = jnp.where((lane >= begin) & (lane < end), rows * local_boxes, fill)
        bound = bound + jnp.where(lane == 2 * k, lax.shift_right_logical(begin, 2), 0)
        bound = bound + jnp.where(lane == 2 * k + 1, lax.shift_right_logical(end, 2), 0)
        begin = end
    bound_ref[...] = bound
    value = (row * 512 + kinds_ref[...] + 1).astype(jnp.float32)
    value = jnp.transpose(value).astype(jnp.int32)
    spot = jnp.transpose(spot.astype(jnp.float32)).astype(jnp.int32)
    wide_lane = lax.broadcasted_iota(jnp.int32, (entries, WIDTH), 1)
    lines = []
    for b in range(local_boxes):
        hit = spot[:, b : b + 1] == wide_lane
        got = jnp.where(hit, value[:, b : b + 1], 0)
        lines.append(jnp.sum(got, axis=0, keepdims=True))
    packed = jnp.concatenate(lines, axis=0)
    packed = jnp.where(packed == 0, fill * 512, packed - 1)
    at_ref[...] = lax.shift_right_logical(packed, 9)
    kind_ref[...] = packed & 511


def slot_tables(send_index):
    own = jnp.concatenate([send_index, shift(send_index, "c", 1)], axis=0)
    return own, shift(own, "y", -1), shift(own, "y", 2), shift(own, "y", 1)


def plan_lists(tables, list_slots, list_kinds):
    place = jnp.stack([lax.axis_index("y"), lax.axis_index("c")]).astype(jnp.int32)
    shape = jax.ShapeDtypeStruct((list_slots.shape[0], WIDTH), jnp.int32)
    at, kind, bound = pl.pallas_call(
        plan_kernel,
        out_shape=[shape] * 3,
        in_specs=[SMEM] * 5 + [VMEM] * 2,
        out_specs=[VMEM] * 3,
        compiler_params=pltpu.CompilerParams(vmem_limit_bytes=4 << 20),
        cost_estimate=pl.CostEstimate(flops=1 << 20, bytes_accessed=1 << 20, transcendentals=0),
        name="plan",
    )(place, *tables, list_slots, list_kinds)
    return at.reshape(-1), kind.reshape(-1), bound


def local(children, interp_theta, interp_phi, translator, send_index, list_slots, list_kinds):
    samp_count = lax.axis_size(SAMP)
    polar_total = interp_theta.shape[1]
    azimuth_total = interp_phi.shape[1]
    child_boxes, _, rows, child_azimuth = children.shape
    own_children = child_boxes // samp_count
    parent_boxes = child_boxes // 8
    out_rows = polar_total // samp_count
    pattern = (2, out_rows, azimuth_total)
    half = parent_boxes // 2

    x = children.reshape(samp_count, own_children, 2, rows, child_azimuth)
    x = lax.all_to_all(x, SAMP, split_axis=0, concat_axis=0, tiled=True)

    cosine, sine = phase_tables(polar_total, azimuth_total)
    theta = interp_theta.T
    tables = slot_tables(send_index)
    x, *tables = lax.optimization_barrier((x, *tables))
    mine = pl.pallas_call(
        aggregate_kernel,
        out_shape=jax.ShapeDtypeStruct((samp_count, own_children // 8) + pattern, jnp.bfloat16),
        in_specs=[VMEM] * 5,
        out_specs=VMEM,
        scratch_shapes=[
            pltpu.VMEM((16 * polar_total, child_azimuth), jnp.bfloat16),
            pltpu.VMEM((16, polar_total, azimuth_total), jnp.float32),
        ],
        compiler_params=pltpu.CompilerParams(vmem_limit_bytes=12 << 20),
        cost_estimate=pl.CostEstimate(flops=335 << 20, bytes_accessed=4 << 20, transcendentals=0),
        name="aggregate",
    )(x, theta, interp_phi, cosine, sine)
    mine = lax.all_to_all(mine, SAMP, split_axis=0, concat_axis=0, tiled=True)
    at, kind, bound = plan_lists(tables, list_slots, list_kinds)
    mine, at, kind, bound = lax.optimization_barrier((mine, at, kind, bound))
    own = mine.reshape((parent_boxes,) + pattern)
    after = shift(own, "y", -1)
    before = shift(own, "y", 1)
    other = shift(own, "c", 1)
    source, own = lax.optimization_barrier((translator, own))
    wide = pl.pallas_call(
        widen_kernel,
        out_shape=pltpu.VMEM(translator.shape, jnp.float32),
        in_specs=[pl.BlockSpec(memory_space=pltpu.HBM)],
        out_specs=VMEM,
        scratch_shapes=[
            pltpu.VMEM(translator.shape, jnp.bfloat16),
            pltpu.SemaphoreType.DMA((4,)),
        ],
        compiler_params=pltpu.CompilerParams(vmem_limit_bytes=56 << 20),
        cost_estimate=pl.CostEstimate(flops=4 << 20, bytes_accessed=8 << 20, transcendentals=0),
        name="widen",
    )(source)

    def translate(k, blocks, so_far):
        shape = (parent_boxes,) + pattern
        out = [(pltpu.VMEM if k < 2 else jax.ShapeDtypeStruct)(shape, jnp.float32)]
        specs = [VMEM]
        scratch = [pltpu.VMEM((POOL_BLOCKS[k] * parent_boxes + 1,) + pattern, jnp.float32)]
        if k == 0:
            out.append(jax.ShapeDtypeStruct(shape, jnp.bfloat16))
            specs.append(pl.BlockSpec(memory_space=pltpu.HBM))
            scratch.append(pltpu.SemaphoreType.DMA)
        return pl.pallas_call(
            functools.partial(translate_kernel, k),
            out_shape=out,
            in_specs=[SMEM] * 3 + [VMEM] * (1 + len(so_far) + len(blocks)),
            out_specs=specs,
            scratch_shapes=scratch,
            compiler_params=pltpu.CompilerParams(vmem_limit_bytes=8 << 20),
            cost_estimate=pl.CostEstimate(
                flops=16 << 20, bytes_accessed=8 << 20, transcendentals=0
            ),
            name=f"translate_{k}",
        )(at, kind, bound, wide, *so_far, *blocks)

    field, parents = translate(0, [own, other], [])
    after, before, field = lax.optimization_barrier((after, before, field))
    far = [shift(before[:half], "y", 1), shift(after[half:], "y", -1)]
    near = [after, shift(after, "c", 1), before, shift(before, "c", 1)]
    (field,) = translate(1, near, [field])
    *far, field = lax.optimization_barrier((*far, field))
    across = [shift(v, "c", 1) for v in far]
    (field,) = translate(2, far + across, [field])
    return parents, field


def solution(mesh):
    y_count, x_count = 4, 4
    fine = Mesh(
        mesh.devices.reshape(y_count, mesh.shape["box"] // y_count, x_count, -1),
        BOX + SAMP,
    )
    return jax.shard_map(
        local,
        mesh=fine,
        in_specs=(
            P(BOX, None, SAMP, None),
            P(),
            P(),
            P(None, None, SAMP, None),
            P(BOX, None, None),
            P(BOX, None),
            P(BOX, None),
        ),
        out_specs=(P(BOX, None, SAMP, None), P(BOX, None, SAMP, None)),
        check_vma=False,
    )
```

time: 70.7 us -> 68.5 us (0.969)
  waiting for transfers between devices: 28.8 us -> 10.3 us
  Pallas kernels: 12.9 us -> 24.3 us
  starting transfers between devices: 19.9 us -> 27.9 us
  local copies, waits for them, and re-layouts: 5.7 us -> 2.39 us
    all_to_all x3 -> x2, waiting for transfers between devices: 28.8 us -> 7.25 us  [the longest x1 5.26 us: local(): mine = lax.all_to_all(mine, SAMP, split_axis=0, concat_axis=0, tiled=True)]
    ppermute x0 -> x13, starting transfers between devices: none -> 15.7 us  [shift(): return lax.ppermute(x, axis, [(i, (i + step) % size) for i in range(size)])]
    pallas_call x1 -> x5, Pallas kernels: 9.81 us -> 21.2 us  [the longest x3 16 us: translate(): pl.pallas_call(functools.partial(translate_kernel, k), out_shape=out, in_...]
    all_to_all x3 -> x2, starting transfers between devices: 19.9 us -> 12.2 us  [the longest x1 7.71 us: local(): x = lax.all_to_all(x, SAMP, split_axis=0, concat_axis=0, tiled=True)]
    ppermute x0 -> x13, waiting for transfers between devices: none -> 3.06 us  [shift(): return lax.ppermute(x, axis, [(i, (i + step) % size) for i in range(size)])]
    gather x1 -> x0, local copies, waits for them, and re-layouts: 1.66 us -> none  [local(): outgoing = mine[send_index[0].reshape(-1)]]
    unnamed x10 -> x8, local copies, waits for them, and re-layouts: 3.27 us -> 2.36 us
    another operation x1 -> x0, local copies, waits for them, and re-layouts: 0.77 us -> none  [local(): outgoing = mine[send_index[0].reshape(-1)]]
  transfers between devices with their start and end apart: 3 -> 15, of which waited for: 3 -> 7; matrix products, arithmetic and copies ran while one was open for 5% -> 6% of each run, Pallas kernels for 0% -> 24%
where the time goes in v2:
time: 68.5 us; the launch traced here: 68 us
  starting transfers between devices  27.9 us (41%)
  Pallas kernels  24.3 us (35%)
  waiting for transfers between devices  10.3 us (15%)
  local copies, waits for them, and re-layouts  2.39 us (3%)
  other arithmetic  2.26 us (3%)
  between operations  0.81 us (1%)
    pallas_call x3, Pallas kernels, translate(): pl.pallas_call(functools.partial(translate_kernel, k), out_shape=out, in_...  16 us
    ppermute x13, starting transfers between devices, shift(): return lax.ppermute(x, axis, [(i, (i + step) % size) for i in range(size)])  15.7 us
    all_to_all x1, starting transfers between devices, local(): x = lax.all_to_all(x, SAMP, split_axis=0, concat_axis=0, tiled=True)  7.71 us
    all_to_all x1, waiting for transfers between devices, local(): mine = lax.all_to_all(mine, SAMP, split_axis=0, concat_axis=0, tiled=True)  5.26 us
    all_to_all x1, starting transfers between devices, local(): mine = lax.all_to_all(mine, SAMP, split_axis=0, concat_axis=0, tiled=True)  4.49 us
    pallas_call x1, Pallas kernels, local(): pl.pallas_call(widen_kernel, out_shape=pltpu.VMEM(translator.shape, jnp.f...  3.09 us
    ppermute x13, waiting for transfers between devices, shift(): return lax.ppermute(x, axis, [(i, (i + step) % size) for i in range(size)])  3.06 us
    pallas_call x1, Pallas kernels, local(): pl.pallas_call(aggregate_kernel, out_shape=jax.ShapeDtypeStruct((samp_cou...  3.06 us
  transfers between devices with their start and end apart: 15, of which 7 were waited for; matrix products, arithmetic and copies ran while one was open for 6% of the time, Pallas kernels for 24%

profile of v2, /device:TPU:1, one launch (start us, length us, event | category | flops | bytes accessed | tf_op | source)
XLA Modules:
  0.0 68.0 jit_solution(9730409065585446070)
XLA Ops:
  0.6 0.0 copy-start.1
  0.6 0.0 copy-start.2
  0.7 1.5 %collective-permute-start = (s32[1,8,16]{2,1,0:T(8,128)}, s32[1,8,16]{2,1,0:T(8,128)S(1)}, u32[]{:S(2)}, u32[]{:S(2)}) collective-permute-start(s32[1,8,16]{2,1,0:T(8,128)} %param.11), channel_id=1, source_target_pairs={{0,16},{16,0},{1,17},{17,1},{2,18},{18,2},{3,19},{19,3},{4,20},{20... | collective-permute-start | bytes 1544 | tf_op jit(solution)/shard_map/ppermute | solution.py:139
  2.1 7.7 %all-to-all-start = ((bf16[16,16,2,4,128]{4,3,2,1,0:T(4,128)(2,1)}), bf16[16,16,2,4,128]{4,3,2,1,0:T(4,128)(2,1)S(1)}, u32[]{:S(2)}, u32[]{:S(2)}) async-start(bf16[16,16,2,4,128]{4,3,2,1,0:T(4,128)(2,1)} %bitcast.18), calls=%async_computation | async-start | bytes 1048576 | tf_op jit(solution)/shard_map/all_to_all | solution.py:231
  9.8 0.7 %constant_dynamic-update-slice_fusion.1 = s32[2,8,16]{2,1,0:T(8,128)S(1)} fusion(s32[1,8,16]{2,1,0:T(8,128)} %param.11), kind=kLoop, calls=%fused_computation.6 | loop fusion | bytes 4608
  10.6 0.1 broadcast_multiply_fusion.1
  10.8 0.0 collective-permute-done
  10.8 2.8 %collective-permute-start.1 = (s32[2,8,16]{2,1,0:T(8,128)S(1)}, s32[2,8,16]{2,1,0:T(8,128)S(1)}, u32[]{:S(2)}, u32[]{:S(2)}) collective-permute-start(s32[2,8,16]{2,1,0:T(8,128)S(1)} %constant_dynamic-update-slice_fusion.own_ref), channel_id=1, source_target_pairs={{0,96},{32,0},{64,32},{96,64},{1,97},{33,1},{65,33},{97,65},{2,98}... | collective-permute-start | bytes 3080 | tf_op jit(solution)/shard_map/ppermute | solution.py:139
  13.6 0.3 collective-permute-start.2
  13.9 0.7 %collective-permute-start.3 = (s32[2,8,16]{2,1,0:T(8,128)S(1)}, s32[2,8,16]{2,1,0:T(8,128)S(1)}, u32[]{:S(2)}, u32[]{:S(2)}) collective-permute-start(s32[2,8,16]{2,1,0:T(8,128)S(1)} %constant_dynamic-update-slice_fusion.own_ref), channel_id=1, source_target_pairs={{0,32},{32,64},{64,96},{96,0},{1,33},{33,65},{65,97},{97,1},{2,34}... | collective-permute-start | bytes 3080 | tf_op jit(solution)/shard_map/ppermute | solution.py:139
  14.6 2.0 %fusion = (f32[4,128,256]{2,1,0:T(8,128)S(1)}, f32[4,128,256]{2,1,0:T(8,128)S(1)}) fusion(f32[128]{0:T(128)S(1)} %fusion.4, f32[128,256]{1,0:T(8,128)S(1)} %get-tuple-element.49, f32[4]{0:T(128)S(1)} %get-tuple-element.52, f32[128,256]{1,0:T(8,128)S(1)} %get-tuple-element.48, f32[4]{0:T(128)S(1)} %get-tuple-element.53), kind=kLoop, calls=%fused_computation.1 | loop fusion | flops 655360 | bytes 1311264 | tf_op jit(solution)/shard_map/sin | solution.py:35
  16.6 0.8 %copy.9 = bf16[64,128]{0,1:T(8,128)(2,1)S(1)} copy(bf16[64,128]{1,0:T(8,128)(2,1)} %param.8) | data formatting | bytes 32768 | tf_op args[1]
  17.4 0.0 collective-permute-done.1.after_ref
  17.4 0.5 collective-permute-done.2.far_ref
  17.9 0.1 collective-permute-done.3.before_ref
  18.0 2.0 %all-to-all-done.x_ref = bf16[16,16,2,4,128]{4,3,2,1,0:T(4,128)(2,1)S(1)} async-done(((bf16[16,16,2,4,128]{4,3,2,1,0:T(4,128)(2,1)}), bf16[16,16,2,4,128]{4,3,2,1,0:T(4,128)(2,1)S(1)}, u32[]{:S(2)}, u32[]{:S(2)}) %all-to-all-start) | async-done | bytes 524320 | tf_op jit(solution)/shard_map/all_to_all | solution.py:231
  20.0 0.0 copy-start
  20.0 0.8 %copy-done = bf16[128,256]{1,0:T(8,128)(2,1)S(1)} copy-done((bf16[128,256]{1,0:T(8,128)(2,1)S(1)}, bf16[128,256]{1,0:T(8,128)(2,1)}, u32[]{:S(2)}) %copy-start) | copy-done | bytes 65560
  20.8 3.1 %aggregate.1 = bf16[16,2,2,8,256]{4,3,2,1,0:T(8,128)(2,1)} custom-call(bf16[16,16,2,4,128]{4,3,2,1,0:T(4,128)(2,1)S(1)} %all-to-all-done.x_ref, bf16[128,64]{1,0:T(8,128)(2,1)S(1)} %bitcast.17, bf16[128,256]{1,0:T(8,128)(2,1)S(1)} %copy-done, f32[4,128,256]{2,1,0:T(8,128)S(1)} %get-tuple-element.47.cos_ref, f32[4,128,256]{2,1,0:T(8,128)S(1)} %get-tuple-element.46.sin_ref), custom_call_target="tpu_custom_call" | custom-call | flops 351272960 | bytes 4194304 | tf_op jit(solution)/shard_map/aggregate/pallas_call | solution.py:237
  23.9 4.5 %all-to-all-start.1 = ((bf16[16,2,2,8,256]{4,3,2,1,0:T(8,128)(2,1)}), bf16[16,2,2,8,256]{4,3,2,1,0:T(8,128)(2,1)S(1)}, u32[]{:S(2)}, u32[]{:S(2)}) async-start(bf16[16,2,2,8,256]{4,3,2,1,0:T(8,128)(2,1)} %aggregate.1), calls=%async_computation.1 | async-start | bytes 524288 | tf_op jit(solution)/shard_map/all_to_all | solution.py:250
  28.4 0.1 pad_add_fusion.place_ref
  28.4 0.0 copy-done.1
  28.4 0.0 copy-done.2
  28.4 2.1 %plan.1 = (s32[32,128]{1,0:T(8,128)S(1)}, s32[32,128]{1,0:T(8,128)S(1)}, s32[32,128]{1,0:T(8,128)S(1)}) custom-call(s32[2]{0:T(128)S(1)} %pad_add_fusion.place_ref, s32[2,8,16]{2,1,0:T(8,128)S(1)} %constant_dynamic-update-slice_fusion.own_ref, s32[2,8,16]{2,1,0:T(8,128)S(1)} %collective-permute-done.1.after_ref, ...), custom_call_target="tpu_custom_call" | custom-call | flops 1048576 | bytes 1048576 | tf_op jit(solution)/shard_map/plan/pallas_call | solution.py:207
  30.6 5.3 %all-to-all-done.1 = bf16[16,2,2,8,256]{4,3,2,1,0:T(8,128)(2,1)S(1)} async-done(((bf16[16,2,2,8,256]{4,3,2,1,0:T(8,128)(2,1)}), bf16[16,2,2,8,256]{4,3,2,1,0:T(8,128)(2,1)S(1)}, u32[]{:S(2)}, u32[]{:S(2)}) %all-to-all-start.1) | async-done | bytes 262176 | tf_op jit(solution)/shard_map/all_to_all | solution.py:250
  35.8 3.4 %collective-permute-start.4 = (bf16[32,2,8,256]{3,2,1,0:T(8,128)(2,1)S(1)}, bf16[32,2,8,256]{3,2,1,0:T(8,128)(2,1)S(1)}, u32[]{:S(2)}, u32[]{:S(2)}) collective-permute-start(bf16[32,2,8,256]{3,2,1,0:T(8,128)(2,1)S(1)} %bitcast.7), channel_id=1, source_target_pairs={{0,16},{16,0},{1,17},{17,1},{2,18},{18,2},{3,19},{19,3},{4,20},{20... | collective-permute-start | bytes 786440 | tf_op jit(solution)/shard_map/ppermute | solution.py:139
  39.3 1.6 %collective-permute-start.5 = (bf16[32,2,8,256]{3,2,1,0:T(8,128)(2,1)S(1)}, bf16[32,2,8,256]{3,2,1,0:T(8,128)(2,1)S(1)}, u32[]{:S(2)}, u32[]{:S(2)}) collective-permute-start(bf16[32,2,8,256]{3,2,1,0:T(8,128)(2,1)S(1)} %bitcast.8), channel_id=1, source_target_pairs={{0,96},{32,0},{64,32},{96,64},{1,97},{33,1},{65,33},{97,65},{2,98}... | collective-permute-start | bytes 786440 | tf_op jit(solution)/shard_map/ppermute | solution.py:139
  40.9 0.0 collective-permute-start.6
  40.9 3.1 %widen.1.trans_ref = f32[316,2,8,256]{3,2,1,0:T(8,128)S(1)} custom-call(bf16[316,2,8,256]{3,2,1,0:T(8,128)(2,1)} %x_ref), custom_call_target="tpu_custom_call" | custom-call | flops 4194304 | bytes 8388608 | tf_op jit(solution)/shard_map/widen/pallas_call | solution.py:258
  44.0 0.0 collective-permute-done.4.refs_1_
  44.0 4.4 %translate_0.1 = (f32[32,2,8,256]{3,2,1,0:T(8,128)S(1)}, bf16[32,2,8,256]{3,2,1,0:T(8,128)(2,1)}) custom-call(s32[4096]{0:T(1024)S(1)} %bitcast.11, s32[4096]{0:T(1024)S(1)} %bitcast.14, s32[32,128]{1,0:T(8,128)S(1)} %get-tuple-element.34.bound_ref, f32[316,2,8,256]{3,2,1,0:T(8,128)S(1)} %widen.1.trans_ref, bf16[32,2,8,256]{3,2,1,0:T(8,128)(2,1)S(1)} %bitcast.10, ...), custom_call_target="tpu_custom_call" | custom-call | flops 16777216 | bytes 8388608 | tf_op jit(solution)/shard_map/translate_0/pallas_call | solution.py:281
  48.4 0.0 collective-permute-done.5.refs_1_
  48.5 1.2 %collective-permute-done.6.refs_3_ = bf16[32,2,8,256]{3,2,1,0:T(8,128)(2,1)S(1)} collective-permute-done((bf16[32,2,8,256]{3,2,1,0:T(8,128)(2,1)S(1)}, bf16[32,2,8,256]{3,2,1,0:T(8,128)(2,1)S(1)}, u32[]{:S(2)}, u32[]{:S(2)}) %collective-permute-start.6) | collective-permute-done | bytes 262176 | tf_op jit(solution)/shard_map/ppermute | solution.py:139
  49.7 1.1 %collective-permute-start.10 = (bf16[32,2,8,256]{3,2,1,0:T(8,128)(2,1)S(1)}, bf16[32,2,8,256]{3,2,1,0:T(8,128)(2,1)S(1)}, u32[]{:S(2)}, u32[]{:S(2)}) collective-permute-start(bf16[32,2,8,256]{3,2,1,0:T(8,128)(2,1)S(1)} %collective-permute-done.6.refs_3_), channel_id=1, source_target_pairs={{0,16},{16,0},{1,17},{17,1},{2,18},{18,2},{3,19},{19,3},{4,20},{20... | collective-permute-start | bytes 786440 | tf_op jit(solution)/shard_map/ppermute | solution.py:139
  50.8 0.0 collective-permute-start.9
  50.9 0.1 collective-permute-start.7
  51.0 2.7 %collective-permute-start.8 = (bf16[16,2,8,256]{3,2,1,0:T(8,128)(2,1)S(1)}, bf16[16,2,8,256]{3,2,1,0:T(8,128)(2,1)S(1)}, u32[]{:S(2)}, u32[]{:S(2)}) collective-permute-start(bf16[16,2,8,256]{3,2,1,0:T(8,128)(2,1)S(1)} %slice.7), channel_id=1, source_target_pairs={{0,96},{32,0},{64,32},{96,64},{1,97},{33,1},{65,33},{97,65},{2,98}... | collective-permute-start | bytes 393224 | tf_op jit(solution)/shard_map/ppermute | solution.py:139
  53.6 0.0 collective-permute-done.10.refs_4_
  53.6 0.0 collective-permute-done.9.refs_2_
  53.6 6.5 %translate_1.1.refs_0_ = f32[32,2,8,256]{3,2,1,0:T(8,128)S(1)} custom-call(s32[4096]{0:T(1024)S(1)} %bitcast.12, s32[4096]{0:T(1024)S(1)} %bitcast.15, s32[32,128]{1,0:T(8,128)S(1)} %get-tuple-element.34.bound_ref, f32[316,2,8,256]{3,2,1,0:T(8,128)S(1)} %widen.1.trans_ref, f32[32,2,8,256]{3,2,1,0:T(8,128)S(1)} %get-tuple-element.42.refs_0_, ...), custom_call_target="tpu_custom_call" | custom-call | flops 16777216 | bytes 8388608 | tf_op jit(solution)/shard_map/translate_1/pallas_call | solution.py:281
  60.1 0.0 collective-permute-done.7.refs_1_
  60.2 0.0 collective-permute-done.8.refs_2_
  60.2 1.4 %collective-permute-start.11 = (bf16[16,2,8,256]{3,2,1,0:T(8,128)(2,1)S(1)}, bf16[16,2,8,256]{3,2,1,0:T(8,128)(2,1)S(1)}, u32[]{:S(2)}, u32[]{:S(2)}) collective-permute-start(bf16[16,2,8,256]{3,2,1,0:T(8,128)(2,1)S(1)} %collective-permute-done.7.refs_1_), channel_id=1, source_target_pairs={{0,16},{16,0},{1,17},{17,1},{2,18},{18,2},{3,19},{19,3},{4,20},{20... | collective-permute-start | bytes 393224 | tf_op jit(solution)/shard_map/ppermute | solution.py:139
  61.5 0.1 collective-permute-start.12
  61.6 0.9 %collective-permute-done.11.refs_3_ = bf16[16,2,8,256]{3,2,1,0:T(8,128)(2,1)S(1)} collective-permute-done((bf16[16,2,8,256]{3,2,1,0:T(8,128)(2,1)S(1)}, bf16[16,2,8,256]{3,2,1,0:T(8,128)(2,1)S(1)}, u32[]{:S(2)}, u32[]{:S(2)}) %collective-permute-start.11) | collective-permute-done | bytes 131104 | tf_op jit(solution)/shard_map/ppermute | solution.py:139
  62.5 0.4 collective-permute-done.12.refs_4_
  62.9 5.1 %translate_2.1 = f32[32,2,8,256]{3,2,1,0:T(8,128)} custom-call(s32[4096]{0:T(1024)S(1)} %bitcast.13, s32[4096]{0:T(1024)S(1)} %bitcast.16, s32[32,128]{1,0:T(8,128)S(1)} %get-tuple-element.34.bound_ref, f32[316,2,8,256]{3,2,1,0:T(8,128)S(1)} %widen.1.trans_ref, f32[32,2,8,256]{3,2,1,0:T(8,128)S(1)} %translate_1.1.refs_0_, ...), custom_call_target="tpu_custom_call" | custom-call | flops 16777216 | bytes 8388608 | tf_op jit(solution)/shard_map/translate_2/pallas_call | solution.py:281
  (7 shorter events, 0.2 us)
Async XLA Ops:
  0.6 27.8 %copy-start.1 = (s32[32,64]{1,0:T(8,128)S(1)}, s32[32,64]{1,0:T(8,128)}, u32[]{:S(2)}) copy-start(s32[32,64]{1,0:T(8,128)} %slots_ref.1) | copy-start | bytes 24580
  0.6 27.8 %copy-start.2 = (s32[32,64]{1,0:T(8,128)S(1)}, s32[32,64]{1,0:T(8,128)}, u32[]{:S(2)}) copy-start(s32[32,64]{1,0:T(8,128)} %kinds_ref.1) | copy-start | bytes 24580
  0.7 10.1 %collective-permute-start = (s32[1,8,16]{2,1,0:T(8,128)}, s32[1,8,16]{2,1,0:T(8,128)S(1)}, u32[]{:S(2)}, u32[]{:S(2)}) collective-permute-start(s32[1,8,16]{2,1,0:T(8,128)} %param.11), channel_id=1, source_target_pairs={{0,16},{16,0},{1,17},{17,1},{2,18},{18,2},{3,19},{19,3},{4,20},{20... | collective-permute-start | bytes 1544 | tf_op jit(solution)/shard_map/ppermute | solution.py:139
  2.1 17.9 %all-to-all-start = ((bf16[16,16,2,4,128]{4,3,2,1,0:T(4,128)(2,1)}), bf16[16,16,2,4,128]{4,3,2,1,0:T(4,128)(2,1)S(1)}, u32[]{:S(2)}, u32[]{:S(2)}) async-start(bf16[16,16,2,4,128]{4,3,2,1,0:T(4,128)(2,1)} %bitcast.18), calls=%async_computation | async-start | bytes 1048576 | tf_op jit(solution)/shard_map/all_to_all | solution.py:231
  10.8 6.6 %collective-permute-start.1 = (s32[2,8,16]{2,1,0:T(8,128)S(1)}, s32[2,8,16]{2,1,0:T(8,128)S(1)}, u32[]{:S(2)}, u32[]{:S(2)}) collective-permute-start(s32[2,8,16]{2,1,0:T(8,128)S(1)} %constant_dynamic-update-slice_fusion.own_ref), channel_id=1, source_target_pairs={{0,96},{32,0},{64,32},{96,64},{1,97},{33,1},{65,33},{97,65},{2,98}... | collective-permute-start | bytes 3080 | tf_op jit(solution)/shard_map/ppermute | solution.py:139
  13.6 4.3 %collective-permute-start.2 = (s32[2,8,16]{2,1,0:T(8,128)S(1)}, s32[2,8,16]{2,1,0:T(8,128)S(1)}, u32[]{:S(2)}, u32[]{:S(2)}) collective-permute-start(s32[2,8,16]{2,1,0:T(8,128)S(1)} %constant_dynamic-update-slice_fusion.own_ref), channel_id=1, source_target_pairs={{0,64},{32,96},{64,0},{96,32},{1,65},{33,97},{65,1},{97,33},{2,66}... | collective-permute-start | bytes 3080 | tf_op jit(solution)/shard_map/ppermute | solution.py:139
  13.9 4.0 %collective-permute-start.3 = (s32[2,8,16]{2,1,0:T(8,128)S(1)}, s32[2,8,16]{2,1,0:T(8,128)S(1)}, u32[]{:S(2)}, u32[]{:S(2)}) collective-permute-start(s32[2,8,16]{2,1,0:T(8,128)S(1)} %constant_dynamic-update-slice_fusion.own_ref), channel_id=1, source_target_pairs={{0,32},{32,64},{64,96},{96,0},{1,33},{33,65},{65,97},{97,1},{2,34}... | collective-permute-start | bytes 3080 | tf_op jit(solution)/shard_map/ppermute | solution.py:139
  20.0 0.8 %copy-start = (bf16[128,256]{1,0:T(8,128)(2,1)S(1)}, bf16[128,256]{1,0:T(8,128)(2,1)}, u32[]{:S(2)}) copy-start(bf16[128,256]{1,0:T(8,128)(2,1)} %phi_ref.1) | copy-start | bytes 196612
  23.9 12.0 %all-to-all-start.1 = ((bf16[16,2,2,8,256]{4,3,2,1,0:T(8,128)(2,1)}), bf16[16,2,2,8,256]{4,3,2,1,0:T(8,128)(2,1)S(1)}, u32[]{:S(2)}, u32[]{:S(2)}) async-start(bf16[16,2,2,8,256]{4,3,2,1,0:T(8,128)(2,1)} %aggregate.1), calls=%async_computation.1 | async-start | bytes 524288 | tf_op jit(solution)/shard_map/all_to_all | solution.py:250
  35.8 8.2 %collective-permute-start.4 = (bf16[32,2,8,256]{3,2,1,0:T(8,128)(2,1)S(1)}, bf16[32,2,8,256]{3,2,1,0:T(8,128)(2,1)S(1)}, u32[]{:S(2)}, u32[]{:S(2)}) collective-permute-start(bf16[32,2,8,256]{3,2,1,0:T(8,128)(2,1)S(1)} %bitcast.7), channel_id=1, source_target_pairs={{0,16},{16,0},{1,17},{17,1},{2,18},{18,2},{3,19},{19,3},{4,20},{20... | collective-permute-start | bytes 786440 | tf_op jit(solution)/shard_map/ppermute | solution.py:139
  39.3 9.2 %collective-permute-start.5 = (bf16[32,2,8,256]{3,2,1,0:T(8,128)(2,1)S(1)}, bf16[32,2,8,256]{3,2,1,0:T(8,128)(2,1)S(1)}, u32[]{:S(2)}, u32[]{:S(2)}) collective-permute-start(bf16[32,2,8,256]{3,2,1,0:T(8,128)(2,1)S(1)} %bitcast.8), channel_id=1, source_target_pairs={{0,96},{32,0},{64,32},{96,64},{1,97},{33,1},{65,33},{97,65},{2,98}... | collective-permute-start | bytes 786440 | tf_op jit(solution)/shard_map/ppermute | solution.py:139
  40.9 8.8 %collective-permute-start.6 = (bf16[32,2,8,256]{3,2,1,0:T(8,128)(2,1)S(1)}, bf16[32,2,8,256]{3,2,1,0:T(8,128)(2,1)S(1)}, u32[]{:S(2)}, u32[]{:S(2)}) collective-permute-start(bf16[32,2,8,256]{3,2,1,0:T(8,128)(2,1)S(1)} %bitcast.9), channel_id=1, source_target_pairs={{0,32},{32,64},{64,96},{96,0},{1,33},{33,65},{65,97},{97,1},{2,34}... | collective-permute-start | bytes 786440 | tf_op jit(solution)/shard_map/ppermute | solution.py:139
  49.7 3.9 %collective-permute-start.10 = (bf16[32,2,8,256]{3,2,1,0:T(8,128)(2,1)S(1)}, bf16[32,2,8,256]{3,2,1,0:T(8,128)(2,1)S(1)}, u32[]{:S(2)}, u32[]{:S(2)}) collective-permute-start(bf16[32,2,8,256]{3,2,1,0:T(8,128)(2,1)S(1)} %collective-permute-done.6.refs_3_), channel_id=1, source_target_pairs={{0,16},{16,0},{1,17},{17,1},{2,18},{18,2},{3,19},{19,3},{4,20},{20... | collective-permute-start | bytes 786440 | tf_op jit(solution)/shard_map/ppermute | solution.py:139
  50.8 2.8 %collective-permute-start.9 = (bf16[32,2,8,256]{3,2,1,0:T(8,128)(2,1)S(1)}, bf16[32,2,8,256]{3,2,1,0:T(8,128)(2,1)S(1)}, u32[]{:S(2)}, u32[]{:S(2)}) collective-permute-start(bf16[32,2,8,256]{3,2,1,0:T(8,128)(2,1)S(1)} %collective-permute-done.5.refs_1_), channel_id=1, source_target_pairs={{0,16},{16,0},{1,17},{17,1},{2,18},{18,2},{3,19},{19,3},{4,20},{20... | collective-permute-start | bytes 786440 | tf_op jit(solution)/shard_map/ppermute | solution.py:139
  50.9 9.3 %collective-permute-start.7 = (bf16[16,2,8,256]{3,2,1,0:T(8,128)(2,1)S(1)}, bf16[16,2,8,256]{3,2,1,0:T(8,128)(2,1)S(1)}, u32[]{:S(2)}, u32[]{:S(2)}) collective-permute-start(bf16[16,2,8,256]{3,2,1,0:T(8,128)(2,1)S(1)} %slice.6), channel_id=1, source_target_pairs={{0,32},{32,64},{64,96},{96,0},{1,33},{33,65},{65,97},{97,1},{2,34}... | collective-permute-start | bytes 393224 | tf_op jit(solution)/shard_map/ppermute | solution.py:139
  51.0 9.2 %collective-permute-start.8 = (bf16[16,2,8,256]{3,2,1,0:T(8,128)(2,1)S(1)}, bf16[16,2,8,256]{3,2,1,0:T(8,128)(2,1)S(1)}, u32[]{:S(2)}, u32[]{:S(2)}) collective-permute-start(bf16[16,2,8,256]{3,2,1,0:T(8,128)(2,1)S(1)} %slice.7), channel_id=1, source_target_pairs={{0,96},{32,0},{64,32},{96,64},{1,97},{33,1},{65,33},{97,65},{2,98}... | collective-permute-start | bytes 393224 | tf_op jit(solution)/shard_map/ppermute | solution.py:139
  60.2 2.4 %collective-permute-start.11 = (bf16[16,2,8,256]{3,2,1,0:T(8,128)(2,1)S(1)}, bf16[16,2,8,256]{3,2,1,0:T(8,128)(2,1)S(1)}, u32[]{:S(2)}, u32[]{:S(2)}) collective-permute-start(bf16[16,2,8,256]{3,2,1,0:T(8,128)(2,1)S(1)} %collective-permute-done.7.refs_1_), channel_id=1, source_target_pairs={{0,16},{16,0},{1,17},{17,1},{2,18},{18,2},{3,19},{19,3},{4,20},{20... | collective-permute-start | bytes 393224 | tf_op jit(solution)/shard_map/ppermute | solution.py:139
  61.5 1.3 %collective-permute-start.12 = (bf16[16,2,8,256]{3,2,1,0:T(8,128)(2,1)S(1)}, bf16[16,2,8,256]{3,2,1,0:T(8,128)(2,1)S(1)}, u32[]{:S(2)}, u32[]{:S(2)}) collective-permute-start(bf16[16,2,8,256]{3,2,1,0:T(8,128)(2,1)S(1)} %collective-permute-done.8.refs_2_), channel_id=1, source_target_pairs={{0,16},{16,0},{1,17},{17,1},{2,18},{18,2},{3,19},{19,3},{4,20},{20... | collective-permute-start | bytes 393224 | tf_op jit(solution)/shard_map/ppermute | solution.py:139

commit v3 on v2

--- a/solution.py
+++ b/solution.py
@@ -8,14 +8,16 @@
 from jax.experimental.pallas import tpu as pltpu
 from jax.sharding import Mesh, PartitionSpec as P
 
+
 KAPPA_H = 12.0
 SAMP = ("x", "z")
 BOX = ("y", "c")
 STEP = 4
 WIDTH = 128
-POOL_BLOCKS = (2, 4, 2)
+POOL_BLOCKS = (2, 2, 2, 1, 1)
 VMEM = pl.BlockSpec(memory_space=pltpu.VMEM)
 SMEM = pl.BlockSpec(memory_space=pltpu.SMEM)
+HBM = pl.BlockSpec(memory_space=pltpu.HBM)
 
 
 def phase_tables(polar_total, azimuth_total):
@@ -35,18 +37,22 @@
     return jnp.cos(phase), jnp.sin(phase)
 
 
+def prepare_kernel(theta_ref, phi_ref, turned_ref, copy_ref):
+    turned_ref[...] = jnp.transpose(theta_ref[...].astype(jnp.float32)).astype(jnp.bfloat16)
+    copy_ref[...] = phi_ref[...]
+
+
 def aggregate_kernel(x_ref, theta_ref, phi_ref, cos_ref, sin_ref, out_ref, mid_ref, raised_ref):
     theta = theta_ref[...]
-    phi = phi_ref[...]
     polar_total = theta.shape[0]
     for p in range(out_ref.shape[1]):
         for o in range(8):
             for r in range(2):
-                x = x_ref[:, p * 8 + o, r].reshape(theta.shape[1], phi.shape[0])
+                x = x_ref[:, p * 8 + o, r].reshape(theta.shape[1], phi_ref.shape[0])
                 mid = jnp.dot(theta, x, preferred_element_type=jnp.float32)
                 k = o * 2 + r
                 mid_ref[k * polar_total : (k + 1) * polar_total, :] = mid.astype(jnp.bfloat16)
-        raised_ref[...] = jnp.dot(mid_ref[...], phi, preferred_element_type=jnp.float32).reshape(
+        raised_ref[...] = jnp.dot(mid_ref[...], phi_ref[...], preferred_element_type=jnp.float32).reshape(
             raised_ref.shape
         )
 
@@ -90,11 +96,13 @@
 
 
 def translate_kernel(k, at_ref, kind_ref, bound_ref, trans_ref, *refs):
-    first = k == 0
+    first, last = k == 0, k == len(POOL_BLOCKS) - 1
     if first:
         *blocks, out_ref, parents_ref, pool_ref, sem = refs
         copy = pltpu.make_async_copy(blocks[0], parents_ref, sem)
         copy.start()
+    elif last:
+        sum_ref, *blocks, final_ref, pool_ref, out_ref, sems = refs
     else:
         sum_ref, *blocks, out_ref, pool_ref = refs
     start = 0
@@ -108,28 +116,48 @@
         start += block.shape[0]
     pool_ref[start] = jnp.zeros(pool_ref.shape[1:], jnp.float32)
 
+    def entries(g):
+        spots = [g * STEP + j for j in range(STEP)]
+        return tuple(at_ref[i] for i in spots) + tuple(kind_ref[i] for i in spots)
+
     def box(b, carry):
         def group(g, acc):
-            real, imag = acc
+            real, imag, now = acc
+            later = entries(g + 1)
             for j in range(STEP):
-                at, kind = at_ref[g * STEP + j], kind_ref[g * STEP + j]
+                at, kind = now[j], now[STEP + j]
                 sr, si = pool_ref[at, 0], pool_ref[at, 1]
                 tr, ti = trans_ref[kind, 0], trans_ref[kind, 1]
                 real = real + (tr * sr - ti * si)
                 imag = imag + (tr * si + ti * sr)
-            return real, imag
+            return real, imag, later
 
         if first:
             zero = jnp.zeros(out_ref.shape[2:], jnp.float32)
             acc = (zero, zero)
         else:
             acc = (sum_ref[b, 0], sum_ref[b, 1])
-        real, imag = lax.fori_loop(bound_ref[b, 2 * k], bound_ref[b, 2 * k + 1], group, acc)
+        begin, end = bound_ref[b, 2 * k], bound_ref[b, 2 * k + 1]
+        real, imag, _ = lax.fori_loop(begin, end, group, acc + (entries(begin),))
         out_ref[b, 0] = real
         out_ref[b, 1] = imag
         return carry
 
-    lax.fori_loop(0, out_ref.shape[0], box, 0)
+    boxes = out_ref.shape[0]
+    if not last:
+        lax.fori_loop(0, boxes, box, 0)
+    else:
+        parts = sems.shape[0]
+        size = boxes // parts
+        copies = []
+        for i in range(parts):
+            lax.fori_loop(i * size, (i + 1) * size, box, 0)
+            rows = pl.ds(i * size, size)
+            out = pltpu.make_async_copy(out_ref.at[rows], final_ref.at[rows], sems.at[i])
+            out.start()
+            copies.append(out)
+        for out in copies:
+            out.wait()
     if first:
         copy.wait()
 
@@ -142,7 +170,7 @@
 def plan_kernel(place_ref, own_ref, after_ref, far_ref, before_ref, slots_ref, kinds_ref, *outs):
     at_ref, kind_ref, bound_ref = outs
     y, c = place_ref[0], place_ref[1]
-    cores, receivers, cap = own_ref.shape
+    cores, _, cap = own_ref.shape
     local_boxes = slots_ref.shape[0]
     me = y * cores + c
     slots = slots_ref[...]
@@ -153,13 +181,13 @@
     row = jnp.zeros_like(slots)
     tables = (own_ref, after_ref, far_ref, before_ref)
     for k, table in enumerate(tables):
-        side = cores if k == 3 else 0
         for core in range(cores):
+            side = core if k == 0 else int(k == 3)
             for u in range(cap):
-                value = table[core, me, u] + (side + core) * local_boxes
+                value = table[core, me, u] + side * local_boxes
                 row = jnp.where(code == (k * cores + core) * cap + u, value, row)
     entries = slots.shape[1]
-    klass = jnp.where(dy == 0, 0, jnp.where(dy == 2, 2, 1))
+    klass = jnp.where(dy == 0, 0, jnp.where(dy == 2, 3, 1) + dc)
     first = lax.broadcasted_iota(jnp.int32, (entries, entries), 0)
     second = lax.broadcasted_iota(jnp.int32, (entries, entries), 1)
     ahead = (first < second).astype(jnp.float32)
@@ -225,15 +253,25 @@
     parent_boxes = child_boxes // 8
     out_rows = polar_total // samp_count
     pattern = (2, out_rows, azimuth_total)
-    half = parent_boxes // 2
 
     x = children.reshape(samp_count, own_children, 2, rows, child_azimuth)
     x = lax.all_to_all(x, SAMP, split_axis=0, concat_axis=0, tiled=True)
 
     cosine, sine = phase_tables(polar_total, azimuth_total)
-    theta = interp_theta.T
+    theta, phi = pl.pallas_call(
+        prepare_kernel,
+        out_shape=[
+            pltpu.VMEM(interp_theta.shape[::-1], jnp.bfloat16),
+            pltpu.VMEM(interp_phi.shape, jnp.bfloat16),
+        ],
+        in_specs=[VMEM] * 2,
+        out_specs=[VMEM] * 2,
+        compiler_params=pltpu.CompilerParams(vmem_limit_bytes=4 << 20),
+        cost_estimate=pl.CostEstimate(flops=1 << 20, bytes_accessed=1 << 18, transcendentals=0),
+        name="prepare",
+    )(interp_theta, interp_phi)
     tables = slot_tables(send_index)
-    x, *tables = lax.optimization_barrier((x, *tables))
+    x, theta, phi, *tables = lax.optimization_barrier((x, theta, phi, *tables))
     mine = pl.pallas_call(
         aggregate_kernel,
         out_shape=jax.ShapeDtypeStruct((samp_count, own_children // 8) + pattern, jnp.bfloat16),
@@ -246,19 +284,20 @@
         compiler_params=pltpu.CompilerParams(vmem_limit_bytes=12 << 20),
         cost_estimate=pl.CostEstimate(flops=335 << 20, bytes_accessed=4 << 20, transcendentals=0),
         name="aggregate",
-    )(x, theta, interp_phi, cosine, sine)
+    )(x, theta, phi, cosine, sine)
     mine = lax.all_to_all(mine, SAMP, split_axis=0, concat_axis=0, tiled=True)
     at, kind, bound = plan_lists(tables, list_slots, list_kinds)
     mine, at, kind, bound = lax.optimization_barrier((mine, at, kind, bound))
     own = mine.reshape((parent_boxes,) + pattern)
     after = shift(own, "y", -1)
     before = shift(own, "y", 1)
+    far = shift(own, "y", 2)
     other = shift(own, "c", 1)
     source, own = lax.optimization_barrier((translator, own))
     wide = pl.pallas_call(
         widen_kernel,
         out_shape=pltpu.VMEM(translator.shape, jnp.float32),
-        in_specs=[pl.BlockSpec(memory_space=pltpu.HBM)],
+        in_specs=[HBM],
         out_specs=VMEM,
         scratch_shapes=[
             pltpu.VMEM(translator.shape, jnp.bfloat16),
@@ -270,14 +309,17 @@
     )(source)
 
     def translate(k, blocks, so_far):
+        first, last = k == 0, k == len(POOL_BLOCKS) - 1
         shape = (parent_boxes,) + pattern
-        out = [(pltpu.VMEM if k < 2 else jax.ShapeDtypeStruct)(shape, jnp.float32)]
-        specs = [VMEM]
+        out = [(jax.ShapeDtypeStruct if last else pltpu.VMEM)(shape, jnp.float32)]
+        specs = [HBM if last else VMEM]
         scratch = [pltpu.VMEM((POOL_BLOCKS[k] * parent_boxes + 1,) + pattern, jnp.float32)]
-        if k == 0:
+        if first:
             out.append(jax.ShapeDtypeStruct(shape, jnp.bfloat16))
-            specs.append(pl.BlockSpec(memory_space=pltpu.HBM))
+            specs.append(HBM)
             scratch.append(pltpu.SemaphoreType.DMA)
+        if last:
+            scratch += [pltpu.VMEM(shape, jnp.float32), pltpu.SemaphoreType.DMA((4,))]
         return pl.pallas_call(
             functools.partial(translate_kernel, k),
             out_shape=out,
@@ -288,17 +330,17 @@
             cost_estimate=pl.CostEstimate(
                 flops=16 << 20, bytes_accessed=8 << 20, transcendentals=0
             ),
-            name=f"translate_{k}",
         )(at, kind, bound, wide, *so_far, *blocks)
 
     field, parents = translate(0, [own, other], [])
     after, before, field = lax.optimization_barrier((after, before, field))
-    far = [shift(before[:half], "y", 1), shift(after[half:], "y", -1)]
-    near = [after, shift(after, "c", 1), before, shift(before, "c", 1)]
-    (field,) = translate(1, near, [field])
-    *far, field = lax.optimization_barrier((*far, field))
-    across = [shift(v, "c", 1) for v in far]
-    (field,) = translate(2, far + across, [field])
+    across = [shift(after, "c", 1), shift(before, "c", 1)]
+    (field,) = translate(1, [after, before], [field])
+    (field,) = translate(2, across, [field])
+    far, field = lax.optimization_barrier((far, field))
+    across = shift(far, "c", 1)
+    (field,) = translate(3, [far], [field])
+    (field,) = translate(4, [across], [field])
     return parents, field
 
 

time: 68.5 us -> 67.9 us (level)
  Pallas kernels: 24.3 us -> 27.3 us
  waiting for transfers between devices: 10.3 us -> 8.04 us
  starting transfers between devices: 27.9 us -> 26.7 us
    ppermute x13 -> x11, starting transfers between devices: 15.7 us -> 12.2 us  [shift(): return lax.ppermute(x, axis, [(i, (i + step) % size) for i in range(size)])]
    pallas_call x3 -> x5, Pallas kernels: 16 us -> 19 us  [translate(): pl.pallas_call(functools.partial(translate_kernel, k), out_shape=out, in_...]
    all_to_all x1, starting transfers between devices: 4.49 us -> 6.01 us  [local(): mine = lax.all_to_all(mine, SAMP, split_axis=0, concat_axis=0, tiled=True)]
    all_to_all x1, waiting for transfers between devices: 1.98 us -> 0.86 us  [local(): x = lax.all_to_all(x, SAMP, split_axis=0, concat_axis=0, tiled=True)]
    ppermute x13 -> x11, waiting for transfers between devices: 3.06 us -> 2.07 us  [shift(): return lax.ppermute(x, axis, [(i, (i + step) % size) for i in range(size)])]
    all_to_all x1, starting transfers between devices: 7.71 us -> 8.56 us  [local(): x = lax.all_to_all(x, SAMP, split_axis=0, concat_axis=0, tiled=True)]
    unnamed x8 -> x9, local copies, waits for them, and re-layouts: 2.36 us -> 2.25 us
  transfers between devices with their start and end apart: 15 -> 13, of which waited for: 7 -> 5; matrix products, arithmetic and copies ran while one was open for 6% -> 4% of each run, Pallas kernels for 24% -> 31%
where the time goes in v3:
time: 67.9 us; the launch traced here: 67.4 us
  Pallas kernels  27.3 us (40%)
  starting transfers between devices  26.7 us (39%)
  waiting for transfers between devices  8.04 us (12%)
  other arithmetic  2.26 us (3%)
  local copies, waits for them, and re-layouts  2.25 us (3%)
  between operations  0.82 us (1%)
    pallas_call x5, Pallas kernels, translate(): pl.pallas_call(functools.partial(translate_kernel, k), out_shape=out, in_...  19 us
    ppermute x11, starting transfers between devices, shift(): return lax.ppermute(x, axis, [(i, (i + step) % size) for i in range(size)])  12.2 us
    all_to_all x1, starting transfers between devices, local(): x = lax.all_to_all(x, SAMP, split_axis=0, concat_axis=0, tiled=True)  8.56 us
    all_to_all x1, starting transfers between devices, local(): mine = lax.all_to_all(mine, SAMP, split_axis=0, concat_axis=0, tiled=True)  6.01 us
    all_to_all x1, waiting for transfers between devices, local(): mine = lax.all_to_all(mine, SAMP, split_axis=0, concat_axis=0, tiled=True)  5.11 us
    pallas_call x1, Pallas kernels, local(): pl.pallas_call(widen_kernel, out_shape=pltpu.VMEM(translator.shape, jnp.f...  3.09 us
    pallas_call x1, Pallas kernels, local(): pl.pallas_call(aggregate_kernel, out_shape=jax.ShapeDtypeStruct((samp_cou...  3.06 us
    unnamed x9, local copies, waits for them, and re-layouts  2.25 us
  transfers between devices with their start and end apart: 13, of which 5 were waited for; matrix products, arithmetic and copies ran while one was open for 4% of the time, Pallas kernels for 31%

profile of v3, /device:TPU:1, one launch (start us, length us, event | category | flops | bytes accessed | tf_op | source)
XLA Modules:
  0.0 67.4 jit_solution(1016366131886396349)
XLA Ops:
  0.6 0.0 copy-start.2
  0.6 0.0 copy-start.3
  0.6 8.6 %all-to-all-start = ((bf16[16,16,2,4,128]{4,3,2,1,0:T(4,128)(2,1)}), bf16[16,16,2,4,128]{4,3,2,1,0:T(4,128)(2,1)S(1)}, u32[]{:S(2)}, u32[]{:S(2)}) async-start(bf16[16,16,2,4,128]{4,3,2,1,0:T(4,128)(2,1)} %bitcast.21), calls=%async_computation | async-start | bytes 1048576 | tf_op jit(solution)/shard_map/all_to_all | solution.py:258
  9.2 1.0 %collective-permute-start = (s32[1,8,16]{2,1,0:T(8,128)}, s32[1,8,16]{2,1,0:T(8,128)S(1)}, u32[]{:S(2)}, u32[]{:S(2)}) collective-permute-start(s32[1,8,16]{2,1,0:T(8,128)} %param.11), channel_id=1, source_target_pairs={{0,16},{16,0},{1,17},{17,1},{2,18},{18,2},{3,19},{19,3},{4,20},{20... | collective-permute-start | bytes 1544 | tf_op jit(solution)/shard_map/ppermute | solution.py:167
  10.3 0.7 %constant_dynamic-update-slice_fusion.1 = s32[2,8,16]{2,1,0:T(8,128)S(1)} fusion(s32[1,8,16]{2,1,0:T(8,128)} %param.11), kind=kLoop, calls=%fused_computation.6 | loop fusion | bytes 4608
  11.0 0.1 broadcast_multiply_fusion.1
  11.2 0.1 collective-permute-done
  11.3 2.7 %collective-permute-start.1 = (s32[2,8,16]{2,1,0:T(8,128)S(1)}, s32[2,8,16]{2,1,0:T(8,128)S(1)}, u32[]{:S(2)}, u32[]{:S(2)}) collective-permute-start(s32[2,8,16]{2,1,0:T(8,128)S(1)} %constant_dynamic-update-slice_fusion.own_ref), channel_id=1, source_target_pairs={{0,96},{32,0},{64,32},{96,64},{1,97},{33,1},{65,33},{97,65},{2,98}... | collective-permute-start | bytes 3080 | tf_op jit(solution)/shard_map/ppermute | solution.py:167
  14.0 0.3 collective-permute-start.2
  14.4 0.7 %collective-permute-start.3 = (s32[2,8,16]{2,1,0:T(8,128)S(1)}, s32[2,8,16]{2,1,0:T(8,128)S(1)}, u32[]{:S(2)}, u32[]{:S(2)}) collective-permute-start(s32[2,8,16]{2,1,0:T(8,128)S(1)} %constant_dynamic-update-slice_fusion.own_ref), channel_id=1, source_target_pairs={{0,32},{32,64},{64,96},{96,0},{1,33},{33,65},{65,97},{97,1},{2,34}... | collective-permute-start | bytes 3080 | tf_op jit(solution)/shard_map/ppermute | solution.py:167
  15.1 2.0 %fusion = (f32[4,128,256]{2,1,0:T(8,128)S(1)}, f32[4,128,256]{2,1,0:T(8,128)S(1)}) fusion(f32[128]{0:T(128)S(1)} %fusion.4, f32[128,256]{1,0:T(8,128)S(1)} %get-tuple-element.55, f32[4]{0:T(128)S(1)} %get-tuple-element.58, f32[128,256]{1,0:T(8,128)S(1)} %get-tuple-element.54, f32[4]{0:T(128)S(1)} %get-tuple-element.59), kind=kLoop, calls=%fused_computation.1 | loop fusion | flops 655360 | bytes 1311264 | tf_op jit(solution)/shard_map/sin | solution.py:37
  17.0 0.0 copy-start
  17.0 0.8 %copy-done = bf16[128,256]{1,0:T(8,128)(2,1)S(1)} copy-done((bf16[128,256]{1,0:T(8,128)(2,1)S(1)}, bf16[128,256]{1,0:T(8,128)(2,1)}, u32[]{:S(2)}) %copy-start) | copy-done | bytes 65560
  17.9 0.0 copy-start.1
  17.9 0.7 %copy-done.1 = bf16[64,128]{1,0:T(8,128)(2,1)S(1)} copy-done((bf16[64,128]{1,0:T(8,128)(2,1)S(1)}, bf16[64,128]{1,0:T(8,128)(2,1)}, u32[]{:S(2)}) %copy-start.1) | copy-done | bytes 16408
  18.6 0.1 prepare.1
  18.7 0.0 collective-permute-done.1.after_ref
  18.7 0.0 collective-permute-done.2.far_ref
  18.7 0.0 collective-permute-done.3.before_ref
  18.7 0.9 %all-to-all-done.x_ref = bf16[16,16,2,4,128]{4,3,2,1,0:T(4,128)(2,1)S(1)} async-done(((bf16[16,16,2,4,128]{4,3,2,1,0:T(4,128)(2,1)}), bf16[16,16,2,4,128]{4,3,2,1,0:T(4,128)(2,1)S(1)}, u32[]{:S(2)}, u32[]{:S(2)}) %all-to-all-start) | async-done | bytes 524320 | tf_op jit(solution)/shard_map/all_to_all | solution.py:258
  19.6 3.1 %aggregate.1 = bf16[16,2,2,8,256]{4,3,2,1,0:T(8,128)(2,1)} custom-call(bf16[16,16,2,4,128]{4,3,2,1,0:T(4,128)(2,1)S(1)} %all-to-all-done.x_ref, bf16[128,64]{1,0:T(8,128)(2,1)S(1)} %get-tuple-element.30.theta_ref, bf16[128,256]{1,0:T(8,128)(2,1)S(1)} %get-tuple-element.31.phi_ref, f32[4,128,256]{2,1,0:T(8,128)S(1)} %get-tuple-element.53.cos_ref, ...), custom_call_target="tpu_custom_call" | custom-call | flops 351272960 | bytes 4194304 | tf_op jit(solution)/shard_map/aggregate/pallas_call | solution.py:275
  22.6 6.0 %all-to-all-start.1 = ((bf16[16,2,2,8,256]{4,3,2,1,0:T(8,128)(2,1)}), bf16[16,2,2,8,256]{4,3,2,1,0:T(8,128)(2,1)S(1)}, u32[]{:S(2)}, u32[]{:S(2)}) async-start(bf16[16,2,2,8,256]{4,3,2,1,0:T(8,128)(2,1)} %aggregate.1), calls=%async_computation.1 | async-start | bytes 524288 | tf_op jit(solution)/shard_map/all_to_all | solution.py:288
  28.7 0.1 pad_add_fusion.place_ref
  28.7 0.0 copy-done.2
  28.7 0.0 copy-done.3
  28.7 2.1 %plan.1 = (s32[32,128]{1,0:T(8,128)S(1)}, s32[32,128]{1,0:T(8,128)S(1)}, s32[32,128]{1,0:T(8,128)S(1)}) custom-call(s32[2]{0:T(128)S(1)} %pad_add_fusion.place_ref, s32[2,8,16]{2,1,0:T(8,128)S(1)} %constant_dynamic-update-slice_fusion.own_ref, s32[2,8,16]{2,1,0:T(8,128)S(1)} %collective-permute-done.1.after_ref, ...), custom_call_target="tpu_custom_call" | custom-call | flops 1048576 | bytes 1048576 | tf_op jit(solution)/shard_map/plan/pallas_call | solution.py:235
  30.9 5.1 %all-to-all-done.1 = bf16[16,2,2,8,256]{4,3,2,1,0:T(8,128)(2,1)S(1)} async-done(((bf16[16,2,2,8,256]{4,3,2,1,0:T(8,128)(2,1)}), bf16[16,2,2,8,256]{4,3,2,1,0:T(8,128)(2,1)S(1)}, u32[]{:S(2)}, u32[]{:S(2)}) %all-to-all-start.1) | async-done | bytes 262176 | tf_op jit(solution)/shard_map/all_to_all | solution.py:288
  36.0 2.8 %collective-permute-start.4 = (bf16[32,2,8,256]{3,2,1,0:T(8,128)(2,1)S(1)}, bf16[32,2,8,256]{3,2,1,0:T(8,128)(2,1)S(1)}, u32[]{:S(2)}, u32[]{:S(2)}) collective-permute-start(bf16[32,2,8,256]{3,2,1,0:T(8,128)(2,1)S(1)} %bitcast.6), channel_id=1, source_target_pairs={{0,16},{16,0},{1,17},{17,1},{2,18},{18,2},{3,19},{19,3},{4,20},{20... | collective-permute-start | bytes 786440 | tf_op jit(solution)/shard_map/ppermute | solution.py:167
  38.8 1.8 %collective-permute-start.6 = (bf16[32,2,8,256]{3,2,1,0:T(8,128)(2,1)S(1)}, bf16[32,2,8,256]{3,2,1,0:T(8,128)(2,1)S(1)}, u32[]{:S(2)}, u32[]{:S(2)}) collective-permute-start(bf16[32,2,8,256]{3,2,1,0:T(8,128)(2,1)S(1)} %bitcast.7), channel_id=1, source_target_pairs={{0,96},{32,0},{64,32},{96,64},{1,97},{33,1},{65,33},{97,65},{2,98}... | collective-permute-start | bytes 786440 | tf_op jit(solution)/shard_map/ppermute | solution.py:167
  40.6 0.0 collective-permute-start.7
  40.6 3.1 %widen.1.trans_ref = f32[316,2,8,256]{3,2,1,0:T(8,128)S(1)} custom-call(bf16[316,2,8,256]{3,2,1,0:T(8,128)(2,1)} %x_ref), custom_call_target="tpu_custom_call" | custom-call | flops 4194304 | bytes 8388608 | tf_op jit(solution)/shard_map/widen/pallas_call | solution.py:297
  43.7 0.0 collective-permute-done.4.refs_1_
  43.7 4.1 %shard_map.86 = (f32[32,2,8,256]{3,2,1,0:T(8,128)S(1)}, bf16[32,2,8,256]{3,2,1,0:T(8,128)(2,1)}) custom-call(s32[4096]{0:T(1024)S(1)} %bitcast.11, s32[4096]{0:T(1024)S(1)} %bitcast.16, s32[32,128]{1,0:T(8,128)S(1)} %get-tuple-element.41.bound_ref, f32[316,2,8,256]{3,2,1,0:T(8,128)S(1)} %widen.1.trans_ref, bf16[32,2,8,256]{3,2,1,0:T(8,128)(2,1)S(1)} %bitcast.9, ...), custom_call_target="tpu_custom_call" | custom-call | flops 16777216 | bytes 8388608 | tf_op jit(solution)/shard_map/pallas_call | solution.py:323
  47.8 0.0 collective-permute-done.6.refs_1_
  47.8 1.6 %collective-permute-done.7.refs_2_ = bf16[32,2,8,256]{3,2,1,0:T(8,128)(2,1)S(1)} collective-permute-done((bf16[32,2,8,256]{3,2,1,0:T(8,128)(2,1)S(1)}, bf16[32,2,8,256]{3,2,1,0:T(8,128)(2,1)S(1)}, u32[]{:S(2)}, u32[]{:S(2)}) %collective-permute-start.7) | collective-permute-done | bytes 262176 | tf_op jit(solution)/shard_map/ppermute | solution.py:167
  49.4 1.1 %collective-permute-start.8 = (bf16[32,2,8,256]{3,2,1,0:T(8,128)(2,1)S(1)}, bf16[32,2,8,256]{3,2,1,0:T(8,128)(2,1)S(1)}, u32[]{:S(2)}, u32[]{:S(2)}) collective-permute-start(bf16[32,2,8,256]{3,2,1,0:T(8,128)(2,1)S(1)} %collective-permute-done.6.refs_1_), channel_id=1, source_target_pairs={{0,16},{16,0},{1,17},{17,1},{2,18},{18,2},{3,19},{19,3},{4,20},{20... | collective-permute-start | bytes 786440 | tf_op jit(solution)/shard_map/ppermute | solution.py:167
  50.6 0.0 collective-permute-start.9
  50.6 0.2 collective-permute-start.5
  50.8 4.2 %shard_map.87.refs_0_ = f32[32,2,8,256]{3,2,1,0:T(8,128)S(1)} custom-call(s32[4096]{0:T(1024)S(1)} %bitcast.12, s32[4096]{0:T(1024)S(1)} %bitcast.17, s32[32,128]{1,0:T(8,128)S(1)} %get-tuple-element.41.bound_ref, f32[316,2,8,256]{3,2,1,0:T(8,128)S(1)} %widen.1.trans_ref, f32[32,2,8,256]{3,2,1,0:T(8,128)S(1)} %get-tuple-element.47.refs_0_, ...), custom_call_target="tpu_custom_call" | custom-call | flops 16777216 | bytes 8388608 | tf_op jit(solution)/shard_map/pallas_call | solution.py:323
  55.0 0.0 collective-permute-done.8.refs_1_
  55.0 0.0 collective-permute-done.9.refs_2_
  55.0 4.1 %shard_map.88.refs_0_ = f32[32,2,8,256]{3,2,1,0:T(8,128)S(1)} custom-call(s32[4096]{0:T(1024)S(1)} %bitcast.13, s32[4096]{0:T(1024)S(1)} %bitcast.18, s32[32,128]{1,0:T(8,128)S(1)} %get-tuple-element.41.bound_ref, f32[316,2,8,256]{3,2,1,0:T(8,128)S(1)} %widen.1.trans_ref, f32[32,2,8,256]{3,2,1,0:T(8,128)S(1)} %shard_map.87.refs_0_, ...), custom_call_target="tpu_custom_call" | custom-call | flops 16777216 | bytes 8388608 | tf_op jit(solution)/shard_map/pallas_call | solution.py:323
  59.1 0.4 collective-permute-done.5.refs_1_
  59.4 1.4 %collective-permute-start.10 = (bf16[32,2,8,256]{3,2,1,0:T(8,128)(2,1)S(1)}, bf16[32,2,8,256]{3,2,1,0:T(8,128)(2,1)S(1)}, u32[]{:S(2)}, u32[]{:S(2)}) collective-permute-start(bf16[32,2,8,256]{3,2,1,0:T(8,128)(2,1)S(1)} %collective-permute-done.5.refs_1_), channel_id=1, source_target_pairs={{0,16},{16,0},{1,17},{17,1},{2,18},{18,2},{3,19},{19,3},{4,20},{20... | collective-permute-start | bytes 786440 | tf_op jit(solution)/shard_map/ppermute | solution.py:167
  60.8 3.0 %shard_map.89.refs_0_ = f32[32,2,8,256]{3,2,1,0:T(8,128)S(1)} custom-call(s32[4096]{0:T(1024)S(1)} %bitcast.14, s32[4096]{0:T(1024)S(1)} %bitcast.19, s32[32,128]{1,0:T(8,128)S(1)} %get-tuple-element.41.bound_ref, f32[316,2,8,256]{3,2,1,0:T(8,128)S(1)} %widen.1.trans_ref, f32[32,2,8,256]{3,2,1,0:T(8,128)S(1)} %shard_map.88.refs_0_, ...), custom_call_target="tpu_custom_call" | custom-call | flops 16777216 | bytes 8388608 | tf_op jit(solution)/shard_map/pallas_call | solution.py:323
  63.8 0.0 collective-permute-done.10.refs_1_
  63.8 3.6 %shard_map.90 = f32[32,2,8,256]{3,2,1,0:T(8,128)} custom-call(s32[4096]{0:T(1024)S(1)} %bitcast.15, s32[4096]{0:T(1024)S(1)} %bitcast.20, s32[32,128]{1,0:T(8,128)S(1)} %get-tuple-element.41.bound_ref, f32[316,2,8,256]{3,2,1,0:T(8,128)S(1)} %widen.1.trans_ref, f32[32,2,8,256]{3,2,1,0:T(8,128)S(1)} %shard_map.89.refs_0_, ...), custom_call_target="tpu_custom_call" | custom-call | flops 16777216 | bytes 8388608 | tf_op jit(solution)/shard_map/pallas_call | solution.py:323
  (5 shorter events, 0.1 us)
Async XLA Ops:
  0.6 28.1 %copy-start.2 = (s32[32,64]{1,0:T(8,128)S(1)}, s32[32,64]{1,0:T(8,128)}, u32[]{:S(2)}) copy-start(s32[32,64]{1,0:T(8,128)} %slots_ref.1) | copy-start | bytes 24580
  0.6 28.1 %copy-start.3 = (s32[32,64]{1,0:T(8,128)S(1)}, s32[32,64]{1,0:T(8,128)}, u32[]{:S(2)}) copy-start(s32[32,64]{1,0:T(8,128)} %kinds_ref.1) | copy-start | bytes 24580
  0.6 18.9 %all-to-all-start = ((bf16[16,16,2,4,128]{4,3,2,1,0:T(4,128)(2,1)}), bf16[16,16,2,4,128]{4,3,2,1,0:T(4,128)(2,1)S(1)}, u32[]{:S(2)}, u32[]{:S(2)}) async-start(bf16[16,16,2,4,128]{4,3,2,1,0:T(4,128)(2,1)} %bitcast.21), calls=%async_computation | async-start | bytes 1048576 | tf_op jit(solution)/shard_map/all_to_all | solution.py:258
  9.2 2.1 %collective-permute-start = (s32[1,8,16]{2,1,0:T(8,128)}, s32[1,8,16]{2,1,0:T(8,128)S(1)}, u32[]{:S(2)}, u32[]{:S(2)}) collective-permute-start(s32[1,8,16]{2,1,0:T(8,128)} %param.11), channel_id=1, source_target_pairs={{0,16},{16,0},{1,17},{17,1},{2,18},{18,2},{3,19},{19,3},{4,20},{20... | collective-permute-start | bytes 1544 | tf_op jit(solution)/shard_map/ppermute | solution.py:167
  11.3 7.4 %collective-permute-start.1 = (s32[2,8,16]{2,1,0:T(8,128)S(1)}, s32[2,8,16]{2,1,0:T(8,128)S(1)}, u32[]{:S(2)}, u32[]{:S(2)}) collective-permute-start(s32[2,8,16]{2,1,0:T(8,128)S(1)} %constant_dynamic-update-slice_fusion.own_ref), channel_id=1, source_target_pairs={{0,96},{32,0},{64,32},{96,64},{1,97},{33,1},{65,33},{97,65},{2,98}... | collective-permute-start | bytes 3080 | tf_op jit(solution)/shard_map/ppermute | solution.py:167
  14.0 4.7 %collective-permute-start.2 = (s32[2,8,16]{2,1,0:T(8,128)S(1)}, s32[2,8,16]{2,1,0:T(8,128)S(1)}, u32[]{:S(2)}, u32[]{:S(2)}) collective-permute-start(s32[2,8,16]{2,1,0:T(8,128)S(1)} %constant_dynamic-update-slice_fusion.own_ref), channel_id=1, source_target_pairs={{0,64},{32,96},{64,0},{96,32},{1,65},{33,97},{65,1},{97,33},{2,66}... | collective-permute-start | bytes 3080 | tf_op jit(solution)/shard_map/ppermute | solution.py:167
  14.4 4.3 %collective-permute-start.3 = (s32[2,8,16]{2,1,0:T(8,128)S(1)}, s32[2,8,16]{2,1,0:T(8,128)S(1)}, u32[]{:S(2)}, u32[]{:S(2)}) collective-permute-start(s32[2,8,16]{2,1,0:T(8,128)S(1)} %constant_dynamic-update-slice_fusion.own_ref), channel_id=1, source_target_pairs={{0,32},{32,64},{64,96},{96,0},{1,33},{33,65},{65,97},{97,1},{2,34}... | collective-permute-start | bytes 3080 | tf_op jit(solution)/shard_map/ppermute | solution.py:167
  17.0 0.8 %copy-start = (bf16[128,256]{1,0:T(8,128)(2,1)S(1)}, bf16[128,256]{1,0:T(8,128)(2,1)}, u32[]{:S(2)}) copy-start(bf16[128,256]{1,0:T(8,128)(2,1)} %phi_ref.1) | copy-start | bytes 196612
  17.9 0.7 %copy-start.1 = (bf16[64,128]{1,0:T(8,128)(2,1)S(1)}, bf16[64,128]{1,0:T(8,128)(2,1)}, u32[]{:S(2)}) copy-start(bf16[64,128]{1,0:T(8,128)(2,1)} %theta_ref.1) | copy-start | bytes 49156
  22.6 13.3 %all-to-all-start.1 = ((bf16[16,2,2,8,256]{4,3,2,1,0:T(8,128)(2,1)}), bf16[16,2,2,8,256]{4,3,2,1,0:T(8,128)(2,1)S(1)}, u32[]{:S(2)}, u32[]{:S(2)}) async-start(bf16[16,2,2,8,256]{4,3,2,1,0:T(8,128)(2,1)} %aggregate.1), calls=%async_computation.1 | async-start | bytes 524288 | tf_op jit(solution)/shard_map/all_to_all | solution.py:288
  36.0 7.7 %collective-permute-start.4 = (bf16[32,2,8,256]{3,2,1,0:T(8,128)(2,1)S(1)}, bf16[32,2,8,256]{3,2,1,0:T(8,128)(2,1)S(1)}, u32[]{:S(2)}, u32[]{:S(2)}) collective-permute-start(bf16[32,2,8,256]{3,2,1,0:T(8,128)(2,1)S(1)} %bitcast.6), channel_id=1, source_target_pairs={{0,16},{16,0},{1,17},{17,1},{2,18},{18,2},{3,19},{19,3},{4,20},{20... | collective-permute-start | bytes 786440 | tf_op jit(solution)/shard_map/ppermute | solution.py:167
  38.8 9.0 %collective-permute-start.6 = (bf16[32,2,8,256]{3,2,1,0:T(8,128)(2,1)S(1)}, bf16[32,2,8,256]{3,2,1,0:T(8,128)(2,1)S(1)}, u32[]{:S(2)}, u32[]{:S(2)}) collective-permute-start(bf16[32,2,8,256]{3,2,1,0:T(8,128)(2,1)S(1)} %bitcast.7), channel_id=1, source_target_pairs={{0,96},{32,0},{64,32},{96,64},{1,97},{33,1},{65,33},{97,65},{2,98}... | collective-permute-start | bytes 786440 | tf_op jit(solution)/shard_map/ppermute | solution.py:167
  40.6 8.8 %collective-permute-start.7 = (bf16[32,2,8,256]{3,2,1,0:T(8,128)(2,1)S(1)}, bf16[32,2,8,256]{3,2,1,0:T(8,128)(2,1)S(1)}, u32[]{:S(2)}, u32[]{:S(2)}) collective-permute-start(bf16[32,2,8,256]{3,2,1,0:T(8,128)(2,1)S(1)} %bitcast.8), channel_id=1, source_target_pairs={{0,32},{32,64},{64,96},{96,0},{1,33},{33,65},{65,97},{97,1},{2,34}... | collective-permute-start | bytes 786440 | tf_op jit(solution)/shard_map/ppermute | solution.py:167
  49.4 5.5 %collective-permute-start.8 = (bf16[32,2,8,256]{3,2,1,0:T(8,128)(2,1)S(1)}, bf16[32,2,8,256]{3,2,1,0:T(8,128)(2,1)S(1)}, u32[]{:S(2)}, u32[]{:S(2)}) collective-permute-start(bf16[32,2,8,256]{3,2,1,0:T(8,128)(2,1)S(1)} %collective-permute-done.6.refs_1_), channel_id=1, source_target_pairs={{0,16},{16,0},{1,17},{17,1},{2,18},{18,2},{3,19},{19,3},{4,20},{20... | collective-permute-start | bytes 786440 | tf_op jit(solution)/shard_map/ppermute | solution.py:167
  50.6 4.4 %collective-permute-start.9 = (bf16[32,2,8,256]{3,2,1,0:T(8,128)(2,1)S(1)}, bf16[32,2,8,256]{3,2,1,0:T(8,128)(2,1)S(1)}, u32[]{:S(2)}, u32[]{:S(2)}) collective-permute-start(bf16[32,2,8,256]{3,2,1,0:T(8,128)(2,1)S(1)} %collective-permute-done.7.refs_2_), channel_id=1, source_target_pairs={{0,16},{16,0},{1,17},{17,1},{2,18},{18,2},{3,19},{19,3},{4,20},{20... | collective-permute-start | bytes 786440 | tf_op jit(solution)/shard_map/ppermute | solution.py:167
  50.6 8.9 %collective-permute-start.5 = (bf16[32,2,8,256]{3,2,1,0:T(8,128)(2,1)S(1)}, bf16[32,2,8,256]{3,2,1,0:T(8,128)(2,1)S(1)}, u32[]{:S(2)}, u32[]{:S(2)}) collective-permute-start(bf16[32,2,8,256]{3,2,1,0:T(8,128)(2,1)S(1)} %bitcast.10), channel_id=1, source_target_pairs={{0,64},{32,96},{64,0},{96,32},{1,65},{33,97},{65,1},{97,33},{2,66}... | collective-permute-start | bytes 786440 | tf_op jit(solution)/shard_map/ppermute | solution.py:167
  59.4 4.4 %collective-permute-start.10 = (bf16[32,2,8,256]{3,2,1,0:T(8,128)(2,1)S(1)}, bf16[32,2,8,256]{3,2,1,0:T(8,128)(2,1)S(1)}, u32[]{:S(2)}, u32[]{:S(2)}) collective-permute-start(bf16[32,2,8,256]{3,2,1,0:T(8,128)(2,1)S(1)} %collective-permute-done.5.refs_1_), channel_id=1, source_target_pairs={{0,16},{16,0},{1,17},{17,1},{2,18},{18,2},{3,19},{19,3},{4,20},{20... | collective-permute-start | bytes 786440 | tf_op jit(solution)/shard_map/ppermute | solution.py:167

commit v4 on v3

v4 whole, which is shorter than its diff:
```python
import math

import jax
import jax.numpy as jnp
from jax import lax
from jax.experimental import pallas as pl
from jax.experimental.pallas import tpu as pltpu
from jax.sharding import Mesh, PartitionSpec as P


KAPPA_H = 12.0
SAMP = ("x", "z")
BOX = ("y", "c")
WIDTH = 128
EARLY = 40
VMEM = pl.BlockSpec(memory_space=pltpu.VMEM)
SMEM = pl.BlockSpec(memory_space=pltpu.SMEM)
HBM = pl.BlockSpec(memory_space=pltpu.HBM)


def phase_tables(polar_total, azimuth_total):
    polar = (jnp.arange(polar_total, dtype=jnp.int32).astype(jnp.float32) + 0.5) * (
        math.pi / polar_total
    )
    azimuth = jnp.arange(azimuth_total, dtype=jnp.int32).astype(jnp.float32) * (
        2.0 * math.pi / azimuth_total
    )
    octant = jnp.arange(4, dtype=jnp.int32)
    sign_x = ((octant & 1) * 2 - 1).astype(jnp.float32)[:, None, None]
    sign_y = ((octant >> 1 & 1) * 2 - 1).astype(jnp.float32)[:, None, None]
    along_x = jnp.sin(polar)[:, None] * jnp.cos(azimuth)[None, :]
    along_y = jnp.sin(polar)[:, None] * jnp.sin(azimuth)[None, :]
    along_z = jnp.cos(polar)[:, None] + jnp.zeros((1, azimuth_total), jnp.float32)
    phase = KAPPA_H * (sign_x * along_x + sign_y * along_y - along_z)
    return jnp.cos(phase), jnp.sin(phase)


def prepare_kernel(theta_ref, phi_ref, turned_ref, copy_ref):
    turned_ref[...] = jnp.transpose(theta_ref[...].astype(jnp.float32)).astype(jnp.bfloat16)
    copy_ref[...] = phi_ref[...]


def aggregate_kernel(x_ref, theta_ref, phi_ref, cos_ref, sin_ref, out_ref, mid_ref, raised_ref):
    theta = theta_ref[...]
    polar_total = theta.shape[0]
    for p in range(out_ref.shape[1]):
        for o in range(8):
            for r in range(2):
                x = x_ref[:, p * 8 + o, r].reshape(theta.shape[1], phi_ref.shape[0])
                mid = jnp.dot(theta, x, preferred_element_type=jnp.float32)
                k = o * 2 + r
                mid_ref[k * polar_total : (k + 1) * polar_total, :] = mid.astype(jnp.bfloat16)
        raised_ref[...] = jnp.dot(mid_ref[...], phi_ref[...], preferred_element_type=jnp.float32).reshape(
            raised_ref.shape
        )

        def slab(s, carry):
            rows = pl.ds(pl.multiple_of(s * 8, 8), 8)
            real = imag = None
            for o in range(4):
                c = cos_ref[o, rows, :]
                d = sin_ref[o, rows, :]
                ar, ai = raised_ref[2 * o, rows, :], raised_ref[2 * o + 1, rows, :]
                br, bi = raised_ref[14 - 2 * o, rows, :], raised_ref[15 - 2 * o, rows, :]
                tr = c * (ar + br) - d * (ai - bi)
                ti = d * (ar - br) + c * (ai + bi)
                real = tr if real is None else real + tr
                imag = ti if imag is None else imag + ti
            out_ref[s, p, 0] = real.astype(jnp.bfloat16)
            out_ref[s, p, 1] = imag.astype(jnp.bfloat16)
            return carry

        lax.fori_loop(0, out_ref.shape[0], slab, 0)


def widen_kernel(x_ref, out_ref, buffer, sems):
    parts = sems.shape[0]
    size = x_ref.shape[0] // parts

    def copy(i):
        at = pl.ds(i * size, size)
        return pltpu.make_async_copy(x_ref.at[at], buffer.at[at], sems.at[i])

    for i in range(parts):
        copy(i).start()
    for i in range(parts):
        copy(i).wait()

        def widen(k, carry):
            out_ref[k] = buffer[k].astype(jnp.float32)
            return carry

        lax.fori_loop(i * size, (i + 1) * size, widen, 0)


def widen_rows(block, pool_ref, start):
    def widen(i, carry):
        pool_ref[start + i] = block[i].astype(jnp.float32)
        return carry

    lax.fori_loop(0, block.shape[0], widen, 0, unroll=4)


def pool_kernel(own_ref, other_ref, pool_ref, parents_ref, sem):
    copy = pltpu.make_async_copy(own_ref, parents_ref, sem)
    copy.start()
    boxes = own_ref.shape[0]
    widen_rows(own_ref, pool_ref, 0)
    widen_rows(other_ref, pool_ref, boxes)
    pool_ref[pool_ref.shape[0] - 1] = jnp.zeros(pool_ref.shape[1:], jnp.float32)
    copy.wait()


def add_entry(list_ref, trans_ref, pool_ref, b, j, real, imag):
    value = list_ref[b, j]
    at, kind = lax.shift_right_logical(value, 9), value & 511
    sr, si = pool_ref[at, 0], pool_ref[at, 1]
    tr, ti = trans_ref[kind, 0], trans_ref[kind, 1]
    return real + (tr * sr - ti * si), imag + (tr * si + ti * sr)


def early_kernel(lists, trans_ref, *refs):
    *blocks, _, out_ref, pool_ref, list_ref, sem = refs
    copy = pltpu.make_async_copy(lists, list_ref, sem)
    copy.start()
    boxes = out_ref.shape[0]
    for i, block in enumerate(blocks):
        widen_rows(block, pool_ref, (2 + i) * boxes)
    copy.wait()

    def box(b, carry):
        real = imag = jnp.zeros(out_ref.shape[2:], jnp.float32)
        for j in range(EARLY):
            real, imag = add_entry(list_ref, trans_ref, pool_ref, b, 64 + j, real, imag)
        out_ref[b, 0] = real
        out_ref[b, 1] = imag
        return carry

    lax.fori_loop(0, boxes, box, 0)


def late_kernel(lists, trans_ref, sum_ref, *refs):
    *blocks, _, final_ref, pool_ref, out_ref, list_ref, sem, sems = refs
    copy = pltpu.make_async_copy(lists, list_ref, sem)
    copy.start()
    boxes = out_ref.shape[0]
    for i, block in enumerate(blocks):
        widen_rows(block, pool_ref, (6 + i) * boxes)
    copy.wait()

    def box(b, carry):
        def more(j, acc):
            return add_entry(list_ref, trans_ref, pool_ref, b, j, *acc)

        acc = (sum_ref[b, 0], sum_ref[b, 1])
        real, imag = lax.fori_loop(list_ref[b, WIDTH - 1], EARLY, more, acc)
        for j in range(EARLY, 64):
            real, imag = add_entry(list_ref, trans_ref, pool_ref, b, j, real, imag)
        out_ref[b, 0] = real
        out_ref[b, 1] = imag
        return carry

    parts = sems.shape[0]
    size = boxes // parts
    copies = []
    for i in range(parts):
        lax.fori_loop(i * size, (i + 1) * size, box, 0)
        rows = pl.ds(i * size, size)
        out = pltpu.make_async_copy(out_ref.at[rows], final_ref.at[rows], sems.at[i])
        out.start()
        copies.append(out)
    for out in copies:
        out.wait()


def shift(x, axis, step):
    size = lax.axis_size(axis)
    return lax.ppermute(x, axis, [(i, (i + step) % size) for i in range(size)])


def plan_kernel(place_ref, own_ref, after_ref, far_ref, before_ref, slots_ref, kinds_ref, out_ref):
    y, c = place_ref[0], place_ref[1]
    cores, _, cap = own_ref.shape
    boxes, entries = slots_ref.shape
    me = y * cores + c
    slots = slots_ref[...]
    sender = lax.shift_right_logical(slots, 4)
    dy = (lax.shift_right_logical(sender, 1) - y) & 3
    dc = (sender & 1) ^ c
    code = (dy * cores + dc) * cap + (slots & (cap - 1))
    row = jnp.zeros_like(slots)
    for k, (table, block) in enumerate(
        ((own_ref, 0), (after_ref, 2), (far_ref, 6), (before_ref, 4))
    ):
        for core in range(cores):
            for u in range(cap):
                value = table[core, me, u] + (block + core) * boxes
                row = jnp.where(code == (k * cores + core) * cap + u, value, row)
    near = dy != 2
    first = lax.broadcasted_iota(jnp.int32, (entries, entries), 0)
    second = lax.broadcasted_iota(jnp.int32, (entries, entries), 1)
    ahead = (first < second).astype(jnp.float32)
    inside = jnp.dot(near.astype(jnp.float32), ahead, preferred_element_type=jnp.float32)
    inside = inside.astype(jnp.int32)
    own_spot = lax.broadcasted_iota(jnp.int32, slots.shape, 1)
    count = jnp.sum(near.astype(jnp.int32), axis=1, keepdims=True)
    spot = jnp.where(near, inside, count + own_spot - inside)
    value = jnp.transpose((row * 512 + kinds_ref[...]).astype(jnp.float32)).astype(jnp.int32)
    spot = jnp.transpose(spot.astype(jnp.float32)).astype(jnp.int32)
    lane = lax.broadcasted_iota(jnp.int32, (entries, WIDTH), 1) & (entries - 1)
    lines = []
    for b in range(boxes):
        got = jnp.where(spot[:, b : b + 1] == lane, value[:, b : b + 1], 0)
        lines.append(jnp.sum(got, axis=0, keepdims=True))
    packed = jnp.concatenate(lines, axis=0)
    lane = lax.broadcasted_iota(jnp.int32, (boxes, WIDTH), 1)
    packed = jnp.where(lane >= entries + count, 8 * boxes * 512, packed)
    out_ref[...] = jnp.where(lane == WIDTH - 1, count, packed)


def slot_tables(send_index):
    own = jnp.concatenate([send_index, shift(send_index, "c", 1)], axis=0)
    return own, shift(own, "y", -1), shift(own, "y", 2), shift(own, "y", 1)


def plan_lists(tables, list_slots, list_kinds):
    place = jnp.stack([lax.axis_index("y"), lax.axis_index("c")]).astype(jnp.int32)
    return pl.pallas_call(
        plan_kernel,
        out_shape=jax.ShapeDtypeStruct((list_slots.shape[0], WIDTH), jnp.int32),
        in_specs=[SMEM] * 5 + [VMEM] * 2,
        out_specs=VMEM,
        compiler_params=pltpu.CompilerParams(vmem_limit_bytes=4 << 20),
        cost_estimate=pl.CostEstimate(flops=1 << 20, bytes_accessed=1 << 20, transcendentals=0),
        name="plan",
    )(place, *tables, list_slots, list_kinds)


def local(children, interp_theta, interp_phi, translator, send_index, list_slots, list_kinds):
    samp_count = lax.axis_size(SAMP)
    polar_total = interp_theta.shape[1]
    azimuth_total = interp_phi.shape[1]
    child_boxes, _, rows, child_azimuth = children.shape
    own_children = child_boxes // samp_count
    parent_boxes = child_boxes // 8
    out_rows = polar_total // samp_count
    pattern = (2, out_rows, azimuth_total)

    x = children.reshape(samp_count, own_children, 2, rows, child_azimuth)
    x = lax.all_to_all(x, SAMP, split_axis=0, concat_axis=0, tiled=True)

    cosine, sine = phase_tables(polar_total, azimuth_total)
    theta, phi = pl.pallas_call(
        prepare_kernel,
        out_shape=[
            pltpu.VMEM(interp_theta.shape[::-1], jnp.bfloat16),
            pltpu.VMEM(interp_phi.shape, jnp.bfloat16),
        ],
        in_specs=[VMEM] * 2,
        out_specs=[VMEM] * 2,
        compiler_params=pltpu.CompilerParams(vmem_limit_bytes=4 << 20),
        cost_estimate=pl.CostEstimate(flops=1 << 20, bytes_accessed=1 << 18, transcendentals=0),
        name="prepare",
    )(interp_theta, interp_phi)
    tables = slot_tables(send_index)
    x, theta, phi, *tables = lax.optimization_barrier((x, theta, phi, *tables))
    mine = pl.pallas_call(
        aggregate_kernel,
        out_shape=jax.ShapeDtypeStruct((samp_count, own_children // 8) + pattern, jnp.bfloat16),
        in_specs=[VMEM] * 5,
        out_specs=VMEM,
        scratch_shapes=[
            pltpu.VMEM((16 * polar_total, child_azimuth), jnp.bfloat16),
            pltpu.VMEM((16, polar_total, azimuth_total), jnp.float32),
        ],
        compiler_params=pltpu.CompilerParams(vmem_limit_bytes=12 << 20),
        cost_estimate=pl.CostEstimate(flops=335 << 20, bytes_accessed=4 << 20, transcendentals=0),
        name="aggregate",
    )(x, theta, phi, cosine, sine)
    mine = lax.all_to_all(mine, SAMP, split_axis=0, concat_axis=0, tiled=True)
    lists = plan_lists(tables, list_slots, list_kinds)
    mine, lists = lax.optimization_barrier((mine, lists))
    own = mine.reshape((parent_boxes,) + pattern)
    after = shift(own, "y", -1)
    before = shift(own, "y", 1)
    other = shift(own, "c", 1)
    source, own = lax.optimization_barrier((translator, own))
    wide = pl.pallas_call(
        widen_kernel,
        out_shape=pltpu.VMEM(translator.shape, jnp.float32),
        in_specs=[HBM],
        out_specs=VMEM,
        scratch_shapes=[
            pltpu.VMEM(translator.shape, jnp.bfloat16),
            pltpu.SemaphoreType.DMA((4,)),
        ],
        compiler_params=pltpu.CompilerParams(vmem_limit_bytes=56 << 20),
        cost_estimate=pl.CostEstimate(flops=4 << 20, bytes_accessed=8 << 20, transcendentals=0),
        name="widen",
    )(source)

    own, wide = lax.optimization_barrier((own, wide))
    far = shift(own, "y", 2)

    shape = (parent_boxes,) + pattern
    pool_shape = pltpu.VMEM((8 * parent_boxes + 1,) + pattern, jnp.float32)
    params = pltpu.CompilerParams(vmem_limit_bytes=8 << 20)
    cost = pl.CostEstimate(flops=16 << 20, bytes_accessed=8 << 20, transcendentals=0)
    list_scratch = [pltpu.SMEM(lists.shape, jnp.int32), pltpu.SemaphoreType.DMA]
    pool, parents = pl.pallas_call(
        pool_kernel,
        out_shape=[pool_shape, jax.ShapeDtypeStruct(shape, jnp.bfloat16)],
        in_specs=[VMEM] * 2,
        out_specs=[VMEM, HBM],
        scratch_shapes=[pltpu.SemaphoreType.DMA],
        compiler_params=params,
        cost_estimate=cost,
        name="pool",
    )(own, other)
    after, before, pool = lax.optimization_barrier((after, before, pool))
    near = [after, shift(after, "c", 1), before, shift(before, "c", 1)]
    early, pool = pl.pallas_call(
        early_kernel,
        out_shape=[pltpu.VMEM(shape, jnp.float32), pool_shape],
        in_specs=[VMEM] * 7,
        out_specs=[VMEM] * 2,
        input_output_aliases={6: 1},
        scratch_shapes=list_scratch,
        compiler_params=params,
        cost_estimate=cost,
        name="early",
    )(lists, wide, *near, pool)
    far, early = lax.optimization_barrier((far, early))
    field, _ = pl.pallas_call(
        late_kernel,
        out_shape=[jax.ShapeDtypeStruct(shape, jnp.float32), pool_shape],
        in_specs=[VMEM] * 6,
        out_specs=[HBM, VMEM],
        input_output_aliases={5: 1},
        scratch_shapes=[pltpu.VMEM(shape, jnp.float32)]
        + list_scratch
        + [pltpu.SemaphoreType.DMA((4,))],
        compiler_params=params,
        cost_estimate=cost,
        name="late",
    )(lists, wide, early, far, shift(far, "c", 1), pool)
    return parents, field


def solution(mesh):
    y_count, x_count = 4, 4
    fine = Mesh(
        mesh.devices.reshape(y_count, mesh.shape["box"] // y_count, x_count, -1),
        BOX + SAMP,
    )
    return jax.shard_map(
        local,
        mesh=fine,
        in_specs=(
            P(BOX, None, SAMP, None),
            P(),
            P(),
            P(None, None, SAMP, None),
            P(BOX, None, None),
            P(BOX, None),
            P(BOX, None),
        ),
        out_specs=(P(BOX, None, SAMP, None), P(BOX, None, SAMP, None)),
        check_vma=False,
    )
```

time: 67.9 us -> 65.5 us (0.965)
  Pallas kernels: 27.3 us -> 16.7 us
  waiting for transfers between devices: 8.04 us -> 12.8 us
  starting transfers between devices: 26.7 us -> 30.2 us
    pallas_call x6 -> x4, Pallas kernels: 21.1 us -> 10.5 us  [the longest x1 3.89 us: local(): pl.pallas_call(early_kernel, out_shape=[pltpu.VMEM(shape, jnp.float32), p...]
    ppermute x11, waiting for transfers between devices: 2.07 us -> 7.62 us  [shift(): return lax.ppermute(x, axis, [(i, (i + step) % size) for i in range(size)])]
    ppermute x11, starting transfers between devices: 12.2 us -> 14.8 us  [shift(): return lax.ppermute(x, axis, [(i, (i + step) % size) for i in range(size)])]
    all_to_all x1, waiting for transfers between devices: 0.86 us -> 0.01 us  [local(): x = lax.all_to_all(x, SAMP, split_axis=0, concat_axis=0, tiled=True)]
    all_to_all x1, starting transfers between devices: 6.01 us -> 6.86 us  [local(): mine = lax.all_to_all(mine, SAMP, split_axis=0, concat_axis=0, tiled=True)]
  transfers between devices with their start and end apart: 13 -> 13, of which waited for: 5 -> 6; matrix products, arithmetic and copies ran while one was open for 4% -> 5% of each run, Pallas kernels for 31% -> 15%
where the time goes in v4:
time: 65.5 us; the launch traced here: 65 us
  starting transfers between devices  30.2 us (46%)
  Pallas kernels  16.7 us (25%)
  waiting for transfers between devices  12.8 us (20%)
  local copies, waits for them, and re-layouts  2.25 us (3%)
  other arithmetic  2.25 us (3%)
  between operations  0.79 us (1%)
    ppermute x11, starting transfers between devices, shift(): return lax.ppermute(x, axis, [(i, (i + step) % size) for i in range(size)])  14.8 us
    all_to_all x1, starting transfers between devices, local(): x = lax.all_to_all(x, SAMP, split_axis=0, concat_axis=0, tiled=True)  8.56 us
    ppermute x11, waiting for transfers between devices, shift(): return lax.ppermute(x, axis, [(i, (i + step) % size) for i in range(size)])  7.62 us
    all_to_all x1, starting transfers between devices, local(): mine = lax.all_to_all(mine, SAMP, split_axis=0, concat_axis=0, tiled=True)  6.86 us
    all_to_all x1, waiting for transfers between devices, local(): mine = lax.all_to_all(mine, SAMP, split_axis=0, concat_axis=0, tiled=True)  5.16 us
    pallas_call x1, Pallas kernels, local(): pl.pallas_call(early_kernel, out_shape=[pltpu.VMEM(shape, jnp.float32), p...  3.89 us
    pallas_call x1, Pallas kernels, local(): pl.pallas_call(late_kernel, out_shape=[jax.ShapeDtypeStruct(shape, jnp.fl...  3.83 us
    pallas_call x1, Pallas kernels, local(): pl.pallas_call(widen_kernel, out_shape=pltpu.VMEM(translator.shape, jnp.f...  3.09 us
  transfers between devices with their start and end apart: 13, of which 6 were waited for; matrix products, arithmetic and copies ran while one was open for 5% of the time, Pallas kernels for 15%

profile of v4, /device:TPU:1, one launch (start us, length us, event | category | flops | bytes accessed | tf_op | source)
XLA Modules:
  0.0 65.0 jit_solution(10665408000708217758)
XLA Ops:
  0.6 0.0 copy-start.3
  0.6 0.0 copy-start.2
  0.6 8.6 %all-to-all-start = ((bf16[16,16,2,4,128]{4,3,2,1,0:T(4,128)(2,1)}), bf16[16,16,2,4,128]{4,3,2,1,0:T(4,128)(2,1)S(1)}, u32[]{:S(2)}, u32[]{:S(2)}) async-start(bf16[16,16,2,4,128]{4,3,2,1,0:T(4,128)(2,1)} %bitcast.9), calls=%async_computation | async-start | bytes 1048576 | tf_op jit(solution)/shard_map/all_to_all | solution.py:250
  9.2 1.0 %collective-permute-start = (s32[1,8,16]{2,1,0:T(8,128)}, s32[1,8,16]{2,1,0:T(8,128)S(1)}, u32[]{:S(2)}, u32[]{:S(2)}) collective-permute-start(s32[1,8,16]{2,1,0:T(8,128)} %param.11), channel_id=1, source_target_pairs={{0,16},{16,0},{1,17},{17,1},{2,18},{18,2},{3,19},{19,3},{4,20},{20... | collective-permute-start | bytes 1544 | tf_op jit(solution)/shard_map/ppermute | solution.py:178
  10.3 0.7 %constant_dynamic-update-slice_fusion.1 = s32[2,8,16]{2,1,0:T(8,128)S(1)} fusion(s32[1,8,16]{2,1,0:T(8,128)} %param.11), kind=kLoop, calls=%fused_computation.6 | loop fusion | bytes 4608
  11.0 0.1 broadcast_multiply_fusion.1
  11.2 0.1 collective-permute-done
  11.3 1.3 %collective-permute-start.3 = (s32[2,8,16]{2,1,0:T(8,128)S(1)}, s32[2,8,16]{2,1,0:T(8,128)S(1)}, u32[]{:S(2)}, u32[]{:S(2)}) collective-permute-start(s32[2,8,16]{2,1,0:T(8,128)S(1)} %constant_dynamic-update-slice_fusion.own_ref), channel_id=1, source_target_pairs={{0,32},{32,64},{64,96},{96,0},{1,33},{33,65},{65,97},{97,1},{2,34}... | collective-permute-start | bytes 3080 | tf_op jit(solution)/shard_map/ppermute | solution.py:178
  12.6 2.6 %collective-permute-start.2 = (s32[2,8,16]{2,1,0:T(8,128)S(1)}, s32[2,8,16]{2,1,0:T(8,128)S(1)}, u32[]{:S(2)}, u32[]{:S(2)}) collective-permute-start(s32[2,8,16]{2,1,0:T(8,128)S(1)} %constant_dynamic-update-slice_fusion.own_ref), channel_id=1, source_target_pairs={{0,64},{32,96},{64,0},{96,32},{1,65},{33,97},{65,1},{97,33},{2,66}... | collective-permute-start | bytes 3080 | tf_op jit(solution)/shard_map/ppermute | solution.py:178
  15.2 1.1 %collective-permute-start.1 = (s32[2,8,16]{2,1,0:T(8,128)S(1)}, s32[2,8,16]{2,1,0:T(8,128)S(1)}, u32[]{:S(2)}, u32[]{:S(2)}) collective-permute-start(s32[2,8,16]{2,1,0:T(8,128)S(1)} %constant_dynamic-update-slice_fusion.own_ref), channel_id=1, source_target_pairs={{0,96},{32,0},{64,32},{96,64},{1,97},{33,1},{65,33},{97,65},{2,98}... | collective-permute-start | bytes 3080 | tf_op jit(solution)/shard_map/ppermute | solution.py:178
  16.3 2.0 %fusion = (f32[4,128,256]{2,1,0:T(8,128)S(1)}, f32[4,128,256]{2,1,0:T(8,128)S(1)}) fusion(f32[128]{0:T(128)S(1)} %fusion.4, f32[128,256]{1,0:T(8,128)S(1)} %get-tuple-element.55, f32[4]{0:T(128)S(1)} %get-tuple-element.58, f32[128,256]{1,0:T(8,128)S(1)} %get-tuple-element.54, f32[4]{0:T(128)S(1)} %get-tuple-element.59), kind=kLoop, calls=%fused_computation.1 | loop fusion | flops 655360 | bytes 1311264 | tf_op jit(solution)/shard_map/sin | solution.py:35
  18.2 0.0 copy-start
  18.2 0.8 %copy-done = bf16[128,256]{1,0:T(8,128)(2,1)S(1)} copy-done((bf16[128,256]{1,0:T(8,128)(2,1)S(1)}, bf16[128,256]{1,0:T(8,128)(2,1)}, u32[]{:S(2)}) %copy-start) | copy-done | bytes 65560
  19.1 0.0 copy-start.1
  19.1 0.7 %copy-done.1 = bf16[64,128]{1,0:T(8,128)(2,1)S(1)} copy-done((bf16[64,128]{1,0:T(8,128)(2,1)S(1)}, bf16[64,128]{1,0:T(8,128)(2,1)}, u32[]{:S(2)}) %copy-start.1) | copy-done | bytes 16408
  19.8 0.1 prepare.1
  19.9 0.0 collective-permute-done.3.before_ref
  19.9 0.0 collective-permute-done.2.far_ref
  19.9 0.0 collective-permute-done.1.after_ref
  19.9 0.0 all-to-all-done.x_ref
  19.9 3.1 %aggregate.1 = bf16[16,2,2,8,256]{4,3,2,1,0:T(8,128)(2,1)} custom-call(bf16[16,16,2,4,128]{4,3,2,1,0:T(4,128)(2,1)S(1)} %all-to-all-done.x_ref, bf16[128,64]{1,0:T(8,128)(2,1)S(1)} %get-tuple-element.30.theta_ref, bf16[128,256]{1,0:T(8,128)(2,1)S(1)} %get-tuple-element.31.phi_ref, f32[4,128,256]{2,1,0:T(8,128)S(1)} %get-tuple-element.53.cos_ref, ...), custom_call_target="tpu_custom_call" | custom-call | flops 351272960 | bytes 4194304 | tf_op jit(solution)/shard_map/aggregate/pallas_call | solution.py:267
  23.0 6.9 %all-to-all-start.1 = ((bf16[16,2,2,8,256]{4,3,2,1,0:T(8,128)(2,1)}), bf16[16,2,2,8,256]{4,3,2,1,0:T(8,128)(2,1)S(1)}, u32[]{:S(2)}, u32[]{:S(2)}) async-start(bf16[16,2,2,8,256]{4,3,2,1,0:T(8,128)(2,1)} %aggregate.1), calls=%async_computation.1 | async-start | bytes 524288 | tf_op jit(solution)/shard_map/all_to_all | solution.py:280
  29.9 0.1 pad_add_fusion.place_ref
  29.9 0.0 copy-done.3
  30.0 0.0 copy-done.2
  30.0 2.1 %plan.1.lists = s32[32,128]{1,0:T(8,128)S(1)} custom-call(s32[2]{0:T(128)S(1)} %pad_add_fusion.place_ref, s32[2,8,16]{2,1,0:T(8,128)S(1)} %constant_dynamic-update-slice_fusion.own_ref, s32[2,8,16]{2,1,0:T(8,128)S(1)} %collective-permute-done.1.after_ref, s32[2,8,16]{2,1,0:T(8,128)S(1)} %collective-permute-done.2.far_ref, ...), custom_call_target="tpu_custom_call" | custom-call | flops 1048576 | bytes 1048576 | tf_op jit(solution)/shard_map/plan/pallas_call | solution.py:228
  32.0 5.2 %all-to-all-done.1 = bf16[16,2,2,8,256]{4,3,2,1,0:T(8,128)(2,1)S(1)} async-done(((bf16[16,2,2,8,256]{4,3,2,1,0:T(8,128)(2,1)}), bf16[16,2,2,8,256]{4,3,2,1,0:T(8,128)(2,1)S(1)}, u32[]{:S(2)}, u32[]{:S(2)}) %all-to-all-start.1) | async-done | bytes 262176 | tf_op jit(solution)/shard_map/all_to_all | solution.py:280
  37.2 2.7 %collective-permute-start.4 = (bf16[32,2,8,256]{3,2,1,0:T(8,128)(2,1)S(1)}, bf16[32,2,8,256]{3,2,1,0:T(8,128)(2,1)S(1)}, u32[]{:S(2)}, u32[]{:S(2)}) collective-permute-start(bf16[32,2,8,256]{3,2,1,0:T(8,128)(2,1)S(1)} %bitcast.4), channel_id=1, source_target_pairs={{0,16},{16,0},{1,17},{17,1},{2,18},{18,2},{3,19},{19,3},{4,20},{20... | collective-permute-start | bytes 786440 | tf_op jit(solution)/shard_map/ppermute | solution.py:178
  39.8 0.4 collective-permute-start.7
  40.2 2.3 %collective-permute-start.6 = (bf16[32,2,8,256]{3,2,1,0:T(8,128)(2,1)S(1)}, bf16[32,2,8,256]{3,2,1,0:T(8,128)(2,1)S(1)}, u32[]{:S(2)}, u32[]{:S(2)}) collective-permute-start(bf16[32,2,8,256]{3,2,1,0:T(8,128)(2,1)S(1)} %bitcast.6), channel_id=1, source_target_pairs={{0,96},{32,0},{64,32},{96,64},{1,97},{33,1},{65,33},{97,65},{2,98}... | collective-permute-start | bytes 786440 | tf_op jit(solution)/shard_map/ppermute | solution.py:178
  42.5 3.1 %widen.1.trans_ref = f32[316,2,8,256]{3,2,1,0:T(8,128)S(1)} custom-call(bf16[316,2,8,256]{3,2,1,0:T(8,128)(2,1)} %x_ref), custom_call_target="tpu_custom_call" | custom-call | flops 4194304 | bytes 8388608 | tf_op jit(solution)/shard_map/widen/pallas_call | solution.py:288
  45.6 0.0 collective-permute-done.4.other_ref
  45.6 0.7 %pool.1 = (f32[257,2,8,256]{3,2,1,0:T(8,128)S(1)}, bf16[32,2,8,256]{3,2,1,0:T(8,128)(2,1)}) custom-call(bf16[32,2,8,256]{3,2,1,0:T(8,128)(2,1)S(1)} %bitcast.7, bf16[32,2,8,256]{3,2,1,0:T(8,128)(2,1)S(1)} %collective-permute-done.4.other_ref), custom_call_target="tpu_custom_call" | custom-call | flops 16777216 | bytes 8388608 | tf_op jit(solution)/shard_map/pool/pallas_call | solution.py:310
  46.3 2.6 %collective-permute-done.7.refs_2_ = bf16[32,2,8,256]{3,2,1,0:T(8,128)(2,1)S(1)} collective-permute-done((bf16[32,2,8,256]{3,2,1,0:T(8,128)(2,1)S(1)}, bf16[32,2,8,256]{3,2,1,0:T(8,128)(2,1)S(1)}, u32[]{:S(2)}, u32[]{:S(2)}) %collective-permute-start.7) | collective-permute-done | bytes 262176 | tf_op jit(solution)/shard_map/ppermute | solution.py:178
  48.9 0.0 collective-permute-done.6.refs_0_
  48.9 0.9 %collective-permute-start.8 = (bf16[32,2,8,256]{3,2,1,0:T(8,128)(2,1)S(1)}, bf16[32,2,8,256]{3,2,1,0:T(8,128)(2,1)S(1)}, u32[]{:S(2)}, u32[]{:S(2)}) collective-permute-start(bf16[32,2,8,256]{3,2,1,0:T(8,128)(2,1)S(1)} %collective-permute-done.6.refs_0_), channel_id=1, source_target_pairs={{0,16},{16,0},{1,17},{17,1},{2,18},{18,2},{3,19},{19,3},{4,20},{20... | collective-permute-start | bytes 786440 | tf_op jit(solution)/shard_map/ppermute | solution.py:178
  49.8 0.0 collective-permute-start.9
  49.8 1.2 %collective-permute-start.5 = (bf16[32,2,8,256]{3,2,1,0:T(8,128)(2,1)S(1)}, bf16[32,2,8,256]{3,2,1,0:T(8,128)(2,1)S(1)}, u32[]{:S(2)}, u32[]{:S(2)}) collective-permute-start(bf16[32,2,8,256]{3,2,1,0:T(8,128)(2,1)S(1)} %bitcast.8), channel_id=1, source_target_pairs={{0,64},{32,96},{64,0},{96,32},{1,65},{33,97},{65,1},{97,33},{2,66}... | collective-permute-start | bytes 786440 | tf_op jit(solution)/shard_map/ppermute | solution.py:178
  51.0 0.0 collective-permute-done.8.refs_1_
  51.0 0.3 collective-permute-done.9.refs_3_
  51.3 3.9 %early.1 = (f32[32,2,8,256]{3,2,1,0:T(8,128)S(1)}, f32[257,2,8,256]{3,2,1,0:T(8,128)S(1)}) custom-call(s32[32,128]{1,0:T(8,128)S(1)} %plan.1.lists, f32[316,2,8,256]{3,2,1,0:T(8,128)S(1)} %widen.1.trans_ref, bf16[32,2,8,256]{3,2,1,0:T(8,128)(2,1)S(1)} %collective-permute-done.6.refs_0_, ...), custom_call_target="tpu_custom_call", output_to_operand_aliasing={{1}: (6, {})} | custom-call | flops 16777216 | bytes 8388608 | tf_op jit(solution)/shard_map/early/pallas_call | solution.py:322
  55.2 3.4 %collective-permute-done.5.refs_0_ = bf16[32,2,8,256]{3,2,1,0:T(8,128)(2,1)S(1)} collective-permute-done((bf16[32,2,8,256]{3,2,1,0:T(8,128)(2,1)S(1)}, bf16[32,2,8,256]{3,2,1,0:T(8,128)(2,1)S(1)}, u32[]{:S(2)}, u32[]{:S(2)}) %collective-permute-start.5) | collective-permute-done | bytes 262176 | tf_op jit(solution)/shard_map/ppermute | solution.py:178
  58.6 1.4 %collective-permute-start.10 = (bf16[32,2,8,256]{3,2,1,0:T(8,128)(2,1)S(1)}, bf16[32,2,8,256]{3,2,1,0:T(8,128)(2,1)S(1)}, u32[]{:S(2)}, u32[]{:S(2)}) collective-permute-start(bf16[32,2,8,256]{3,2,1,0:T(8,128)(2,1)S(1)} %collective-permute-done.5.refs_0_), channel_id=1, source_target_pairs={{0,16},{16,0},{1,17},{17,1},{2,18},{18,2},{3,19},{19,3},{4,20},{20... | collective-permute-start | bytes 786440 | tf_op jit(solution)/shard_map/ppermute | solution.py:178
  60.0 1.2 %collective-permute-done.10.refs_1_ = bf16[32,2,8,256]{3,2,1,0:T(8,128)(2,1)S(1)} collective-permute-done((bf16[32,2,8,256]{3,2,1,0:T(8,128)(2,1)S(1)}, bf16[32,2,8,256]{3,2,1,0:T(8,128)(2,1)S(1)}, u32[]{:S(2)}, u32[]{:S(2)}) %collective-permute-start.10) | collective-permute-done | bytes 262176 | tf_op jit(solution)/shard_map/ppermute | solution.py:178
  61.2 3.8 %late.1 = (f32[32,2,8,256]{3,2,1,0:T(8,128)}, f32[257,2,8,256]{3,2,1,0:T(8,128)S(1)}) custom-call(s32[32,128]{1,0:T(8,128)S(1)} %plan.1.lists, f32[316,2,8,256]{3,2,1,0:T(8,128)S(1)} %widen.1.trans_ref, f32[32,2,8,256]{3,2,1,0:T(8,128)S(1)} %get-tuple-element.48.sum_ref, ...), custom_call_target="tpu_custom_call", output_to_operand_aliasing={{1}: (5, {})} | custom-call | flops 16777216 | bytes 8388608 | tf_op jit(solution)/shard_map/late/pallas_call | solution.py:334
  (5 shorter events, 0.1 us)
Async XLA Ops:
  0.6 29.3 %copy-start.3 = (s32[32,64]{1,0:T(8,128)S(1)}, s32[32,64]{1,0:T(8,128)}, u32[]{:S(2)}) copy-start(s32[32,64]{1,0:T(8,128)} %kinds_ref.1) | copy-start | bytes 24580
  0.6 29.3 %copy-start.2 = (s32[32,64]{1,0:T(8,128)S(1)}, s32[32,64]{1,0:T(8,128)}, u32[]{:S(2)}) copy-start(s32[32,64]{1,0:T(8,128)} %slots_ref.1) | copy-start | bytes 24580
  0.6 19.3 %all-to-all-start = ((bf16[16,16,2,4,128]{4,3,2,1,0:T(4,128)(2,1)}), bf16[16,16,2,4,128]{4,3,2,1,0:T(4,128)(2,1)S(1)}, u32[]{:S(2)}, u32[]{:S(2)}) async-start(bf16[16,16,2,4,128]{4,3,2,1,0:T(4,128)(2,1)} %bitcast.9), calls=%async_computation | async-start | bytes 1048576 | tf_op jit(solution)/shard_map/all_to_all | solution.py:250
  9.2 2.1 %collective-permute-start = (s32[1,8,16]{2,1,0:T(8,128)}, s32[1,8,16]{2,1,0:T(8,128)S(1)}, u32[]{:S(2)}, u32[]{:S(2)}) collective-permute-start(s32[1,8,16]{2,1,0:T(8,128)} %param.11), channel_id=1, source_target_pairs={{0,16},{16,0},{1,17},{17,1},{2,18},{18,2},{3,19},{19,3},{4,20},{20... | collective-permute-start | bytes 1544 | tf_op jit(solution)/shard_map/ppermute | solution.py:178
  11.3 8.6 %collective-permute-start.3 = (s32[2,8,16]{2,1,0:T(8,128)S(1)}, s32[2,8,16]{2,1,0:T(8,128)S(1)}, u32[]{:S(2)}, u32[]{:S(2)}) collective-permute-start(s32[2,8,16]{2,1,0:T(8,128)S(1)} %constant_dynamic-update-slice_fusion.own_ref), channel_id=1, source_target_pairs={{0,32},{32,64},{64,96},{96,0},{1,33},{33,65},{65,97},{97,1},{2,34}... | collective-permute-start | bytes 3080 | tf_op jit(solution)/shard_map/ppermute | solution.py:178
  12.6 7.3 %collective-permute-start.2 = (s32[2,8,16]{2,1,0:T(8,128)S(1)}, s32[2,8,16]{2,1,0:T(8,128)S(1)}, u32[]{:S(2)}, u32[]{:S(2)}) collective-permute-start(s32[2,8,16]{2,1,0:T(8,128)S(1)} %constant_dynamic-update-slice_fusion.own_ref), channel_id=1, source_target_pairs={{0,64},{32,96},{64,0},{96,32},{1,65},{33,97},{65,1},{97,33},{2,66}... | collective-permute-start | bytes 3080 | tf_op jit(solution)/shard_map/ppermute | solution.py:178
  15.2 4.7 %collective-permute-start.1 = (s32[2,8,16]{2,1,0:T(8,128)S(1)}, s32[2,8,16]{2,1,0:T(8,128)S(1)}, u32[]{:S(2)}, u32[]{:S(2)}) collective-permute-start(s32[2,8,16]{2,1,0:T(8,128)S(1)} %constant_dynamic-update-slice_fusion.own_ref), channel_id=1, source_target_pairs={{0,96},{32,0},{64,32},{96,64},{1,97},{33,1},{65,33},{97,65},{2,98}... | collective-permute-start | bytes 3080 | tf_op jit(solution)/shard_map/ppermute | solution.py:178
  18.2 0.8 %copy-start = (bf16[128,256]{1,0:T(8,128)(2,1)S(1)}, bf16[128,256]{1,0:T(8,128)(2,1)}, u32[]{:S(2)}) copy-start(bf16[128,256]{1,0:T(8,128)(2,1)} %phi_ref.1) | copy-start | bytes 196612
  19.1 0.7 %copy-start.1 = (bf16[64,128]{1,0:T(8,128)(2,1)S(1)}, bf16[64,128]{1,0:T(8,128)(2,1)}, u32[]{:S(2)}) copy-start(bf16[64,128]{1,0:T(8,128)(2,1)} %theta_ref.1) | copy-start | bytes 49156
  23.0 14.2 %all-to-all-start.1 = ((bf16[16,2,2,8,256]{4,3,2,1,0:T(8,128)(2,1)}), bf16[16,2,2,8,256]{4,3,2,1,0:T(8,128)(2,1)S(1)}, u32[]{:S(2)}, u32[]{:S(2)}) async-start(bf16[16,2,2,8,256]{4,3,2,1,0:T(8,128)(2,1)} %aggregate.1), calls=%async_computation.1 | async-start | bytes 524288 | tf_op jit(solution)/shard_map/all_to_all | solution.py:280
  37.2 8.4 %collective-permute-start.4 = (bf16[32,2,8,256]{3,2,1,0:T(8,128)(2,1)S(1)}, bf16[32,2,8,256]{3,2,1,0:T(8,128)(2,1)S(1)}, u32[]{:S(2)}, u32[]{:S(2)}) collective-permute-start(bf16[32,2,8,256]{3,2,1,0:T(8,128)(2,1)S(1)} %bitcast.4), channel_id=1, source_target_pairs={{0,16},{16,0},{1,17},{17,1},{2,18},{18,2},{3,19},{19,3},{4,20},{20... | collective-permute-start | bytes 786440 | tf_op jit(solution)/shard_map/ppermute | solution.py:178
  39.8 9.1 %collective-permute-start.7 = (bf16[32,2,8,256]{3,2,1,0:T(8,128)(2,1)S(1)}, bf16[32,2,8,256]{3,2,1,0:T(8,128)(2,1)S(1)}, u32[]{:S(2)}, u32[]{:S(2)}) collective-permute-start(bf16[32,2,8,256]{3,2,1,0:T(8,128)(2,1)S(1)} %bitcast.5), channel_id=1, source_target_pairs={{0,32},{32,64},{64,96},{96,0},{1,33},{33,65},{65,97},{97,1},{2,34}... | collective-permute-start | bytes 786440 | tf_op jit(solution)/shard_map/ppermute | solution.py:178
  40.2 8.7 %collective-permute-start.6 = (bf16[32,2,8,256]{3,2,1,0:T(8,128)(2,1)S(1)}, bf16[32,2,8,256]{3,2,1,0:T(8,128)(2,1)S(1)}, u32[]{:S(2)}, u32[]{:S(2)}) collective-permute-start(bf16[32,2,8,256]{3,2,1,0:T(8,128)(2,1)S(1)} %bitcast.6), channel_id=1, source_target_pairs={{0,96},{32,0},{64,32},{96,64},{1,97},{33,1},{65,33},{97,65},{2,98}... | collective-permute-start | bytes 786440 | tf_op jit(solution)/shard_map/ppermute | solution.py:178
  48.9 2.1 %collective-permute-start.8 = (bf16[32,2,8,256]{3,2,1,0:T(8,128)(2,1)S(1)}, bf16[32,2,8,256]{3,2,1,0:T(8,128)(2,1)S(1)}, u32[]{:S(2)}, u32[]{:S(2)}) collective-permute-start(bf16[32,2,8,256]{3,2,1,0:T(8,128)(2,1)S(1)} %collective-permute-done.6.refs_0_), channel_id=1, source_target_pairs={{0,16},{16,0},{1,17},{17,1},{2,18},{18,2},{3,19},{19,3},{4,20},{20... | collective-permute-start | bytes 786440 | tf_op jit(solution)/shard_map/ppermute | solution.py:178
  49.8 1.5 %collective-permute-start.9 = (bf16[32,2,8,256]{3,2,1,0:T(8,128)(2,1)S(1)}, bf16[32,2,8,256]{3,2,1,0:T(8,128)(2,1)S(1)}, u32[]{:S(2)}, u32[]{:S(2)}) collective-permute-start(bf16[32,2,8,256]{3,2,1,0:T(8,128)(2,1)S(1)} %collective-permute-done.7.refs_2_), channel_id=1, source_target_pairs={{0,16},{16,0},{1,17},{17,1},{2,18},{18,2},{3,19},{19,3},{4,20},{20... | collective-permute-start | bytes 786440 | tf_op jit(solution)/shard_map/ppermute | solution.py:178
  49.8 8.9 %collective-permute-start.5 = (bf16[32,2,8,256]{3,2,1,0:T(8,128)(2,1)S(1)}, bf16[32,2,8,256]{3,2,1,0:T(8,128)(2,1)S(1)}, u32[]{:S(2)}, u32[]{:S(2)}) collective-permute-start(bf16[32,2,8,256]{3,2,1,0:T(8,128)(2,1)S(1)} %bitcast.8), channel_id=1, source_target_pairs={{0,64},{32,96},{64,0},{96,32},{1,65},{33,97},{65,1},{97,33},{2,66}... | collective-permute-start | bytes 786440 | tf_op jit(solution)/shard_map/ppermute | solution.py:178
  58.6 2.5 %collective-permute-start.10 = (bf16[32,2,8,256]{3,2,1,0:T(8,128)(2,1)S(1)}, bf16[32,2,8,256]{3,2,1,0:T(8,128)(2,1)S(1)}, u32[]{:S(2)}, u32[]{:S(2)}) collective-permute-start(bf16[32,2,8,256]{3,2,1,0:T(8,128)(2,1)S(1)} %collective-permute-done.5.refs_0_), channel_id=1, source_target_pairs={{0,16},{16,0},{1,17},{17,1},{2,18},{18,2},{3,19},{19,3},{4,20},{20... | collective-permute-start | bytes 786440 | tf_op jit(solution)/shard_map/ppermute | solution.py:178

commit v5 on v4

--- a/solution.py
+++ b/solution.py
@@ -12,7 +12,9 @@
 SAMP = ("x", "z")
 BOX = ("y", "c")
 WIDTH = 128
-EARLY = 40
+FIRST = 12
+EARLY = 44
+CHUNK = 16
 VMEM = pl.BlockSpec(memory_space=pltpu.VMEM)
 SMEM = pl.BlockSpec(memory_space=pltpu.SMEM)
 HBM = pl.BlockSpec(memory_space=pltpu.HBM)
@@ -35,42 +37,37 @@
     return jnp.cos(phase), jnp.sin(phase)
 
 
-def prepare_kernel(theta_ref, phi_ref, turned_ref, copy_ref):
-    turned_ref[...] = jnp.transpose(theta_ref[...].astype(jnp.float32)).astype(jnp.bfloat16)
-    copy_ref[...] = phi_ref[...]
-
-
-def aggregate_kernel(x_ref, theta_ref, phi_ref, cos_ref, sin_ref, out_ref, mid_ref, raised_ref):
-    theta = theta_ref[...]
-    polar_total = theta.shape[0]
+def aggregate_kernel(x_ref, theta_ref, phi_ref, cos_ref, sin_ref, out_ref, mid_ref):
+    theta = jnp.transpose(theta_ref[...].astype(jnp.float32)).astype(jnp.bfloat16)
+    phi = phi_ref[...]
+    chunks = theta.shape[0] // CHUNK
     for p in range(out_ref.shape[1]):
         for o in range(8):
             for r in range(2):
-                x = x_ref[:, p * 8 + o, r].reshape(theta.shape[1], phi_ref.shape[0])
-                mid = jnp.dot(theta, x, preferred_element_type=jnp.float32)
-                k = o * 2 + r
-                mid_ref[k * polar_total : (k + 1) * polar_total, :] = mid.astype(jnp.bfloat16)
-        raised_ref[...] = jnp.dot(mid_ref[...], phi_ref[...], preferred_element_type=jnp.float32).reshape(
-            raised_ref.shape
-        )
-
-        def slab(s, carry):
-            rows = pl.ds(pl.multiple_of(s * 8, 8), 8)
-            real = imag = None
-            for o in range(4):
-                c = cos_ref[o, rows, :]
-                d = sin_ref[o, rows, :]
-                ar, ai = raised_ref[2 * o, rows, :], raised_ref[2 * o + 1, rows, :]
-                br, bi = raised_ref[14 - 2 * o, rows, :], raised_ref[15 - 2 * o, rows, :]
-                tr = c * (ar + br) - d * (ai - bi)
-                ti = d * (ar - br) + c * (ai + bi)
-                real = tr if real is None else real + tr
-                imag = ti if imag is None else imag + ti
-            out_ref[s, p, 0] = real.astype(jnp.bfloat16)
-            out_ref[s, p, 1] = imag.astype(jnp.bfloat16)
-            return carry
-
-        lax.fori_loop(0, out_ref.shape[0], slab, 0)
+                x = x_ref[:, p * 8 + o, r].reshape(theta.shape[1], phi.shape[0])
+                mid = jnp.dot(theta, x, preferred_element_type=jnp.float32).astype(jnp.bfloat16)
+                for h in range(chunks):
+                    at = (h * 16 + o * 2 + r) * CHUNK
+                    mid_ref[at : at + CHUNK, :] = mid[h * CHUNK : (h + 1) * CHUNK]
+        for h in range(chunks):
+            mid = mid_ref[h * 16 * CHUNK : (h + 1) * 16 * CHUNK, :]
+            raised = jnp.dot(mid, phi, preferred_element_type=jnp.float32)
+            for s in range(CHUNK // 8):
+                row = h * CHUNK + s * 8
+                real = imag = None
+                for o in range(4):
+                    c = cos_ref[o, row : row + 8, :]
+                    d = sin_ref[o, row : row + 8, :]
+                    ar, ai, br, bi = (
+                        raised[k * CHUNK + s * 8 : k * CHUNK + s * 8 + 8]
+                        for k in (2 * o, 2 * o + 1, 14 - 2 * o, 15 - 2 * o)
+                    )
+                    tr = c * (ar + br) - d * (ai - bi)
+                    ti = d * (ar - br) + c * (ai + bi)
+                    real = tr if real is None else real + tr
+                    imag = ti if imag is None else imag + ti
+                out_ref[row // 8, p, 0] = real.astype(jnp.bfloat16)
+                out_ref[row // 8, p, 1] = imag.astype(jnp.bfloat16)
 
 
 def widen_kernel(x_ref, out_ref, buffer, sems):
@@ -99,16 +96,6 @@
         return carry
 
     lax.fori_loop(0, block.shape[0], widen, 0, unroll=4)
-
-
-def pool_kernel(own_ref, other_ref, pool_ref, parents_ref, sem):
-    copy = pltpu.make_async_copy(own_ref, parents_ref, sem)
-    copy.start()
-    boxes = own_ref.shape[0]
-    widen_rows(own_ref, pool_ref, 0)
-    widen_rows(other_ref, pool_ref, boxes)
-    pool_ref[pool_ref.shape[0] - 1] = jnp.zeros(pool_ref.shape[1:], jnp.float32)
-    copy.wait()
 
 
 def add_entry(list_ref, trans_ref, pool_ref, b, j, real, imag):
@@ -119,7 +106,42 @@
     return real + (tr * sr - ti * si), imag + (tr * si + ti * sr)
 
 
-def early_kernel(lists, trans_ref, *refs):
+def add_box(list_ref, trans_ref, pool_ref, b, some, rest, acc):
+    def more(j, acc):
+        return add_entry(list_ref, trans_ref, pool_ref, b, j, *acc)
+
+    if rest is not None:
+        acc = lax.fori_loop(*rest, more, acc)
+    for j in some:
+        acc = add_entry(list_ref, trans_ref, pool_ref, b, j, *acc)
+    return acc
+
+
+def first_kernel(lists, trans_ref, own_ref, other_ref, out_ref, pool_ref, parents_ref, *scratch):
+    list_ref, sem, out_sem = scratch
+    copy = pltpu.make_async_copy(lists, list_ref, sem)
+    copy.start()
+    store = pltpu.make_async_copy(own_ref, parents_ref, out_sem)
+    store.start()
+    boxes = own_ref.shape[0]
+    widen_rows(own_ref, pool_ref, 0)
+    widen_rows(other_ref, pool_ref, boxes)
+    pool_ref[pool_ref.shape[0] - 1] = jnp.zeros(pool_ref.shape[1:], jnp.float32)
+    copy.wait()
+
+    def box(b, carry):
+        zero = jnp.zeros(out_ref.shape[2:], jnp.float32)
+        some = range(64, 64 + FIRST)
+        out_ref[b, 0], out_ref[b, 1] = add_box(
+            list_ref, trans_ref, pool_ref, b, some, None, (zero, zero)
+        )
+        return carry
+
+    lax.fori_loop(0, boxes, box, 0)
+    store.wait()
+
+
+def early_kernel(lists, trans_ref, sum_ref, *refs):
     *blocks, _, out_ref, pool_ref, list_ref, sem = refs
     copy = pltpu.make_async_copy(lists, list_ref, sem)
     copy.start()
@@ -129,11 +151,12 @@
     copy.wait()
 
     def box(b, carry):
-        real = imag = jnp.zeros(out_ref.shape[2:], jnp.float32)
-        for j in range(EARLY):
-            real, imag = add_entry(list_ref, trans_ref, pool_ref, b, 64 + j, real, imag)
-        out_ref[b, 0] = real
-        out_ref[b, 1] = imag
+        rest = (list_ref[b, WIDTH - 2], jnp.minimum(list_ref[b, WIDTH - 1], FIRST))
+        some = range(64 + FIRST, 64 + EARLY)
+        acc = (sum_ref[b, 0], sum_ref[b, 1])
+        out_ref[b, 0], out_ref[b, 1] = add_box(
+            list_ref, trans_ref, pool_ref, b, some, rest, acc
+        )
         return carry
 
     lax.fori_loop(0, boxes, box, 0)
@@ -149,15 +172,11 @@
     copy.wait()
 
     def box(b, carry):
-        def more(j, acc):
-            return add_entry(list_ref, trans_ref, pool_ref, b, j, *acc)
-
+        rest = (list_ref[b, WIDTH - 1], EARLY)
         acc = (sum_ref[b, 0], sum_ref[b, 1])
-        real, imag = lax.fori_loop(list_ref[b, WIDTH - 1], EARLY, more, acc)
-        for j in range(EARLY, 64):
-            real, imag = add_entry(list_ref, trans_ref, pool_ref, b, j, real, imag)
-        out_ref[b, 0] = real
-        out_ref[b, 1] = imag
+        out_ref[b, 0], out_ref[b, 1] = add_box(
+            list_ref, trans_ref, pool_ref, b, range(EARLY, 64), rest, acc
+        )
         return carry
 
     parts = sems.shape[0]
@@ -178,7 +197,7 @@
     return lax.ppermute(x, axis, [(i, (i + step) % size) for i in range(size)])
 
 
-def plan_kernel(place_ref, own_ref, after_ref, far_ref, before_ref, slots_ref, kinds_ref, out_ref):
+def plan_kernel(place_ref, own_ref, after_ref, before_ref, far_ref, slots_ref, kinds_ref, out_ref):
     y, c = place_ref[0], place_ref[1]
     cores, _, cap = own_ref.shape
     boxes, entries = slots_ref.shape
@@ -196,15 +215,17 @@
             for u in range(cap):
                 value = table[core, me, u] + (block + core) * boxes
                 row = jnp.where(code == (k * cores + core) * cap + u, value, row)
-    near = dy != 2
     first = lax.broadcasted_iota(jnp.int32, (entries, entries), 0)
     second = lax.broadcasted_iota(jnp.int32, (entries, entries), 1)
     ahead = (first < second).astype(jnp.float32)
-    inside = jnp.dot(near.astype(jnp.float32), ahead, preferred_element_type=jnp.float32)
-    inside = inside.astype(jnp.int32)
-    own_spot = lax.broadcasted_iota(jnp.int32, slots.shape, 1)
-    count = jnp.sum(near.astype(jnp.int32), axis=1, keepdims=True)
-    spot = jnp.where(near, inside, count + own_spot - inside)
+    spot = jnp.zeros_like(slots)
+    begin = jnp.zeros((boxes, 1), jnp.int32)
+    ends = []
+    for mine in (dy == 0, (dy & 1) == 1, dy == 2):
+        inside = jnp.dot(mine.astype(jnp.float32), ahead, preferred_element_type=jnp.float32)
+        spot = jnp.where(mine, begin + inside.astype(jnp.int32), spot)
+        begin = begin + jnp.sum(mine.astype(jnp.int32), axis=1, keepdims=True)
+        ends.append(begin)
     value = jnp.transpose((row * 512 + kinds_ref[...]).astype(jnp.float32)).astype(jnp.int32)
     spot = jnp.transpose(spot.astype(jnp.float32)).astype(jnp.int32)
     lane = lax.broadcasted_iota(jnp.int32, (entries, WIDTH), 1) & (entries - 1)
@@ -214,13 +235,15 @@
         lines.append(jnp.sum(got, axis=0, keepdims=True))
     packed = jnp.concatenate(lines, axis=0)
     lane = lax.broadcasted_iota(jnp.int32, (boxes, WIDTH), 1)
-    packed = jnp.where(lane >= entries + count, 8 * boxes * 512, packed)
-    out_ref[...] = jnp.where(lane == WIDTH - 1, count, packed)
+    masked = (lane >= entries) & (lane >= entries + jnp.where(lane < entries + FIRST, *ends[:2]))
+    packed = jnp.where(masked, 8 * boxes * 512, packed)
+    packed = jnp.where(lane == WIDTH - 2, ends[0], packed)
+    out_ref[...] = jnp.where(lane == WIDTH - 1, ends[1], packed)
 
 
 def slot_tables(send_index):
     own = jnp.concatenate([send_index, shift(send_index, "c", 1)], axis=0)
-    return own, shift(own, "y", -1), shift(own, "y", 2), shift(own, "y", 1)
+    return own, shift(own, "y", -1), shift(own, "y", 1)
 
 
 def plan_lists(tables, list_slots, list_kinds):
@@ -250,20 +273,10 @@
     x = lax.all_to_all(x, SAMP, split_axis=0, concat_axis=0, tiled=True)
 
     cosine, sine = phase_tables(polar_total, azimuth_total)
-    theta, phi = pl.pallas_call(
-        prepare_kernel,
-        out_shape=[
-            pltpu.VMEM(interp_theta.shape[::-1], jnp.bfloat16),
-            pltpu.VMEM(interp_phi.shape, jnp.bfloat16),
-        ],
-        in_specs=[VMEM] * 2,
-        out_specs=[VMEM] * 2,
-        compiler_params=pltpu.CompilerParams(vmem_limit_bytes=4 << 20),
-        cost_estimate=pl.CostEstimate(flops=1 << 20, bytes_accessed=1 << 18, transcendentals=0),
-        name="prepare",
-    )(interp_theta, interp_phi)
-    tables = slot_tables(send_index)
-    x, theta, phi, *tables = lax.optimization_barrier((x, theta, phi, *tables))
+    nothing = lax.optimization_barrier(jnp.zeros((), jnp.bfloat16))
+    theta, phi = interp_theta + nothing, interp_phi + nothing
+    near_tables = slot_tables(send_index)
+    x, theta, phi, *near_tables = lax.optimization_barrier((x, theta, phi, *near_tables))
     mine = pl.pallas_call(
         aggregate_kernel,
         out_shape=jax.ShapeDtypeStruct((samp_count, own_children // 8) + pattern, jnp.bfloat16),
@@ -271,15 +284,14 @@
         out_specs=VMEM,
         scratch_shapes=[
             pltpu.VMEM((16 * polar_total, child_azimuth), jnp.bfloat16),
-            pltpu.VMEM((16, polar_total, azimuth_total), jnp.float32),
         ],
         compiler_params=pltpu.CompilerParams(vmem_limit_bytes=12 << 20),
         cost_estimate=pl.CostEstimate(flops=335 << 20, bytes_accessed=4 << 20, transcendentals=0),
         name="aggregate",
     )(x, theta, phi, cosine, sine)
     mine = lax.all_to_all(mine, SAMP, split_axis=0, concat_axis=0, tiled=True)
-    lists = plan_lists(tables, list_slots, list_kinds)
-    mine, lists = lax.optimization_barrier((mine, lists))
+    far_table = shift(near_tables[0], "y", 2)
+    mine, far_table = lax.optimization_barrier((mine, far_table))
     own = mine.reshape((parent_boxes,) + pattern)
     after = shift(own, "y", -1)
     before = shift(own, "y", 1)
@@ -299,7 +311,8 @@
         name="widen",
     )(source)
 
-    own, wide = lax.optimization_barrier((own, wide))
+    own, wide, far_table = lax.optimization_barrier((own, wide, far_table))
+    lists = plan_lists((*near_tables, far_table), list_slots, list_kinds)
     far = shift(own, "y", 2)
 
     shape = (parent_boxes,) + pattern
@@ -307,29 +320,33 @@
     params = pltpu.CompilerParams(vmem_limit_bytes=8 << 20)
     cost = pl.CostEstimate(flops=16 << 20, bytes_accessed=8 << 20, transcendentals=0)
     list_scratch = [pltpu.SMEM(lists.shape, jnp.int32), pltpu.SemaphoreType.DMA]
-    pool, parents = pl.pallas_call(
-        pool_kernel,
-        out_shape=[pool_shape, jax.ShapeDtypeStruct(shape, jnp.bfloat16)],
-        in_specs=[VMEM] * 2,
-        out_specs=[VMEM, HBM],
-        scratch_shapes=[pltpu.SemaphoreType.DMA],
+    field, pool, parents = pl.pallas_call(
+        first_kernel,
+        out_shape=[
+            pltpu.VMEM(shape, jnp.float32),
+            pool_shape,
+            jax.ShapeDtypeStruct(shape, jnp.bfloat16),
+        ],
+        in_specs=[VMEM] * 4,
+        out_specs=[VMEM, VMEM, HBM],
+        scratch_shapes=list_scratch + [pltpu.SemaphoreType.DMA],
         compiler_params=params,
         cost_estimate=cost,
-        name="pool",
-    )(own, other)
+        name="first",
+    )(lists, wide, own, other)
     after, before, pool = lax.optimization_barrier((after, before, pool))
     near = [after, shift(after, "c", 1), before, shift(before, "c", 1)]
     early, pool = pl.pallas_call(
         early_kernel,
         out_shape=[pltpu.VMEM(shape, jnp.float32), pool_shape],
-        in_specs=[VMEM] * 7,
+        in_specs=[VMEM] * 8,
         out_specs=[VMEM] * 2,
-        input_output_aliases={6: 1},
+        input_output_aliases={7: 1},
         scratch_shapes=list_scratch,
         compiler_params=params,
         cost_estimate=cost,
         name="early",
-    )(lists, wide, *near, pool)
+    )(lists, wide, field, *near, pool)
     far, early = lax.optimization_barrier((far, early))
     field, _ = pl.pallas_call(
         late_kernel,

time: 65.5 us -> 63.1 us (0.963)
  other arithmetic: 2.25 us -> 3.83 us
  local copies, waits for them, and re-layouts: 2.25 us -> 0.7 us
  waiting for transfers between devices: 12.8 us -> 11.5 us
  starting transfers between devices: 30.2 us -> 29.3 us
    all_to_all x1, waiting for transfers between devices: 5.16 us -> 3.26 us  [local(): mine = lax.all_to_all(mine, SAMP, split_axis=0, concat_axis=0, tiled=True)]
    add x0 -> x2, other arithmetic: none -> 1.57 us  [local(): theta, phi = (interp_theta + nothing, interp_phi + nothing)]
    unnamed x9 -> x5, local copies, waits for them, and re-layouts: 2.25 us -> 0.69 us
    all_to_all x1, waiting for transfers between devices: 0.01 us -> 1.48 us  [local(): x = lax.all_to_all(x, SAMP, split_axis=0, concat_axis=0, tiled=True)]
    all_to_all x1, starting transfers between devices: 6.86 us -> 5.51 us  [local(): mine = lax.all_to_all(mine, SAMP, split_axis=0, concat_axis=0, tiled=True)]
    pallas_call x2 -> x1, Pallas kernels: 0.81 us -> 2 us  [local(): pl.pallas_call(first_kernel, out_shape=[pltpu.VMEM(shape, jnp.float32), p...]
    pallas_call x1, Pallas kernels: 3.06 us -> 1.98 us  [local(): pl.pallas_call(aggregate_kernel, out_shape=jax.ShapeDtypeStruct((samp_cou...]
    ppermute x11, waiting for transfers between devices: 7.62 us -> 6.72 us  [shift(): return lax.ppermute(x, axis, [(i, (i + step) % size) for i in range(size)])]
  transfers between devices with their start and end apart: 13 -> 13, of which waited for: 6 -> 6; matrix products, arithmetic and copies ran while one was open for 5% -> 7% of each run, Pallas kernels for 15% -> 18%
where the time goes in v5:
time: 63.1 us; the launch traced here: 62.6 us
  starting transfers between devices  29.3 us (46%)
  Pallas kernels  16.5 us (26%)
  waiting for transfers between devices  11.5 us (18%)
  other arithmetic  3.83 us (6%)
  between operations  0.75 us (1%)
  local copies, waits for them, and re-layouts  0.7 us (1%)
    ppermute x11, starting transfers between devices, shift(): return lax.ppermute(x, axis, [(i, (i + step) % size) for i in range(size)])  15.4 us
    all_to_all x1, starting transfers between devices, local(): x = lax.all_to_all(x, SAMP, split_axis=0, concat_axis=0, tiled=True)  8.43 us
    ppermute x11, waiting for transfers between devices, shift(): return lax.ppermute(x, axis, [(i, (i + step) % size) for i in range(size)])  6.72 us
    all_to_all x1, starting transfers between devices, local(): mine = lax.all_to_all(mine, SAMP, split_axis=0, concat_axis=0, tiled=True)  5.51 us
    pallas_call x1, Pallas kernels, local(): pl.pallas_call(early_kernel, out_shape=[pltpu.VMEM(shape, jnp.float32), p...  3.77 us
    pallas_call x1, Pallas kernels, local(): pl.pallas_call(late_kernel, out_shape=[jax.ShapeDtypeStruct(shape, jnp.fl...  3.6 us
    all_to_all x1, waiting for transfers between devices, local(): mine = lax.all_to_all(mine, SAMP, split_axis=0, concat_axis=0, tiled=True)  3.26 us
    pallas_call x1, Pallas kernels, local(): pl.pallas_call(widen_kernel, out_shape=pltpu.VMEM(translator.shape, jnp.f...  3.09 us
  transfers between devices with their start and end apart: 13, of which 6 were waited for; matrix products, arithmetic and copies ran while one was open for 7% of the time, Pallas kernels for 18%

profile of v5, /device:TPU:1, one launch (start us, length us, event | category | flops | bytes accessed | tf_op | source)
XLA Modules:
  0.0 62.6 jit_solution(13160171302810938115)
XLA Ops:
  0.6 8.4 %all-to-all-start = ((bf16[16,16,2,4,128]{4,3,2,1,0:T(4,128)(2,1)}), bf16[16,16,2,4,128]{4,3,2,1,0:T(4,128)(2,1)S(1)}, u32[]{:S(2)}, u32[]{:S(2)}) async-start(bf16[16,16,2,4,128]{4,3,2,1,0:T(4,128)(2,1)} %bitcast.9), calls=%async_computation | async-start | bytes 1048576 | tf_op jit(solution)/shard_map/all_to_all | solution.py:273
  9.1 1.0 %collective-permute-start = (s32[1,8,16]{2,1,0:T(8,128)}, s32[1,8,16]{2,1,0:T(8,128)S(1)}, u32[]{:S(2)}, u32[]{:S(2)}) collective-permute-start(s32[1,8,16]{2,1,0:T(8,128)} %param.11), channel_id=1, source_target_pairs={{0,16},{16,0},{1,17},{17,1},{2,18},{18,2},{3,19},{19,3},{4,20},{20... | collective-permute-start | bytes 1544 | tf_op jit(solution)/shard_map/ppermute | solution.py:197
  10.2 0.1 broadcast_multiply_fusion.1
  10.3 2.0 %fusion = (f32[4,128,256]{2,1,0:T(8,128)S(1)}, f32[4,128,256]{2,1,0:T(8,128)S(1)}) fusion(f32[128]{0:T(128)S(1)} %fusion.4, f32[128,256]{1,0:T(8,128)S(1)} %get-tuple-element.53, f32[4]{0:T(128)S(1)} %get-tuple-element.56, f32[128,256]{1,0:T(8,128)S(1)} %get-tuple-element.52, f32[4]{0:T(128)S(1)} %get-tuple-element.57), kind=kLoop, calls=%fused_computation.1 | loop fusion | flops 655360 | bytes 1311264 | tf_op jit(solution)/shard_map/sin | solution.py:37
  12.3 0.8 %broadcast_add_fusion.phi_ref = bf16[128,256]{1,0:T(8,128)(2,1)S(1)} fusion(bf16[128,256]{1,0:T(8,128)(2,1)} %param.9, bf16[]{:T(256)} %constant.10.clone.1), kind=kLoop, calls=%fused_computation.5 | loop fusion | flops 32768 | bytes 131074 | tf_op jit(solution)/shard_map/add | solution.py:277
  13.2 0.7 %constant_dynamic-update-slice_fusion.1 = s32[2,8,16]{2,1,0:T(8,128)S(1)} fusion(s32[1,8,16]{2,1,0:T(8,128)} %param.11), kind=kLoop, calls=%fused_computation.8 | loop fusion | bytes 4608
  13.8 0.0 collective-permute-done
  13.9 1.3 %collective-permute-start.2 = (s32[2,8,16]{2,1,0:T(8,128)S(1)}, s32[2,8,16]{2,1,0:T(8,128)S(1)}, u32[]{:S(2)}, u32[]{:S(2)}) collective-permute-start(s32[2,8,16]{2,1,0:T(8,128)S(1)} %constant_dynamic-update-slice_fusion.own_ref), channel_id=1, source_target_pairs={{0,32},{32,64},{64,96},{96,0},{1,33},{33,65},{65,97},{97,1},{2,34}... | collective-permute-start | bytes 3080 | tf_op jit(solution)/shard_map/ppermute | solution.py:197
  15.1 1.5 %collective-permute-start.1 = (s32[2,8,16]{2,1,0:T(8,128)S(1)}, s32[2,8,16]{2,1,0:T(8,128)S(1)}, u32[]{:S(2)}, u32[]{:S(2)}) collective-permute-start(s32[2,8,16]{2,1,0:T(8,128)S(1)} %constant_dynamic-update-slice_fusion.own_ref), channel_id=1, source_target_pairs={{0,96},{32,0},{64,32},{96,64},{1,97},{33,1},{65,33},{97,65},{2,98}... | collective-permute-start | bytes 3080 | tf_op jit(solution)/shard_map/ppermute | solution.py:197
  16.7 0.7 %broadcast_add_fusion.1.theta_ref = bf16[64,128]{1,0:T(8,128)(2,1)S(1)} fusion(bf16[64,128]{1,0:T(8,128)(2,1)} %param.8, bf16[]{:T(256)} %constant.10.clone.1), kind=kLoop, calls=%fused_computation.6 | loop fusion | flops 8192 | bytes 32770 | tf_op jit(solution)/shard_map/add | solution.py:277
  17.4 0.5 collective-permute-done.2.before_ref
  17.9 0.0 collective-permute-done.1.after_ref
  17.9 1.5 %all-to-all-done.x_ref = bf16[16,16,2,4,128]{4,3,2,1,0:T(4,128)(2,1)S(1)} async-done(((bf16[16,16,2,4,128]{4,3,2,1,0:T(4,128)(2,1)}), bf16[16,16,2,4,128]{4,3,2,1,0:T(4,128)(2,1)S(1)}, u32[]{:S(2)}, u32[]{:S(2)}) %all-to-all-start) | async-done | bytes 524320 | tf_op jit(solution)/shard_map/all_to_all | solution.py:273
  19.4 2.0 %aggregate.1 = bf16[16,2,2,8,256]{4,3,2,1,0:T(8,128)(2,1)} custom-call(bf16[16,16,2,4,128]{4,3,2,1,0:T(4,128)(2,1)S(1)} %all-to-all-done.x_ref, bf16[64,128]{1,0:T(8,128)(2,1)S(1)} %broadcast_add_fusion.1.theta_ref, bf16[128,256]{1,0:T(8,128)(2,1)S(1)} %broadcast_add_fusion.phi_ref, f32[4,128,256]{2,1,0:T(8,128)S(1)} %get-tuple-element.51.cos_ref, ...), custom_call_target="tpu_custom_call" | custom-call | flops 351272960 | bytes 4194304 | tf_op jit(solution)/shard_map/aggregate/pallas_call | solution.py:280
  21.4 0.0 copy-start
  21.4 0.0 copy-start.1
  21.4 5.5 %all-to-all-start.1 = ((bf16[16,2,2,8,256]{4,3,2,1,0:T(8,128)(2,1)}), bf16[16,2,2,8,256]{4,3,2,1,0:T(8,128)(2,1)S(1)}, u32[]{:S(2)}, u32[]{:S(2)}) async-start(bf16[16,2,2,8,256]{4,3,2,1,0:T(8,128)(2,1)} %aggregate.1), calls=%async_computation.1 | async-start | bytes 524288 | tf_op jit(solution)/shard_map/all_to_all | solution.py:292
  26.9 2.5 %collective-permute-start.3 = (s32[2,8,16]{2,1,0:T(8,128)S(1)}, s32[2,8,16]{2,1,0:T(8,128)S(1)}, u32[]{:S(2)}, u32[]{:S(2)}) collective-permute-start(s32[2,8,16]{2,1,0:T(8,128)S(1)} %constant_dynamic-update-slice_fusion.own_ref), channel_id=1, source_target_pairs={{0,64},{32,96},{64,0},{96,32},{1,65},{33,97},{65,1},{97,33},{2,66}... | collective-permute-start | bytes 3080 | tf_op jit(solution)/shard_map/ppermute | solution.py:197
  29.4 1.6 %collective-permute-done.3.far_ref = s32[2,8,16]{2,1,0:T(8,128)S(1)} collective-permute-done((s32[2,8,16]{2,1,0:T(8,128)S(1)}, s32[2,8,16]{2,1,0:T(8,128)S(1)}, u32[]{:S(2)}, u32[]{:S(2)}) %collective-permute-start.3) | collective-permute-done | bytes 1056 | tf_op jit(solution)/shard_map/ppermute | solution.py:197
  31.0 3.3 %all-to-all-done.1 = bf16[16,2,2,8,256]{4,3,2,1,0:T(8,128)(2,1)S(1)} async-done(((bf16[16,2,2,8,256]{4,3,2,1,0:T(8,128)(2,1)}), bf16[16,2,2,8,256]{4,3,2,1,0:T(8,128)(2,1)S(1)}, u32[]{:S(2)}, u32[]{:S(2)}) %all-to-all-start.1) | async-done | bytes 262176 | tf_op jit(solution)/shard_map/all_to_all | solution.py:292
  34.3 2.6 %collective-permute-start.4 = (bf16[32,2,8,256]{3,2,1,0:T(8,128)(2,1)S(1)}, bf16[32,2,8,256]{3,2,1,0:T(8,128)(2,1)S(1)}, u32[]{:S(2)}, u32[]{:S(2)}) collective-permute-start(bf16[32,2,8,256]{3,2,1,0:T(8,128)(2,1)S(1)} %bitcast.4), channel_id=1, source_target_pairs={{0,16},{16,0},{1,17},{17,1},{2,18},{18,2},{3,19},{19,3},{4,20},{20... | collective-permute-start | bytes 786440 | tf_op jit(solution)/shard_map/ppermute | solution.py:197
  36.9 1.3 %collective-permute-start.7 = (bf16[32,2,8,256]{3,2,1,0:T(8,128)(2,1)S(1)}, bf16[32,2,8,256]{3,2,1,0:T(8,128)(2,1)S(1)}, u32[]{:S(2)}, u32[]{:S(2)}) collective-permute-start(bf16[32,2,8,256]{3,2,1,0:T(8,128)(2,1)S(1)} %bitcast.5), channel_id=1, source_target_pairs={{0,32},{32,64},{64,96},{96,0},{1,33},{33,65},{65,97},{97,1},{2,34}... | collective-permute-start | bytes 786440 | tf_op jit(solution)/shard_map/ppermute | solution.py:197
  38.1 1.4 %collective-permute-start.6 = (bf16[32,2,8,256]{3,2,1,0:T(8,128)(2,1)S(1)}, bf16[32,2,8,256]{3,2,1,0:T(8,128)(2,1)S(1)}, u32[]{:S(2)}, u32[]{:S(2)}) collective-permute-start(bf16[32,2,8,256]{3,2,1,0:T(8,128)(2,1)S(1)} %bitcast.6), channel_id=1, source_target_pairs={{0,96},{32,0},{64,32},{96,64},{1,97},{33,1},{65,33},{97,65},{2,98}... | collective-permute-start | bytes 786440 | tf_op jit(solution)/shard_map/ppermute | solution.py:197
  39.5 0.1 pad_add_fusion.place_ref
  39.6 3.1 %widen.1.trans_ref = f32[316,2,8,256]{3,2,1,0:T(8,128)S(1)} custom-call(bf16[316,2,8,256]{3,2,1,0:T(8,128)(2,1)} %x_ref), custom_call_target="tpu_custom_call" | custom-call | flops 4194304 | bytes 8388608 | tf_op jit(solution)/shard_map/widen/pallas_call | solution.py:300
  42.7 0.0 copy-done
  42.7 0.0 copy-done.1
  42.7 2.1 %plan.1.lists = s32[32,128]{1,0:T(8,128)S(1)} custom-call(s32[2]{0:T(128)S(1)} %pad_add_fusion.place_ref, s32[2,8,16]{2,1,0:T(8,128)S(1)} %constant_dynamic-update-slice_fusion.own_ref, s32[2,8,16]{2,1,0:T(8,128)S(1)} %collective-permute-done.1.after_ref, s32[2,8,16]{2,1,0:T(8,128)S(1)} %collective-permute-done.2.before_ref, ...), custom_call_target="tpu_custom_call" | custom-call | flops 1048576 | bytes 1048576 | tf_op jit(solution)/shard_map/plan/pallas_call | solution.py:251
  44.8 0.0 collective-permute-done.4.other_ref
  44.9 2.0 %first.1 = (f32[32,2,8,256]{3,2,1,0:T(8,128)S(1)}, f32[257,2,8,256]{3,2,1,0:T(8,128)S(1)}, bf16[32,2,8,256]{3,2,1,0:T(8,128)(2,1)}) custom-call(s32[32,128]{1,0:T(8,128)S(1)} %plan.1.lists, f32[316,2,8,256]{3,2,1,0:T(8,128)S(1)} %widen.1.trans_ref, bf16[32,2,8,256]{3,2,1,0:T(8,128)(2,1)S(1)} %bitcast.7, ...), custom_call_target="tpu_custom_call" | custom-call | flops 16777216 | bytes 8388608 | tf_op jit(solution)/shard_map/first/pallas_call | solution.py:323
  46.9 0.0 collective-permute-done.7.refs_2_
  46.9 0.0 collective-permute-done.6.refs_0_
  46.9 0.6 %collective-permute-start.8 = (bf16[32,2,8,256]{3,2,1,0:T(8,128)(2,1)S(1)}, bf16[32,2,8,256]{3,2,1,0:T(8,128)(2,1)S(1)}, u32[]{:S(2)}, u32[]{:S(2)}) collective-permute-start(bf16[32,2,8,256]{3,2,1,0:T(8,128)(2,1)S(1)} %collective-permute-done.6.refs_0_), channel_id=1, source_target_pairs={{0,16},{16,0},{1,17},{17,1},{2,18},{18,2},{3,19},{19,3},{4,20},{20... | collective-permute-start | bytes 786440 | tf_op jit(solution)/shard_map/ppermute | solution.py:197
  47.5 0.1 collective-permute-start.9
  47.6 1.8 %collective-permute-start.5 = (bf16[32,2,8,256]{3,2,1,0:T(8,128)(2,1)S(1)}, bf16[32,2,8,256]{3,2,1,0:T(8,128)(2,1)S(1)}, u32[]{:S(2)}, u32[]{:S(2)}) collective-permute-start(bf16[32,2,8,256]{3,2,1,0:T(8,128)(2,1)S(1)} %bitcast.8), channel_id=1, source_target_pairs={{0,64},{32,96},{64,0},{96,32},{1,65},{33,97},{65,1},{97,33},{2,66}... | collective-permute-start | bytes 786440 | tf_op jit(solution)/shard_map/ppermute | solution.py:197
  49.4 0.0 collective-permute-done.8.refs_1_
  49.4 0.0 collective-permute-done.9.refs_3_
  49.4 3.8 %early.1 = (f32[32,2,8,256]{3,2,1,0:T(8,128)S(1)}, f32[257,2,8,256]{3,2,1,0:T(8,128)S(1)}) custom-call(s32[32,128]{1,0:T(8,128)S(1)} %plan.1.lists, f32[316,2,8,256]{3,2,1,0:T(8,128)S(1)} %widen.1.trans_ref, f32[32,2,8,256]{3,2,1,0:T(8,128)S(1)} %get-tuple-element.40.sum_ref, ...), custom_call_target="tpu_custom_call", output_to_operand_aliasing={{1}: (7, {})} | custom-call | flops 16777216 | bytes 8388608 | tf_op jit(solution)/shard_map/early/pallas_call | solution.py:339
  53.2 3.4 %collective-permute-done.5.refs_0_ = bf16[32,2,8,256]{3,2,1,0:T(8,128)(2,1)S(1)} collective-permute-done((bf16[32,2,8,256]{3,2,1,0:T(8,128)(2,1)S(1)}, bf16[32,2,8,256]{3,2,1,0:T(8,128)(2,1)S(1)}, u32[]{:S(2)}, u32[]{:S(2)}) %collective-permute-start.5) | collective-permute-done | bytes 262176 | tf_op jit(solution)/shard_map/ppermute | solution.py:197
  56.6 1.3 %collective-permute-start.10 = (bf16[32,2,8,256]{3,2,1,0:T(8,128)(2,1)S(1)}, bf16[32,2,8,256]{3,2,1,0:T(8,128)(2,1)S(1)}, u32[]{:S(2)}, u32[]{:S(2)}) collective-permute-start(bf16[32,2,8,256]{3,2,1,0:T(8,128)(2,1)S(1)} %collective-permute-done.5.refs_0_), channel_id=1, source_target_pairs={{0,16},{16,0},{1,17},{17,1},{2,18},{18,2},{3,19},{19,3},{4,20},{20... | collective-permute-start | bytes 786440 | tf_op jit(solution)/shard_map/ppermute | solution.py:197
  57.8 1.2 %collective-permute-done.10.refs_1_ = bf16[32,2,8,256]{3,2,1,0:T(8,128)(2,1)S(1)} collective-permute-done((bf16[32,2,8,256]{3,2,1,0:T(8,128)(2,1)S(1)}, bf16[32,2,8,256]{3,2,1,0:T(8,128)(2,1)S(1)}, u32[]{:S(2)}, u32[]{:S(2)}) %collective-permute-start.10) | collective-permute-done | bytes 262176 | tf_op jit(solution)/shard_map/ppermute | solution.py:197
  59.0 3.6 %late.1 = (f32[32,2,8,256]{3,2,1,0:T(8,128)}, f32[257,2,8,256]{3,2,1,0:T(8,128)S(1)}) custom-call(s32[32,128]{1,0:T(8,128)S(1)} %plan.1.lists, f32[316,2,8,256]{3,2,1,0:T(8,128)S(1)} %widen.1.trans_ref, f32[32,2,8,256]{3,2,1,0:T(8,128)S(1)} %get-tuple-element.46.sum_ref, ...), custom_call_target="tpu_custom_call", output_to_operand_aliasing={{1}: (5, {})} | custom-call | flops 16777216 | bytes 8388608 | tf_op jit(solution)/shard_map/late/pallas_call | solution.py:351
  (5 shorter events, 0.1 us)
Async XLA Ops:
  0.6 18.8 %all-to-all-start = ((bf16[16,16,2,4,128]{4,3,2,1,0:T(4,128)(2,1)}), bf16[16,16,2,4,128]{4,3,2,1,0:T(4,128)(2,1)S(1)}, u32[]{:S(2)}, u32[]{:S(2)}) async-start(bf16[16,16,2,4,128]{4,3,2,1,0:T(4,128)(2,1)} %bitcast.9), calls=%async_computation | async-start | bytes 1048576 | tf_op jit(solution)/shard_map/all_to_all | solution.py:273
  9.1 4.8 %collective-permute-start = (s32[1,8,16]{2,1,0:T(8,128)}, s32[1,8,16]{2,1,0:T(8,128)S(1)}, u32[]{:S(2)}, u32[]{:S(2)}) collective-permute-start(s32[1,8,16]{2,1,0:T(8,128)} %param.11), channel_id=1, source_target_pairs={{0,16},{16,0},{1,17},{17,1},{2,18},{18,2},{3,19},{19,3},{4,20},{20... | collective-permute-start | bytes 1544 | tf_op jit(solution)/shard_map/ppermute | solution.py:197
  13.9 4.1 %collective-permute-start.2 = (s32[2,8,16]{2,1,0:T(8,128)S(1)}, s32[2,8,16]{2,1,0:T(8,128)S(1)}, u32[]{:S(2)}, u32[]{:S(2)}) collective-permute-start(s32[2,8,16]{2,1,0:T(8,128)S(1)} %constant_dynamic-update-slice_fusion.own_ref), channel_id=1, source_target_pairs={{0,32},{32,64},{64,96},{96,0},{1,33},{33,65},{65,97},{97,1},{2,34}... | collective-permute-start | bytes 3080 | tf_op jit(solution)/shard_map/ppermute | solution.py:197
  15.1 2.8 %collective-permute-start.1 = (s32[2,8,16]{2,1,0:T(8,128)S(1)}, s32[2,8,16]{2,1,0:T(8,128)S(1)}, u32[]{:S(2)}, u32[]{:S(2)}) collective-permute-start(s32[2,8,16]{2,1,0:T(8,128)S(1)} %constant_dynamic-update-slice_fusion.own_ref), channel_id=1, source_target_pairs={{0,96},{32,0},{64,32},{96,64},{1,97},{33,1},{65,33},{97,65},{2,98}... | collective-permute-start | bytes 3080 | tf_op jit(solution)/shard_map/ppermute | solution.py:197
  21.4 21.3 %copy-start = (s32[32,64]{1,0:T(8,128)S(1)}, s32[32,64]{1,0:T(8,128)}, u32[]{:S(2)}) copy-start(s32[32,64]{1,0:T(8,128)} %slots_ref.1) | copy-start | bytes 24580
  21.4 21.3 %copy-start.1 = (s32[32,64]{1,0:T(8,128)S(1)}, s32[32,64]{1,0:T(8,128)}, u32[]{:S(2)}) copy-start(s32[32,64]{1,0:T(8,128)} %kinds_ref.1) | copy-start | bytes 24580
  21.4 12.9 %all-to-all-start.1 = ((bf16[16,2,2,8,256]{4,3,2,1,0:T(8,128)(2,1)}), bf16[16,2,2,8,256]{4,3,2,1,0:T(8,128)(2,1)S(1)}, u32[]{:S(2)}, u32[]{:S(2)}) async-start(bf16[16,2,2,8,256]{4,3,2,1,0:T(8,128)(2,1)} %aggregate.1), calls=%async_computation.1 | async-start | bytes 524288 | tf_op jit(solution)/shard_map/all_to_all | solution.py:292
  26.9 4.1 %collective-permute-start.3 = (s32[2,8,16]{2,1,0:T(8,128)S(1)}, s32[2,8,16]{2,1,0:T(8,128)S(1)}, u32[]{:S(2)}, u32[]{:S(2)}) collective-permute-start(s32[2,8,16]{2,1,0:T(8,128)S(1)} %constant_dynamic-update-slice_fusion.own_ref), channel_id=1, source_target_pairs={{0,64},{32,96},{64,0},{96,32},{1,65},{33,97},{65,1},{97,33},{2,66}... | collective-permute-start | bytes 3080 | tf_op jit(solution)/shard_map/ppermute | solution.py:197
  34.3 10.6 %collective-permute-start.4 = (bf16[32,2,8,256]{3,2,1,0:T(8,128)(2,1)S(1)}, bf16[32,2,8,256]{3,2,1,0:T(8,128)(2,1)S(1)}, u32[]{:S(2)}, u32[]{:S(2)}) collective-permute-start(bf16[32,2,8,256]{3,2,1,0:T(8,128)(2,1)S(1)} %bitcast.4), channel_id=1, source_target_pairs={{0,16},{16,0},{1,17},{17,1},{2,18},{18,2},{3,19},{19,3},{4,20},{20... | collective-permute-start | bytes 786440 | tf_op jit(solution)/shard_map/ppermute | solution.py:197
  36.9 10.0 %collective-permute-start.7 = (bf16[32,2,8,256]{3,2,1,0:T(8,128)(2,1)S(1)}, bf16[32,2,8,256]{3,2,1,0:T(8,128)(2,1)S(1)}, u32[]{:S(2)}, u32[]{:S(2)}) collective-permute-start(bf16[32,2,8,256]{3,2,1,0:T(8,128)(2,1)S(1)} %bitcast.5), channel_id=1, source_target_pairs={{0,32},{32,64},{64,96},{96,0},{1,33},{33,65},{65,97},{97,1},{2,34}... | collective-permute-start | bytes 786440 | tf_op jit(solution)/shard_map/ppermute | solution.py:197
  38.1 8.8 %collective-permute-start.6 = (bf16[32,2,8,256]{3,2,1,0:T(8,128)(2,1)S(1)}, bf16[32,2,8,256]{3,2,1,0:T(8,128)(2,1)S(1)}, u32[]{:S(2)}, u32[]{:S(2)}) collective-permute-start(bf16[32,2,8,256]{3,2,1,0:T(8,128)(2,1)S(1)} %bitcast.6), channel_id=1, source_target_pairs={{0,96},{32,0},{64,32},{96,64},{1,97},{33,1},{65,33},{97,65},{2,98}... | collective-permute-start | bytes 786440 | tf_op jit(solution)/shard_map/ppermute | solution.py:197
  46.9 2.5 %collective-permute-start.8 = (bf16[32,2,8,256]{3,2,1,0:T(8,128)(2,1)S(1)}, bf16[32,2,8,256]{3,2,1,0:T(8,128)(2,1)S(1)}, u32[]{:S(2)}, u32[]{:S(2)}) collective-permute-start(bf16[32,2,8,256]{3,2,1,0:T(8,128)(2,1)S(1)} %collective-permute-done.6.refs_0_), channel_id=1, source_target_pairs={{0,16},{16,0},{1,17},{17,1},{2,18},{18,2},{3,19},{19,3},{4,20},{20... | collective-permute-start | bytes 786440 | tf_op jit(solution)/shard_map/ppermute | solution.py:197
  47.5 1.9 %collective-permute-start.9 = (bf16[32,2,8,256]{3,2,1,0:T(8,128)(2,1)S(1)}, bf16[32,2,8,256]{3,2,1,0:T(8,128)(2,1)S(1)}, u32[]{:S(2)}, u32[]{:S(2)}) collective-permute-start(bf16[32,2,8,256]{3,2,1,0:T(8,128)(2,1)S(1)} %collective-permute-done.7.refs_2_), channel_id=1, source_target_pairs={{0,16},{16,0},{1,17},{17,1},{2,18},{18,2},{3,19},{19,3},{4,20},{20... | collective-permute-start | bytes 786440 | tf_op jit(solution)/shard_map/ppermute | solution.py:197
  47.6 9.0 %collective-permute-start.5 = (bf16[32,2,8,256]{3,2,1,0:T(8,128)(2,1)S(1)}, bf16[32,2,8,256]{3,2,1,0:T(8,128)(2,1)S(1)}, u32[]{:S(2)}, u32[]{:S(2)}) collective-permute-start(bf16[32,2,8,256]{3,2,1,0:T(8,128)(2,1)S(1)} %bitcast.8), channel_id=1, source_target_pairs={{0,64},{32,96},{64,0},{96,32},{1,65},{33,97},{65,1},{97,33},{2,66}... | collective-permute-start | bytes 786440 | tf_op jit(solution)/shard_map/ppermute | solution.py:197
  56.6 2.4 %collective-permute-start.10 = (bf16[32,2,8,256]{3,2,1,0:T(8,128)(2,1)S(1)}, bf16[32,2,8,256]{3,2,1,0:T(8,128)(2,1)S(1)}, u32[]{:S(2)}, u32[]{:S(2)}) collective-permute-start(bf16[32,2,8,256]{3,2,1,0:T(8,128)(2,1)S(1)} %collective-permute-done.5.refs_0_), channel_id=1, source_target_pairs={{0,16},{16,0},{1,17},{17,1},{2,18},{18,2},{3,19},{19,3},{4,20},{20... | collective-permute-start | bytes 786440 | tf_op jit(solution)/shard_map/ppermute | solution.py:197
